TPU v7x, 256 devices: a whole 4x4x8 slice. The times are simulated.
256 devices in a mesh: pw: 64 (over y_lo, z, x), atom: 4 (over y_hi, core).
Axes of the slice: x: 4, y: 4 (y_hi: 2, y_lo: 2; y = y_hi * 2 + y_lo), z: 8, core: 2. Of those that a mesh axis runs over, the one named last changes fastest.
Arguments:
- bands_in: float32 [2, 8, 32768], P(None, None, 'pw'), may hold values from -6 to 6
- template: bfloat16 [2, 64, 32768], P(None, None, 'pw'), may hold values from -0.03125 to 0.03125
- potential: bfloat16 [1024, 8192], P(('pw', 'atom')), may hold values from -0.5 to 0.5
- miller: int32 [3, 32768], P(None, 'pw'), may hold values from -32 to 32, as said below
- positions: float32 [3, 1024], replicated, may hold values from 0 to 1
- species: int32 [1024], replicated, may hold values from 0 to 1
- atom_order: int32 [1024], replicated, may hold values from 0 to 1023, each once
- reciprocal: float32 [3], replicated, may hold values from 0.03 to 0.1
Outputs:
- applied_once: float32 [2, 8, 32768], P(None, None, 'pw')
- applied_twice: float32 [2, 8, 32768], P(None, None, 'pw')
Inputs may be any that keep to these rules, and one draw needn't show every extreme that they name: `atom_order`: each atom stands in exactly one slot. `miller`: no two plane waves have the same triple of Miller indices; the triples (-32, -32, -32) and (32, 32, 32) are always among them.
All inputs are finite; a program needn't handle non-finite values.
Results may differ from a plain program's by a relative error of at most 0.005.
Values may be sent and summed in bfloat16 or wider, within the bound.
No kernel may reach another device: no remote copies, remote signals or barrier semaphores. Data moves between devices by JAX's collectives and lax.ppermute only.
A program may use at most 64 MiB of HBM per device.

v0:
```python
import math

import jax
import jax.numpy as jnp
from jax import lax
from jax.sharding import PartitionSpec as P

full_turn = 2.0 * math.pi


def phases(miller_real, centres):
    angles = full_turn * (
        centres[0][:, None] * miller_real[0][None, :]
        + centres[1][:, None] * miller_real[1][None, :]
        + centres[2][:, None] * miller_real[2][None, :]
    )
    return (jnp.cos(angles), jnp.sin(angles))


def project_block(template_flat, fields, cos_part, sin_part, chosen):
    band_count = fields.shape[1]
    real_wave = cos_part[:, None, :] * fields[0][None] - sin_part[:, None, :] * fields[1][None]
    imag_wave = sin_part[:, None, :] * fields[0][None] + cos_part[:, None, :] * fields[1][None]
    stacked = jnp.stack([real_wave, imag_wave], axis=1).astype(jnp.bfloat16)
    atom_count = stacked.shape[0]
    flattened = stacked.reshape(atom_count * 2 * band_count, stacked.shape[3])
    correlations = lax.dot_general(
        template_flat, flattened, (((1,), (1,)), ((), ())), preferred_element_type=jnp.float32
    )
    species_count = chosen.shape[1]
    harmonics = template_flat.shape[0] // species_count
    correlations = correlations.reshape(species_count, harmonics, atom_count, 2, band_count)
    accumulated = jnp.zeros((harmonics, atom_count, 2, band_count), jnp.float32)
    for species_id in range(species_count):
        accumulated = (
            accumulated + chosen[:, species_id][None, :, None, None] * correlations[species_id]
        )
    return jnp.transpose(accumulated, (1, 2, 0, 3))


def product(matrices, vectors):
    return jnp.einsum("alm,amb->alb", matrices, vectors, precision=lax.Precision.HIGHEST)


def apply_potential(potential, coeffs):
    atom_count = coeffs.shape[0]
    harmonics = coeffs.shape[2]
    matrices = potential.astype(jnp.float32).reshape(atom_count, 2, harmonics, harmonics)
    real_new = product(matrices[:, 0], coeffs[:, 0]) - product(matrices[:, 1], coeffs[:, 1])
    imag_new = product(matrices[:, 0], coeffs[:, 1]) + product(matrices[:, 1], coeffs[:, 0])
    return jnp.stack([real_new, imag_new], axis=1).astype(jnp.bfloat16)


def return_block(template_flat, applied, cos_part, sin_part, chosen):
    atom_count, _, harmonics, band_count = applied.shape
    species_count = chosen.shape[1]
    reordered = jnp.transpose(applied, (2, 0, 1, 3))
    selected = jnp.stack(
        [
            reordered * chosen[:, species_id][None, :, None, None].astype(jnp.bfloat16)
            for species_id in range(species_count)
        ]
    )
    selected = selected.reshape(species_count * harmonics, atom_count * 2 * band_count)
    images = lax.dot_general(
        selected, template_flat, (((0,), (0,)), ((), ())), preferred_element_type=jnp.float32
    )
    images = images.reshape(atom_count, 2, band_count, template_flat.shape[1])
    real_out = jnp.sum(
        cos_part[:, None, :] * images[:, 0] + sin_part[:, None, :] * images[:, 1], axis=0
    )
    imag_out = jnp.sum(
        cos_part[:, None, :] * images[:, 1] - sin_part[:, None, :] * images[:, 0], axis=0
    )
    return jnp.stack([real_out, imag_out])


def per_device(bands_in, template, potential, miller, positions, species, atom_order, reciprocal):
    pw_count = lax.axis_size("pw")
    group_count = lax.axis_size("atom")
    group_id = lax.axis_index("atom")
    slot_dev = potential.shape[0]
    per_group = slot_dev * pw_count
    species_count, harmonics, wave_count = template.shape
    band_count = bands_in.shape[1]
    template_flat = template.reshape(species_count * harmonics, wave_count)
    local_rows = jnp.arange(per_group, dtype=jnp.int32)
    slot_ids = (local_rows // slot_dev * group_count + group_id) * slot_dev + local_rows % slot_dev
    atoms_here = atom_order[slot_ids]
    centres = positions[:, atoms_here]
    kinds = species[atoms_here]
    chosen = (kinds[:, None] == jnp.arange(species_count, dtype=jnp.int32)[None, :]).astype(
        jnp.float32
    )
    miller_real = miller.astype(jnp.float32)
    kinetic = 0.5 * (
        (reciprocal[0] * miller_real[0]) ** 2
        + (reciprocal[1] * miller_real[1]) ** 2
        + (reciprocal[2] * miller_real[2]) ** 2
    )
    cos_all, sin_all = phases(miller_real, centres)
    block_size = math.gcd(per_group, 32)
    block_count = per_group // block_size
    row_width = 2 * harmonics * band_count

    def apply_once(fields):

        def projected(blocknum):
            first_row = blocknum * block_size
            chosen_part = lax.dynamic_slice_in_dim(chosen, first_row, block_size, 0)
            cos_part = lax.dynamic_slice_in_dim(cos_all, first_row, block_size, 0)
            sin_part = lax.dynamic_slice_in_dim(sin_all, first_row, block_size, 0)
            return project_block(template_flat, fields, cos_part, sin_part, chosen_part)

        coeffs = lax.map(projected, jnp.arange(block_count, dtype=jnp.int32)).reshape(
            per_group, row_width
        )
        summed = lax.psum(coeffs, "pw")
        segment = lax.all_gather(potential, "pw", axis=0, tiled=True)
        row_count = segment.shape[0]
        segment_coeffs = summed.reshape(row_count, 2, harmonics, band_count)
        applied = apply_potential(segment, segment_coeffs).reshape(row_count, row_width)
        applied = applied.reshape(per_group, 2, harmonics, band_count)

        def returned(blocknum, summed_up):
            first_row = (blocknum * block_size).astype(jnp.int32)
            chosen_part = lax.dynamic_slice_in_dim(chosen, first_row, block_size, 0)
            applied_part = lax.dynamic_slice_in_dim(applied, first_row, block_size, 0)
            cos_part = lax.dynamic_slice_in_dim(cos_all, first_row, block_size, 0)
            sin_part = lax.dynamic_slice_in_dim(sin_all, first_row, block_size, 0)
            return summed_up + return_block(
                template_flat, applied_part, cos_part, sin_part, chosen_part
            )

        summed_up = lax.fori_loop(
            0, block_count, returned, jnp.zeros((2, band_count, wave_count), jnp.float32)
        )
        return lax.psum(summed_up, "atom") + kinetic[None, None, :] * fields

    applied_once = apply_once(bands_in)
    applied_twice = apply_once(applied_once)
    return (applied_once, applied_twice)


def solution(mesh):
    in_specs = (
        P(None, None, "pw"),
        P(None, None, "pw"),
        P(("pw", "atom"), None),
        P(None, "pw"),
        P(),
        P(),
        P(),
        P(),
    )
    out_specs = (P(None, None, "pw"), P(None, None, "pw"))
    return jax.shard_map(
        per_device, mesh=mesh, in_specs=in_specs, out_specs=out_specs, check_vma=False
    )
```

profile of v0, /device:TPU:1, one launch (start us, length us, event | category | flops | bytes accessed | tf_op | source)
XLA Modules:
  0.0 1699.0 jit_solution(8377880044509035921)
XLA Ops:
  8.7 0.9 copy.40
  9.7 1.4 gather_fusion
  12.1 1.9 gather_fusion.2
  14.0 3.1 fusion.24
  17.4 25.3 %while.48 = (s32[]{:T(128)}, f32[8,32,2,64,8]{3,4,1,0,2:T(8,128)S(1)}, s32[8]{0:T(128)S(1)}, f32[256,2]{0,1:T(2,128)S(1)}, f32[256,512]{1,0:T(8,128)}, /*index=5...) while((s32[]{:T(128)}, ...), condition=%wide.region_1.2_spmd, body=%wide.region_0.1_spmd.sunk | while | flops 68517896 | bytes 4819139 | solution.py:115
  18.6 0.9 constant_dynamic-slice_fusion.22
  21.8 0.9 constant_dynamic-slice_fusion.22
  25.0 0.9 constant_dynamic-slice_fusion.22
  28.1 0.9 constant_dynamic-slice_fusion.22
  31.3 0.9 constant_dynamic-slice_fusion.22
  34.5 0.9 constant_dynamic-slice_fusion.22
  37.6 0.9 constant_dynamic-slice_fusion.22
  42.7 1.3 copy-done.4
  44.9 1.9 add_multiply_fusion.1
  46.9 224.2 %all-gather.3.cloned.1.call-done = bf16[64,4,8192]{2,1,0:T(4,128)(2,1)} async-done(((bf16[1,4,8192]{2,1,0:T(4,128)(2,1)}), bf16[64,4,8192]{2,1,0:T(4,128)(2,1)}) %all-gather.3.cloned.1.call-update) | async-done | bytes 4194320 | tf_op jit(solution)/shard_map/all_gather | solution.py:119
  271.1 13.4 reshape.268
  284.4 602.4 %all-reduce.3.cloned.1.call-done = f32[256,2,64,8]{2,3,0,1:T(8,128)} async-done(((f32[256,2,64,8]{2,3,0,1:T(8,128)}), f32[256,2,64,8]{2,3,0,1:T(8,128)}) %all-reduce.3.cloned.1.call-update) | async-done | bytes 1048592 | tf_op jit(solution)/shard_map/psum | solution.py:118
  886.8 8.6 fusion.6
  895.4 8.6 fusion.7
  904.1 6.6 fusion.21
  910.7 6.6 fusion.20
  917.5 16.8 while.50
  934.3 57.2 %psum.29 = f32[2,8,512]{2,1,0:T(8,128)S(1)} all-reduce(f32[2,8,512]{2,1,0:T(8,128)S(1)} %get-tuple-element.335), channel_id=1, replica_groups=mesh['pw'=64,'atom'=4] {'atom'}, use_global_device_ids=true, to_apply=%region_7.8 | all-reduce | flops 8192 | bytes 65536 | tf_op jit(solution)/shard_map/psum | solution.py:138
  991.7 25.3 %while.49 = (s32[]{:T(128)}, f32[8,32,2,64,8]{3,4,1,0,2:T(8,128)S(1)}, s32[8]{0:T(128)S(1)}, f32[256,2]{0,1:T(2,128)S(1)}, f32[256,512]{1,0:T(8,128)}, /*index=5...) while((s32[]{:T(128)}, ...), condition=%wide.region_9.10_spmd, body=%wide.region_8.9_spmd.sunk | while | flops 68517896 | bytes 4819139 | solution.py:115
  1017.1 1.3 copy-done.3
  1018.4 567.7 %all-reduce.5.cloned.1.call-done = f32[256,2,64,8]{2,3,0,1:T(8,128)} async-done(((f32[256,2,64,8]{2,3,0,1:T(8,128)}), f32[256,2,64,8]{2,3,0,1:T(8,128)}) %all-reduce.5.cloned.1.call-update) | async-done | bytes 1048592 | tf_op jit(solution)/shard_map/psum | solution.py:118
  1586.2 8.6 fusion.4
  1594.8 8.5 fusion.5
  1603.3 8.3 fusion.23
  1611.6 6.6 fusion.22
  1618.5 16.8 while.51
  1635.2 56.6 %psum.31 = f32[2,8,512]{2,1,0:T(8,128)S(1)} all-reduce(f32[2,8,512]{2,1,0:T(8,128)S(1)} %get-tuple-element.337), channel_id=1, replica_groups=mesh['pw'=64,'atom'=4] {'atom'}, use_global_device_ids=true, to_apply=%region_15.16 | all-reduce | flops 8192 | bytes 65536 | tf_op jit(solution)/shard_map/psum | solution.py:138
  (395 shorter events, 70.2 us)
Async XLA Ops:
  7.2 2.5 copy-start
  7.2 10.1 copy-start.8
  7.2 10.1 copy-start.2
  7.2 263.9 %all-gather.3.cloned.1.call-start = ((), (), s32[]{:S(2)}) async-start(), calls=%async_computation.2 | async-start | bytes 4259840 | tf_op jit(solution)/shard_map/all_gather | solution.py:119
  7.9 878.9 %all-reduce.3.cloned.1.call-start = ((), (), s32[]{:S(2)}) async-start(), calls=%async_computation | async-start | bytes 4194304 | tf_op jit(solution)/shard_map/psum | solution.py:118
  17.3 26.9 %copy-start.9 = (f32[3]{0:T(128)S(1)}, f32[3]{0:T(128)}, u32[]{:S(2)}) copy-start(f32[3]{0:T(128)} %param.23) | copy-start | bytes 40
  42.7 1.3 copy-start.4
  44.0 1542.1 %all-reduce.5.cloned.1.call-start = ((), (), s32[]{:S(2)}) async-start(), calls=%async_computation.1 | async-start | bytes 4194304 | tf_op jit(solution)/shard_map/psum | solution.py:118
  886.8 17.3 %copy-start.1 = (bf16[256,2,64,64]{3,2,1,0:T(8,128)(2,1)S(1)}, bf16[256,2,64,64]{3,2,1,0:T(8,128)(2,1)}, u32[]{:S(2)}) copy-start(bf16[256,2,64,64]{3,2,1,0:T(8,128)(2,1)} %reshape.268) | copy-start | bytes 12582916
  895.4 8.6 copy-start.5
  1017.0 1.3 copy-start.3
  1017.0 674.8 %copy-start.7 = (f32[2,8,512]{2,1,0:T(8,128)}, f32[2,8,512]{2,1,0:T(8,128)S(1)}, u32[]{:S(2)}) copy-start(f32[2,8,512]{2,1,0:T(8,128)S(1)} %get-tuple-element.947) | copy-start | bytes 98308
  1586.1 8.6 copy-start.6
  1586.1 25.4 %slice-start = ((s8[8388608]{0:T(1024)(128)(4,1)}), s8[4194304]{0:T(1024)(128)(4,1)S(1)}, s32[]{:S(2)}) async-start(s8[8388608]{0:T(1024)(128)(4,1)} %bitcast.282), calls=%async_computation.3 | async-start | bytes 8388608
  1594.8 16.8 slice-start.1
Sparse Core Ops, SparseCore 0:
  9.8 261.2 all-gather.2
  273.7 613.1 all-reduce.2
  1018.5 567.5 all-reduce.4
where the time goes:
time: 1700 us
  waiting for transfers between devices  1400 us (82%)
  blocking collectives  114 us (7%)
  local copies, waits for them, and re-layouts  73.1 us (4%)
  matrix products  71.7 us (4%)
  other arithmetic  18.1 us (1%)
    psum x2, waiting for transfers between devices, apply_once(): summed = lax.psum(coeffs, 'pw')  1170 us
    all_gather x1, waiting for transfers between devices, apply_once(): segment = lax.all_gather(potential, 'pw', axis=0, tiled=True)  224 us
    psum x2, blocking collectives, apply_once(): return lax.psum(summed_up, 'atom') + kinetic[None, None, :] * fields  114 us
    dot_general x8, matrix products, product(): jnp.einsum('alm,amb->alb', matrices, vectors, precision=lax.Precision.HIG...  62.5 us
  transfers between devices with their start and end apart: 3, of which 3 were waited for; matrix products, arithmetic and copies ran while one was open for 3% of the time, Pallas kernels for 0%

commit v1 on v0

v1 whole, which is shorter than its diff:
```python
import functools

import jax
import jax.numpy as jnp
from jax import lax
from jax.experimental import pallas as pl
from jax.experimental.pallas import tpu as pltpu
from jax.sharding import PartitionSpec as P

f32 = jnp.float32
bf16 = jnp.bfloat16

COS_TURN = (
    0.9999999890590225,
    -19.739204499453912,
    64.93911745989556,
    -85.45013953088248,
    60.167630950949295,
    -25.96759924849463,
    6.528658161366808,
)
SIN_TURN = (
    6.283185302511503,
    -41.34170040531749,
    81.60513138579344,
    -76.70301535379849,
    42.02592698556796,
    -14.899846667364866,
    3.238137509743233,
)
NT = (((1,), (1,)), ((), ()))
NN = (((1,), (0,)), ((), ()))
CHUNK = 16


def dot(left, right, dims):
    return lax.dot_general(left, right, dims, preferred_element_type=f32)


def horner(coefs, arg):
    total = jnp.full_like(arg, coefs[-1])
    for coef in coefs[-2::-1]:
        total = total * arg + coef
    return total


def three_parts(values):
    high = values.astype(bf16)
    rest = values - high.astype(f32)
    middle = rest.astype(bf16)
    low = (rest - middle.astype(f32)).astype(bf16)
    return high, middle, low


def atom_table(positions, species, order, group, rows, groups, slot_dev):
    atoms = order.shape[1]
    row = lax.broadcasted_iota(jnp.int32, (rows, atoms), 0)
    lane = lax.broadcasted_iota(jnp.int32, (rows, atoms), 1)
    slot = (row // slot_dev * groups + group) * slot_dev + row % slot_dev
    pick_slot = jnp.where(lane == slot, 1.0, 0.0).astype(bf16)
    coarse, fine = order // 128, order % 128
    pad = jnp.zeros((14, atoms), f32)
    digits = jnp.concatenate([coarse.astype(f32), fine.astype(f32), pad], axis=0).astype(bf16)
    found = dot(pick_slot, digits, NT)
    atom = (found[:, 0:1] * 128.0 + found[:, 1:2]).astype(jnp.int32)
    pick_atom = jnp.where(lane == atom, 1.0, 0.0).astype(bf16)
    high, middle, low = three_parts(positions)
    pad = jnp.zeros((6, atoms), bf16)
    facts = jnp.concatenate([high, middle, low, species.astype(f32).astype(bf16), pad], axis=0)
    return dot(pick_atom, facts, NT)


def field_pair(real, imag):
    return jnp.concatenate([real, imag], axis=0), jnp.concatenate([-imag, real], axis=0)


def project_chunk(base, cosine, sine, straight, turned, weights, select, out_ref, wave_ref):
    rows = straight.shape[0]
    for atom in range(CHUNK):
        wave = cosine[atom : atom + 1, :] * straight + sine[atom : atom + 1, :] * turned
        wave_ref[atom * rows : (atom + 1) * rows, :] = wave.astype(bf16)
    both = dot(wave_ref[...], weights, NT)
    low = lax.broadcasted_iota(jnp.int32, (rows, 128), 1) < 64
    for pair in range(CHUNK // 2):
        even = both[2 * pair * rows : (2 * pair + 1) * rows, :]
        odd = both[(2 * pair + 1) * rows : (2 * pair + 2) * rows, :]
        first = jnp.where(low, even[:, :128], odd[:, :128])
        second = jnp.where(low, even[:, 128:], odd[:, 128:])
        mask = select[pair : pair + 1, :]
        chosen = first * mask + second * (1.0 - mask)
        start = pl.multiple_of((base // 2 + pair) * rows, rows)
        out_ref[pl.ds(start, rows), :] = chosen.astype(bf16)


def first_kernel(
    groups, slot_dev, group_ref, bands_ref, template_ref, miller_ref, positions_ref, species_ref,
    order_ref, out_ref, cos_ref, sin_ref, select_ref, table_ref, wave_ref,
):
    atoms = cos_ref.shape[0]
    table_ref[...] = atom_table(
        positions_ref[...], species_ref[...], order_ref[...], group_ref[0], atoms, groups, slot_dev
    )
    miller = miller_ref[...].astype(f32)
    half = bands_ref.shape[0] // 2
    straight, turned = field_pair(bands_ref[:half, :], bands_ref[half:, :])
    template = template_ref[...]
    weights = jnp.concatenate([template, template[64:, :], template[:64, :]], axis=0)
    low = lax.broadcasted_iota(jnp.int32, (CHUNK // 2, 128), 1) < 64

    def step(block, carry):
        base = pl.multiple_of(block * CHUNK, CHUNK)
        table = table_ref[pl.ds(base, CHUNK), :]
        turns = jnp.zeros((CHUNK, miller.shape[1]), f32)
        for axis in range(3):
            centre = table[:, axis : axis + 1] + table[:, 3 + axis : 4 + axis]
            centre = centre + table[:, 6 + axis : 7 + axis]
            turns = turns + centre * miller[axis : axis + 1, :]
        turns = turns - jnp.round(turns)
        square = turns * turns
        cosine = horner(COS_TURN, square)
        sine = turns * horner(SIN_TURN, square)
        cos_ref[pl.ds(base, CHUNK), :] = cosine
        sin_ref[pl.ds(base, CHUNK), :] = sine
        kinds = table[:, 9:10]
        picked = []
        for pair in range(CHUNK // 2):
            even = 1.0 - kinds[2 * pair : 2 * pair + 1, :]
            odd = kinds[2 * pair + 1 : 2 * pair + 2, :]
            picked.append(jnp.where(low[:1, :], even, odd))
        select = jnp.concatenate(picked, axis=0)
        select_ref[pl.ds(pl.multiple_of(block * (CHUNK // 2), CHUNK // 2), CHUNK // 2), :] = select
        project_chunk(base, cosine, sine, straight, turned, weights, select, out_ref, wave_ref)
        return carry

    lax.fori_loop(0, atoms // CHUNK, step, 0)


def kinetic_of(miller, lengths_ref):
    total = jnp.zeros((1, miller.shape[1]), f32)
    for axis in range(3):
        wave_number = lengths_ref[axis] * miller[axis : axis + 1, :]
        total = total + wave_number * wave_number
    return 0.5 * total


def sum_fields(lengths_ref, fields_ref, miller_ref, parts):
    total = kinetic_of(miller_ref[...].astype(f32), lengths_ref) * fields_ref[...]
    own, core, row, both = [part[...] for part in parts]
    return total + ((own + core) + (row + both))


def next_kernel(
    lengths_ref, fields_ref, miller_ref, own_ref, core_ref, row_ref, both_ref, template_ref,
    cos_ref, sin_ref, select_ref, fields_out_ref, out_ref, wave_ref,
):
    atoms = cos_ref.shape[0]
    fields = sum_fields(lengths_ref, fields_ref, miller_ref, (own_ref, core_ref, row_ref, both_ref))
    fields_out_ref[...] = fields
    half = fields.shape[0] // 2
    straight, turned = field_pair(fields[:half, :], fields[half:, :])
    template = template_ref[...]
    weights = jnp.concatenate([template, template[64:, :], template[:64, :]], axis=0)

    def step(block, carry):
        base = pl.multiple_of(block * CHUNK, CHUNK)
        cosine = cos_ref[pl.ds(base, CHUNK), :]
        sine = sin_ref[pl.ds(base, CHUNK), :]
        select = select_ref[pl.ds(pl.multiple_of(block * (CHUNK // 2), CHUNK // 2), CHUNK // 2), :]
        project_chunk(base, cosine, sine, straight, turned, weights, select, out_ref, wave_ref)
        return carry

    lax.fori_loop(0, atoms // CHUNK, step, 0)


def last_kernel(
    lengths_ref, fields_ref, miller_ref, own_ref, core_ref, row_ref, both_ref, fields_out_ref
):
    fields_out_ref[...] = sum_fields(
        lengths_ref, fields_ref, miller_ref, (own_ref, core_ref, row_ref, both_ref)
    )


def potential_kernel(parts_ref, potential_ref, out_ref):
    summed = jnp.sum(parts_ref[...].astype(f32), axis=0)
    pairs = potential_ref.shape[0]
    rows = summed.shape[0] // pairs
    half = rows // 2
    low = lax.broadcasted_iota(jnp.int32, (64, 128), 1) < 64
    results = []
    for pair in range(pairs):
        blocks = []
        for part in range(2):
            matrices = potential_ref[pair, part].astype(f32)
            blocks.append(jnp.where(low, matrices, 0.0))
            blocks.append(jnp.where(low, 0.0, matrices))
        weights = jnp.concatenate(blocks, axis=0).astype(bf16)
        pieces = jnp.concatenate(three_parts(summed[pair * rows : (pair + 1) * rows, :]), axis=0)
        product = dot(pieces, weights, NT)
        product = product[2 * rows :, :] + product[rows : 2 * rows, :] + product[:rows, :]
        real, imag = product[:, :128], product[:, 128:]
        results.append(real[:half, :] - imag[half:, :])
        results.append(real[half:, :] + imag[:half, :])
    applied = jnp.concatenate(results, axis=0).astype(bf16)
    out_ref[...] = jnp.broadcast_to(applied[None], out_ref.shape)


def return_kernel(applied_ref, template_ref, cos_ref, sin_ref, select_ref, out_ref, stack_ref):
    atoms = cos_ref.shape[0]
    rows, waves = out_ref.shape
    half = rows // 2
    template = template_ref[...]
    weights = jnp.concatenate(
        [template[:64, :], template[:64, :], template[64:, :], template[64:, :]], axis=0
    )
    low = jnp.where(lax.broadcasted_iota(jnp.int32, (1, 128), 1) < 64, 1.0, 0.0)

    def step(block, carry):
        straight, turned = carry
        base = pl.multiple_of(block * CHUNK, CHUNK)
        cosine = cos_ref[pl.ds(base, CHUNK), :]
        sine = sin_ref[pl.ds(base, CHUNK), :]
        select = select_ref[pl.ds(pl.multiple_of(block * (CHUNK // 2), CHUNK // 2), CHUNK // 2), :]
        for pair in range(CHUNK // 2):
            start = pl.multiple_of((base // 2 + pair) * rows, rows)
            applied = applied_ref[pl.ds(start, rows), :].astype(f32)
            mask = select[pair : pair + 1, :]
            is_first = low * mask + (1.0 - low) * (1.0 - mask)
            kept, other = applied * is_first, applied * (1.0 - is_first)
            top = slice(2 * pair * rows, (2 * pair + 1) * rows)
            bottom = slice((2 * pair + 1) * rows, (2 * pair + 2) * rows)
            stack_ref[top, :128] = (kept * low).astype(bf16)
            stack_ref[top, 128:] = (other * low).astype(bf16)
            stack_ref[bottom, :128] = (kept * (1.0 - low)).astype(bf16)
            stack_ref[bottom, 128:] = (other * (1.0 - low)).astype(bf16)
        images = dot(stack_ref[...], weights, NN)
        for atom in range(CHUNK):
            image = images[atom * rows : (atom + 1) * rows, :]
            straight = straight + cosine[atom : atom + 1, :] * image
            turned = turned + sine[atom : atom + 1, :] * image
        return straight, turned

    zero = jnp.zeros((rows, waves), f32)
    straight, turned = lax.fori_loop(0, atoms // CHUNK, step, (zero, zero))
    out_ref[:half, :] = straight[:half, :] + turned[half:, :]
    out_ref[half:, :] = straight[half:, :] - turned[:half, :]


def vmem(count):
    return [pl.BlockSpec(memory_space=pltpu.VMEM)] * count


def smem(count):
    return [pl.BlockSpec(memory_space=pltpu.SMEM)] * count


def shape(dims, dtype):
    return jax.ShapeDtypeStruct(dims, dtype)


def per_device(bands_in, template, potential, miller, positions, species, atom_order, reciprocal):
    pw_count = lax.axis_size("pw")
    group_count = lax.axis_size("atom")
    slot_dev = potential.shape[0]
    atoms = slot_dev * pw_count
    species_count, harmonics, waves = template.shape
    rows = 2 * bands_in.shape[1]
    pairs = slot_dev // 2
    message = pairs * rows
    template = template.reshape(species_count * harmonics, waves)
    fields = bands_in.reshape(rows, waves)
    matrices = potential.reshape(pairs, 2, 2, harmonics, harmonics)
    matrices = matrices.transpose(0, 2, 3, 1, 4).reshape(pairs, 2, harmonics, 2 * harmonics)
    group = lax.axis_index("atom").astype(jnp.int32).reshape(1)
    coefs_shape = shape((atoms // 2 * rows, 2 * harmonics), bf16)
    fields_shape = shape((rows, waves), f32)
    phase_shape = shape((atoms, waves), f32)
    wave_scratch = pltpu.VMEM((CHUNK * rows, waves), bf16)

    coefs, cosine, sine, select = pl.pallas_call(
        functools.partial(first_kernel, group_count, slot_dev),
        in_specs=smem(1) + vmem(6),
        out_specs=tuple(vmem(4)),
        out_shape=(coefs_shape, phase_shape, phase_shape, shape((atoms // 2, 128), f32)),
        scratch_shapes=[pltpu.VMEM((atoms, 16), f32), wave_scratch],
        name="first",
    )(group, fields, template, miller, positions, species.reshape(1, -1), atom_order.reshape(1, -1))

    def return_fields(coefs):
        parts = lax.all_to_all(
            coefs.reshape(pw_count, message, 2 * harmonics), "pw", 0, 0, tiled=True
        )
        applied = pl.pallas_call(
            potential_kernel,
            in_specs=vmem(2),
            out_specs=vmem(1)[0],
            out_shape=shape((pw_count, message, 2 * harmonics), bf16),
            name="potential",
        )(parts, matrices)
        applied = lax.all_to_all(applied, "pw", 0, 0, tiled=True)
        own = pl.pallas_call(
            return_kernel,
            in_specs=vmem(5),
            out_specs=vmem(1)[0],
            out_shape=fields_shape,
            scratch_shapes=[pltpu.VMEM((CHUNK * rows, 4 * harmonics), bf16)],
            name="back",
        )(applied.reshape(atoms // 2 * rows, 2 * harmonics), template, cosine, sine, select)
        others = [
            lax.ppermute(own, "atom", [(source, source ^ flip) for source in range(group_count)])
            for flip in range(1, group_count)
        ]
        return [own] + others

    parts = return_fields(coefs)
    once, coefs = pl.pallas_call(
        next_kernel,
        in_specs=smem(1) + vmem(10),
        out_specs=tuple(vmem(2)),
        out_shape=(fields_shape, coefs_shape),
        scratch_shapes=[wave_scratch],
        name="next",
    )(reciprocal, fields, miller, *parts, template, cosine, sine, select)
    parts = return_fields(coefs)
    twice = pl.pallas_call(
        last_kernel,
        in_specs=smem(1) + vmem(6),
        out_specs=vmem(1)[0],
        out_shape=fields_shape,
        name="last",
    )(reciprocal, once, miller, *parts)
    return once.reshape(bands_in.shape), twice.reshape(bands_in.shape)


def solution(mesh):
    in_specs = (
        P(None, None, "pw"),
        P(None, None, "pw"),
        P(("pw", "atom"), None),
        P(None, "pw"),
        P(),
        P(),
        P(),
        P(),
    )
    out_specs = (P(None, None, "pw"), P(None, None, "pw"))
    return jax.shard_map(
        per_device, mesh=mesh, in_specs=in_specs, out_specs=out_specs, check_vma=False
    )
```

time: 1700 us -> 153 us (0.09)
  waiting for transfers between devices: 1400 us -> 21.7 us
  matrix products: 71.7 us -> 0 us
  local copies, waits for them, and re-layouts: 73.1 us -> 3.68 us
  blocking collectives: 114 us -> 66.3 us
  Pallas kernels: 0 us -> 33.4 us
  starting transfers between devices: 0.3 us -> 26.2 us
  other arithmetic: 18.1 us -> 0 us
    psum x2 -> x0, waiting for transfers between devices: 1170 us -> none  [apply_once(): summed = lax.psum(coeffs, 'pw')]
    all_gather x1 -> x0, waiting for transfers between devices: 224 us -> none  [apply_once(): segment = lax.all_gather(potential, 'pw', axis=0, tiled=True)]
    psum x2 -> x0, blocking collectives: 114 us -> none  [apply_once(): return lax.psum(summed_up, 'atom') + kinetic[None, None, :] * fields]
    dot_general x40 -> x0, matrix products: 71.7 us -> none  [the longest x8 62.5 us: product(): jnp.einsum('alm,amb->alb', matrices, vectors, precision=lax.Precision.HIG...]
    all_to_all x0 -> x3, blocking collectives: none -> 66.3 us  [the longest x2 43.9 us: return_fields(): applied = lax.all_to_all(applied, 'pw', 0, 0, tiled=True)]
    dynamic_slice x64 -> x0, local copies, waits for them, and re-layouts: 38.2 us -> none  [the longest x16 13.8 us: returned(): sin_part = lax.dynamic_slice_in_dim(sin_all, first_row, block_size, 0)]
    pallas_call x0 -> x7, Pallas kernels: none -> 33.4 us  [the longest x2 11.7 us: return_fields(): pl.pallas_call(return_kernel, in_specs=vmem(5), out_specs=vmem(1)[0], out...]
  transfers between devices with their start and end apart: 3 -> 7, of which waited for: 3 -> 4; matrix products, arithmetic and copies ran while one was open for 3% -> 1% of each run, Pallas kernels for 0% -> 0%
where the time goes in v1:
time: 153 us; the launch traced here: 152 us
  blocking collectives  66.3 us (43%)
  Pallas kernels  33.4 us (22%)
  starting transfers between devices  26.2 us (17%)
  waiting for transfers between devices  21.7 us (14%)
  local copies, waits for them, and re-layouts  3.68 us (2%)
    all_to_all x2, blocking collectives, return_fields(): applied = lax.all_to_all(applied, 'pw', 0, 0, tiled=True)  43.9 us
    all_to_all x1, blocking collectives, return_fields(): lax.all_to_all(coefs.reshape(pw_count, message, 2 * harmonics), 'pw', 0,...  22.4 us
    all_to_all x1, waiting for transfers between devices, return_fields(): lax.all_to_all(coefs.reshape(pw_count, message, 2 * harmonics), 'pw', 0,...  15.1 us
    all_to_all x1, starting transfers between devices, return_fields(): lax.all_to_all(coefs.reshape(pw_count, message, 2 * harmonics), 'pw', 0,...  13.6 us
    ppermute x6, starting transfers between devices, return_fields(): lax.ppermute(own, 'atom', [(source, source ^ flip) for source in range(gr...  12.6 us
    pallas_call x2, Pallas kernels, return_fields(): pl.pallas_call(return_kernel, in_specs=vmem(5), out_specs=vmem(1)[0], out...  11.7 us
    pallas_call x1, Pallas kernels, per_device(): pl.pallas_call(functools.partial(first_kernel, group_count, slot_dev), in...  9.41 us
    ppermute x6, waiting for transfers between devices, return_fields(): lax.ppermute(own, 'atom', [(source, source ^ flip) for source in range(gr...  6.62 us
  transfers between devices with their start and end apart: 7, of which 4 were waited for; matrix products, arithmetic and copies ran while one was open for 1% of the time, Pallas kernels for 0%

profile of v1, /device:TPU:1, one launch (start us, length us, event | category | flops | bytes accessed | tf_op | source)
XLA Modules:
  0.0 152.0 jit_solution(10647102438971641663)
XLA Ops:
  0.6 9.4 %first.1 = (bf16[2048,128]{1,0:T(8,128)(2,1)}, f32[256,512]{1,0:T(8,128)}, f32[256,512]{1,0:T(8,128)}, f32[128,128]{1,0:T(8,128)}) custom-call(s32[1]{0:T(128)} %bitcast.1.group_ref, f32[16,512]{1,0:T(8,128)} %bitcast.23, bf16[128,512]{1,0:T(8,128)(2,1)} %bitcast.14, s32[3,512]{1,0:T(4,128)} %miller_ref.5, f32[3,1024]{1,0:T(4,128)} %positions_ref.1, ...), custom_call_target="tpu_custom_call" | custom-call | tf_op jit(solution)/shard_map/first/pallas_call | solution.py:279
  10.0 13.6 %all-to-all-start = ((bf16[64,32,128]{2,1,0:T(8,128)(2,1)}), bf16[64,32,128]{2,1,0:T(8,128)(2,1)S(1)}, u32[]{:S(2)}, u32[]{:S(2)}) async-start(bf16[64,32,128]{2,1,0:T(8,128)(2,1)} %bitcast.20), calls=%async_computation | async-start | bytes 1048576 | tf_op jit(solution)/shard_map/all_to_all | solution.py:289
  23.7 0.2 reshape.49
  23.8 0.1 copy.12
  24.0 0.7 reshape.50.potential_ref
  24.7 15.1 %all-to-all-done.parts_ref = bf16[64,32,128]{2,1,0:T(8,128)(2,1)S(1)} async-done(((bf16[64,32,128]{2,1,0:T(8,128)(2,1)}), bf16[64,32,128]{2,1,0:T(8,128)(2,1)S(1)}, u32[]{:S(2)}, u32[]{:S(2)}) %all-to-all-start) | async-done | bytes 524320 | tf_op jit(solution)/shard_map/all_to_all | solution.py:289
  39.8 0.8 copy-done
  40.6 2.1 %potential.2 = bf16[64,32,128]{2,1,0:T(8,128)(2,1)} custom-call(bf16[64,32,128]{2,1,0:T(8,128)(2,1)} %copy-done, bf16[2,2,64,128]{3,2,1,0:T(8,128)(2,1)} %reshape.50.potential_ref), custom_call_target="tpu_custom_call" | custom-call | tf_op jit(solution)/shard_map/potential/pallas_call | solution.py:292
  42.8 21.8 %all_to_all.20 = bf16[64,32,128]{2,1,0:T(8,128)(2,1)} all-to-all(bf16[64,32,128]{2,1,0:T(8,128)(2,1)} %potential.2), channel_id=1, replica_groups=mesh['pw'=64,'atom'=4] {'pw'}, dimensions={0} | all-to-all | bytes 1048576 | tf_op jit(solution)/shard_map/all_to_all | solution.py:299
  64.6 5.8 %back.2.own_ref = f32[16,512]{1,0:T(8,128)} custom-call(bf16[2048,128]{1,0:T(8,128)(2,1)} %bitcast.19, bf16[128,512]{1,0:T(8,128)(2,1)} %bitcast.15, f32[256,512]{1,0:T(8,128)} %get-tuple-element.9.cos_ref, f32[256,512]{1,0:T(8,128)} %get-tuple-element.10.sin_ref, f32[128,128]{1,0:T(8,128)} %get-tuple-element.11.select_ref), custom_call_target="tpu_custom_call" | custom-call | tf_op jit(solution)/shard_map/back/pallas_call | solution.py:300
  70.4 6.3 %collective-permute-start.2 = (f32[16,512]{1,0:T(8,128)}, f32[16,512]{1,0:T(8,128)S(1)}, u32[]{:S(2)}, u32[]{:S(2)}) collective-permute-start(f32[16,512]{1,0:T(8,128)} %back.2.own_ref), channel_id=1, source_target_pairs={{0,3},{1,2},{2,1},{3,0},{4,7},{5,6},{6,5},{7,4},{8,11},{9,10},{10,... | collective-permute-start | bytes 98312 | tf_op jit(solution)/shard_map/ppermute | solution.py:309
  76.8 0.3 collective-permute-start.1
  77.1 0.1 collective-permute-start
  77.2 2.0 %collective-permute-done.2.both_ref = f32[16,512]{1,0:T(8,128)S(1)} collective-permute-done((f32[16,512]{1,0:T(8,128)}, f32[16,512]{1,0:T(8,128)S(1)}, u32[]{:S(2)}, u32[]{:S(2)}) %collective-permute-start.2) | collective-permute-done | bytes 32800 | tf_op jit(solution)/shard_map/ppermute | solution.py:309
  79.2 2.1 %collective-permute-done.1.row_ref = f32[16,512]{1,0:T(8,128)S(1)} collective-permute-done((f32[16,512]{1,0:T(8,128)}, f32[16,512]{1,0:T(8,128)S(1)}, u32[]{:S(2)}, u32[]{:S(2)}) %collective-permute-start.1) | collective-permute-done | bytes 32800 | tf_op jit(solution)/shard_map/ppermute | solution.py:309
  81.3 0.0 collective-permute-done.core_ref
  81.3 0.6 copy-done.4
  81.9 0.6 copy-done.6
  82.5 6.6 %next.1 = (f32[16,512]{1,0:T(8,128)}, bf16[2048,128]{1,0:T(8,128)(2,1)}) custom-call(f32[3]{0:T(128)} %lengths_ref.3, f32[16,512]{1,0:T(8,128)} %bitcast.24, s32[3,512]{1,0:T(4,128)} %miller_ref.5, f32[16,512]{1,0:T(8,128)} %back.2.own_ref, f32[16,512]{1,0:T(8,128)} %copy-done.6, f32[16,512]{1,0:T(8,128)} %copy-done.4, f32[16,512]{1,0:T(8,128)} %copy-done.2, ...), custom_call_target="tpu_custom_call" | custom-call | tf_op jit(solution)/shard_map/next/pallas_call | solution.py:315
  89.0 22.4 %all_to_all.21.parts_ref = bf16[64,32,128]{2,1,0:T(8,128)(2,1)} all-to-all(bf16[64,32,128]{2,1,0:T(8,128)(2,1)} %bitcast.21), channel_id=1, replica_groups=mesh['pw'=64,'atom'=4] {'pw'}, dimensions={0} | all-to-all | bytes 1048576 | tf_op jit(solution)/shard_map/all_to_all | solution.py:289
  111.5 2.1 %potential.3 = bf16[64,32,128]{2,1,0:T(8,128)(2,1)} custom-call(bf16[64,32,128]{2,1,0:T(8,128)(2,1)} %all_to_all.21.parts_ref, bf16[2,2,64,128]{3,2,1,0:T(8,128)(2,1)} %reshape.50.potential_ref), custom_call_target="tpu_custom_call" | custom-call | tf_op jit(solution)/shard_map/potential/pallas_call | solution.py:292
  113.6 22.1 %all_to_all.22 = bf16[64,32,128]{2,1,0:T(8,128)(2,1)} all-to-all(bf16[64,32,128]{2,1,0:T(8,128)(2,1)} %potential.3), channel_id=1, replica_groups=mesh['pw'=64,'atom'=4] {'pw'}, dimensions={0} | all-to-all | bytes 1048576 | tf_op jit(solution)/shard_map/all_to_all | solution.py:299
  135.6 5.8 %back.3.own_ref = f32[16,512]{1,0:T(8,128)} custom-call(bf16[2048,128]{1,0:T(8,128)(2,1)} %bitcast.18, bf16[128,512]{1,0:T(8,128)(2,1)} %bitcast.17, f32[256,512]{1,0:T(8,128)} %get-tuple-element.9.cos_ref, f32[256,512]{1,0:T(8,128)} %get-tuple-element.10.sin_ref, f32[128,128]{1,0:T(8,128)} %get-tuple-element.11.select_ref), custom_call_target="tpu_custom_call" | custom-call | tf_op jit(solution)/shard_map/back/pallas_call | solution.py:300
  141.5 3.6 %collective-permute-start.5 = (f32[16,512]{1,0:T(8,128)}, f32[16,512]{1,0:T(8,128)S(1)}, u32[]{:S(2)}, u32[]{:S(2)}) collective-permute-start(f32[16,512]{1,0:T(8,128)} %back.3.own_ref), channel_id=1, source_target_pairs={{0,3},{1,2},{2,1},{3,0},{4,7},{5,6},{6,5},{7,4},{8,11},{9,10},{10,... | collective-permute-start | bytes 98312 | tf_op jit(solution)/shard_map/ppermute | solution.py:309
  145.1 2.2 %collective-permute-start.4 = (f32[16,512]{1,0:T(8,128)}, f32[16,512]{1,0:T(8,128)S(1)}, u32[]{:S(2)}, u32[]{:S(2)}) collective-permute-start(f32[16,512]{1,0:T(8,128)} %back.3.own_ref), channel_id=1, source_target_pairs={{0,2},{1,3},{2,0},{3,1},{4,6},{5,7},{6,4},{7,5},{8,10},{9,11},{10,... | collective-permute-start | bytes 98312 | tf_op jit(solution)/shard_map/ppermute | solution.py:309
  147.3 0.0 collective-permute-start.3
  147.3 0.0 collective-permute-done.5.both_ref
  147.3 2.5 %collective-permute-done.4.row_ref = f32[16,512]{1,0:T(8,128)S(1)} collective-permute-done((f32[16,512]{1,0:T(8,128)}, f32[16,512]{1,0:T(8,128)S(1)}, u32[]{:S(2)}, u32[]{:S(2)}) %collective-permute-start.4) | collective-permute-done | bytes 32800 | tf_op jit(solution)/shard_map/ppermute | solution.py:309
  149.9 0.0 collective-permute-done.3.core_ref
  149.9 0.6 copy-done.5
  150.5 0.0 copy-done.7
  150.5 1.5 last.1
  (11 shorter events, 0.0 us)
Async XLA Ops:
  10.0 13.6 %copy-start.1 = (bf16[4,8192]{1,0:T(4,128)(2,1)S(1)}, bf16[4,8192]{1,0:T(4,128)(2,1)}, u32[]{:S(2)}) copy-start(bf16[4,8192]{1,0:T(4,128)(2,1)} %param.10) | copy-start | bytes 196612
  10.0 29.8 %all-to-all-start = ((bf16[64,32,128]{2,1,0:T(8,128)(2,1)}), bf16[64,32,128]{2,1,0:T(8,128)(2,1)S(1)}, u32[]{:S(2)}, u32[]{:S(2)}) async-start(bf16[64,32,128]{2,1,0:T(8,128)(2,1)} %bitcast.20), calls=%async_computation | async-start | bytes 1048576 | tf_op jit(solution)/shard_map/all_to_all | solution.py:289
  39.8 0.8 copy-start
  70.4 8.8 %collective-permute-start.2 = (f32[16,512]{1,0:T(8,128)}, f32[16,512]{1,0:T(8,128)S(1)}, u32[]{:S(2)}, u32[]{:S(2)}) collective-permute-start(f32[16,512]{1,0:T(8,128)} %back.2.own_ref), channel_id=1, source_target_pairs={{0,3},{1,2},{2,1},{3,0},{4,7},{5,6},{6,5},{7,4},{8,11},{9,10},{10,... | collective-permute-start | bytes 98312 | tf_op jit(solution)/shard_map/ppermute | solution.py:309
  76.8 4.5 %collective-permute-start.1 = (f32[16,512]{1,0:T(8,128)}, f32[16,512]{1,0:T(8,128)S(1)}, u32[]{:S(2)}, u32[]{:S(2)}) collective-permute-start(f32[16,512]{1,0:T(8,128)} %back.2.own_ref), channel_id=1, source_target_pairs={{0,2},{1,3},{2,0},{3,1},{4,6},{5,7},{6,4},{7,5},{8,10},{9,11},{10,... | collective-permute-start | bytes 98312 | tf_op jit(solution)/shard_map/ppermute | solution.py:309
  77.1 4.1 %collective-permute-start = (f32[16,512]{1,0:T(8,128)}, f32[16,512]{1,0:T(8,128)S(1)}, u32[]{:S(2)}, u32[]{:S(2)}) collective-permute-start(f32[16,512]{1,0:T(8,128)} %back.2.own_ref), channel_id=1, source_target_pairs={{0,1},{1,0},{2,3},{3,2},{4,5},{5,4},{6,7},{7,6},{8,9},{9,8},{10,11... | collective-permute-start | bytes 98312 | tf_op jit(solution)/shard_map/ppermute | solution.py:309
  79.2 2.1 %copy-start.2 = (f32[16,512]{1,0:T(8,128)}, f32[16,512]{1,0:T(8,128)S(1)}, u32[]{:S(2)}) copy-start(f32[16,512]{1,0:T(8,128)S(1)} %collective-permute-done.2.both_ref) | copy-start | bytes 98308
  81.3 0.6 copy-start.4
  81.9 0.6 copy-start.6
  141.5 5.9 %collective-permute-start.5 = (f32[16,512]{1,0:T(8,128)}, f32[16,512]{1,0:T(8,128)S(1)}, u32[]{:S(2)}, u32[]{:S(2)}) collective-permute-start(f32[16,512]{1,0:T(8,128)} %back.3.own_ref), channel_id=1, source_target_pairs={{0,3},{1,2},{2,1},{3,0},{4,7},{5,6},{6,5},{7,4},{8,11},{9,10},{10,... | collective-permute-start | bytes 98312 | tf_op jit(solution)/shard_map/ppermute | solution.py:309
  145.1 4.8 %collective-permute-start.4 = (f32[16,512]{1,0:T(8,128)}, f32[16,512]{1,0:T(8,128)S(1)}, u32[]{:S(2)}, u32[]{:S(2)}) collective-permute-start(f32[16,512]{1,0:T(8,128)} %back.3.own_ref), channel_id=1, source_target_pairs={{0,2},{1,3},{2,0},{3,1},{4,6},{5,7},{6,4},{7,5},{8,10},{9,11},{10,... | collective-permute-start | bytes 98312 | tf_op jit(solution)/shard_map/ppermute | solution.py:309
  147.3 2.6 %collective-permute-start.3 = (f32[16,512]{1,0:T(8,128)}, f32[16,512]{1,0:T(8,128)S(1)}, u32[]{:S(2)}, u32[]{:S(2)}) collective-permute-start(f32[16,512]{1,0:T(8,128)} %back.3.own_ref), channel_id=1, source_target_pairs={{0,1},{1,0},{2,3},{3,2},{4,5},{5,4},{6,7},{7,6},{8,9},{9,8},{10,11... | collective-permute-start | bytes 98312 | tf_op jit(solution)/shard_map/ppermute | solution.py:309
  147.3 2.5 %copy-start.3 = (f32[16,512]{1,0:T(8,128)}, f32[16,512]{1,0:T(8,128)S(1)}, u32[]{:S(2)}) copy-start(f32[16,512]{1,0:T(8,128)S(1)} %collective-permute-done.5.both_ref) | copy-start | bytes 98308
  149.9 0.6 copy-start.5
  149.9 0.6 copy-start.7

commit v2 on v1

v2 whole, which is shorter than its diff:
```python
import functools

import jax
import jax.numpy as jnp
from jax import lax
from jax.experimental import pallas as pl
from jax.experimental.pallas import tpu as pltpu
from jax.sharding import Mesh
from jax.sharding import PartitionSpec as P

f32 = jnp.float32
bf16 = jnp.bfloat16

COS_TURN = (
    0.9999999890590225,
    -19.739204499453912,
    64.93911745989556,
    -85.45013953088248,
    60.167630950949295,
    -25.96759924849463,
    6.528658161366808,
)
SIN_TURN = (
    6.283185302511503,
    -41.34170040531749,
    81.60513138579344,
    -76.70301535379849,
    42.02592698556796,
    -14.899846667364866,
    3.238137509743233,
)
NT = (((1,), (1,)), ((), ()))
NN = (((1,), (0,)), ((), ()))
CHUNK = 16


def dot(left, right, dims):
    return lax.dot_general(left, right, dims, preferred_element_type=f32)


def horner(coefs, arg):
    total = jnp.full_like(arg, coefs[-1])
    for coef in coefs[-2::-1]:
        total = total * arg + coef
    return total


def three_parts(values):
    high = values.astype(bf16)
    rest = values - high.astype(f32)
    middle = rest.astype(bf16)
    low = (rest - middle.astype(f32)).astype(bf16)
    return high, middle, low


def atom_table(positions, species, order, group, rows, groups, slot_dev):
    atoms = order.shape[1]
    row = lax.broadcasted_iota(jnp.int32, (rows, atoms), 0)
    lane = lax.broadcasted_iota(jnp.int32, (rows, atoms), 1)
    slot = (row // slot_dev * groups + group) * slot_dev + row % slot_dev
    pick_slot = jnp.where(lane == slot, 1.0, 0.0).astype(bf16)
    coarse, fine = order // 128, order % 128
    pad = jnp.zeros((14, atoms), f32)
    digits = jnp.concatenate([coarse.astype(f32), fine.astype(f32), pad], axis=0).astype(bf16)
    found = dot(pick_slot, digits, NT)
    atom = (found[:, 0:1] * 128.0 + found[:, 1:2]).astype(jnp.int32)
    pick_atom = jnp.where(lane == atom, 1.0, 0.0).astype(bf16)
    high, middle, low = three_parts(positions)
    pad = jnp.zeros((6, atoms), bf16)
    facts = jnp.concatenate([high, middle, low, species.astype(f32).astype(bf16), pad], axis=0)
    return dot(pick_atom, facts, NT)


def field_pair(fields):
    half = fields.shape[0] // 2
    return fields, jnp.concatenate([-fields[half:, :], fields[:half, :]], axis=0)


def project_weights(template):
    return jnp.concatenate([template, template[64:, :], template[:64, :]], axis=0)


def phases_of(table, miller):
    turns = jnp.zeros((table.shape[0], miller.shape[1]), f32)
    for axis in range(3):
        centre = table[:, axis : axis + 1] + table[:, 3 + axis : 4 + axis]
        centre = centre + table[:, 6 + axis : 7 + axis]
        turns = turns + centre * miller[axis : axis + 1, :]
    turns = turns - jnp.round(turns)
    square = turns * turns
    return horner(COS_TURN, square), turns * horner(SIN_TURN, square)


def prepare_kernel(
    groups, slot_dev, group_ref, miller_ref, positions_ref, species_ref, order_ref,
    cos_ref, sin_ref, select_ref, table_ref,
):
    atoms = cos_ref.shape[0]
    table_ref[...] = atom_table(
        positions_ref[...], species_ref[...], order_ref[...], group_ref[0], atoms, groups, slot_dev
    )
    miller = miller_ref[...].astype(f32)
    low = lax.broadcasted_iota(jnp.int32, (1, 128), 1) < 64

    def step(block, carry):
        base = pl.multiple_of(block * CHUNK, CHUNK)
        table = table_ref[pl.ds(base, CHUNK), :]
        cosine, sine = phases_of(table, miller)
        cos_ref[pl.ds(base, CHUNK), :] = cosine
        sin_ref[pl.ds(base, CHUNK), :] = sine
        kinds = table[:, 9:10]
        picked = []
        for pair in range(CHUNK // 2):
            even = 1.0 - kinds[2 * pair : 2 * pair + 1, :]
            odd = kinds[2 * pair + 1 : 2 * pair + 2, :]
            picked.append(jnp.where(low, even, odd))
        size = CHUNK // 2
        select_ref[pl.ds(pl.multiple_of(block * size, size), size), :] = jnp.concatenate(
            picked, axis=0
        )
        return carry

    lax.fori_loop(0, atoms // CHUNK, step, 0)


def project_chunk(base, phases, fields, weights, select, out_ref, wave_ref):
    rows = fields[0][0].shape[0]
    both = None
    for side in range(2):
        cosine, sine = phases[side]
        straight, turned = fields[side]
        for atom in range(CHUNK):
            wave = cosine[atom : atom + 1, :] * straight + sine[atom : atom + 1, :] * turned
            wave_ref[side, atom * rows : (atom + 1) * rows, :] = wave.astype(bf16)
        product = dot(wave_ref[side], weights[side], NT)
        both = product if both is None else both + product
    low = lax.broadcasted_iota(jnp.int32, (rows, 128), 1) < 64
    for pair in range(CHUNK // 2):
        even = both[2 * pair * rows : (2 * pair + 1) * rows, :]
        odd = both[(2 * pair + 1) * rows : (2 * pair + 2) * rows, :]
        first = jnp.where(low, even[:, :128], odd[:, :128])
        second = jnp.where(low, even[:, 128:], odd[:, 128:])
        mask = select[pair : pair + 1, :]
        chosen = first * mask + second * (1.0 - mask)
        start = pl.multiple_of((base // 2 + pair) * rows, rows)
        out_ref[pl.ds(start, rows), :] = chosen.astype(bf16)


def first_kernel(
    table_ref, miller_ref, own_fields_ref, fields_ref, own_template_ref, template_ref,
    own_cos_ref, own_sin_ref, select_ref, out_ref, cos_ref, sin_ref, wave_ref,
):
    miller = miller_ref[...].astype(f32)
    fields = [field_pair(own_fields_ref[...]), field_pair(fields_ref[...])]
    weights = [project_weights(own_template_ref[...]), project_weights(template_ref[...])]

    def step(block, carry):
        base = pl.multiple_of(block * CHUNK, CHUNK)
        chunk = pl.ds(base, CHUNK)
        other = phases_of(table_ref[chunk, :], miller)
        cos_ref[chunk, :] = other[0]
        sin_ref[chunk, :] = other[1]
        phases = [(own_cos_ref[chunk, :], own_sin_ref[chunk, :]), other]
        size = CHUNK // 2
        select = select_ref[pl.ds(pl.multiple_of(block * size, size), size), :]
        project_chunk(base, phases, fields, weights, select, out_ref, wave_ref)
        return carry

    lax.fori_loop(0, cos_ref.shape[0] // CHUNK, step, 0)


def kinetic_of(miller_ref, lengths_ref):
    miller = miller_ref[...].astype(f32)
    total = jnp.zeros((1, miller.shape[1]), f32)
    for axis in range(3):
        wave_number = lengths_ref[axis] * miller[axis : axis + 1, :]
        total = total + wave_number * wave_number
    return 0.5 * total


def next_kernel(
    lengths_ref, own_miller_ref, miller_ref, own_fields_ref, fields_ref, mine_ref, low_ref,
    high_ref, both_ref, own_template_ref, template_ref, own_cos_ref, own_sin_ref, cos_ref, sin_ref,
    select_ref, fields_out_ref, out_ref, wave_ref,
):
    own = kinetic_of(own_miller_ref, lengths_ref) * own_fields_ref[...]
    own = own + ((mine_ref[0] + high_ref[0]) + (low_ref[1] + both_ref[1]))
    fields_out_ref[...] = own
    other = kinetic_of(miller_ref, lengths_ref) * fields_ref[...]
    other = other + ((mine_ref[1] + high_ref[1]) + (low_ref[0] + both_ref[0]))
    fields = [field_pair(own), field_pair(other)]
    weights = [project_weights(own_template_ref[...]), project_weights(template_ref[...])]

    def step(block, carry):
        base = pl.multiple_of(block * CHUNK, CHUNK)
        chunk = pl.ds(base, CHUNK)
        phases = [
            (own_cos_ref[chunk, :], own_sin_ref[chunk, :]),
            (cos_ref[chunk, :], sin_ref[chunk, :]),
        ]
        size = CHUNK // 2
        select = select_ref[pl.ds(pl.multiple_of(block * size, size), size), :]
        project_chunk(base, phases, fields, weights, select, out_ref, wave_ref)
        return carry

    lax.fori_loop(0, cos_ref.shape[0] // CHUNK, step, 0)


def last_kernel(
    lengths_ref, miller_ref, fields_ref, mine_ref, low_ref, high_ref, both_ref, fields_out_ref
):
    total = kinetic_of(miller_ref, lengths_ref) * fields_ref[...]
    fields_out_ref[...] = total + ((mine_ref[0] + high_ref[...]) + (low_ref[...] + both_ref[...]))


def potential_kernel(parts_ref, potential_ref, out_ref):
    summed = jnp.sum(parts_ref[...].astype(f32), axis=0)
    pairs = potential_ref.shape[0]
    rows = summed.shape[0] // pairs
    half = rows // 2
    low = lax.broadcasted_iota(jnp.int32, (64, 128), 1) < 64
    results = []
    for pair in range(pairs):
        blocks = []
        for part in range(2):
            matrices = potential_ref[pair, part].astype(f32)
            blocks.append(jnp.where(low, matrices, 0.0))
            blocks.append(jnp.where(low, 0.0, matrices))
        weights = jnp.concatenate(blocks, axis=0).astype(bf16)
        pieces = jnp.concatenate(three_parts(summed[pair * rows : (pair + 1) * rows, :]), axis=0)
        product = dot(pieces, weights, NT)
        product = product[2 * rows :, :] + product[rows : 2 * rows, :] + product[:rows, :]
        real, imag = product[:, :128], product[:, 128:]
        results.append(real[:half, :] - imag[half:, :])
        results.append(real[half:, :] + imag[:half, :])
    applied = jnp.concatenate(results, axis=0).astype(bf16)
    out_ref[...] = jnp.broadcast_to(applied[None], out_ref.shape)


def return_kernel(
    applied_ref, own_template_ref, template_ref, own_cos_ref, own_sin_ref, cos_ref, sin_ref,
    select_ref, out_ref, stack_ref,
):
    atoms = cos_ref.shape[0]
    _, rows, waves = out_ref.shape
    half = rows // 2
    weights = []
    for ref in (own_template_ref, template_ref):
        low, high = ref[:64, :], ref[64:, :]
        weights.append(jnp.concatenate([low, low, high, high], axis=0))
    low = jnp.where(lax.broadcasted_iota(jnp.int32, (1, 128), 1) < 64, 1.0, 0.0)
    zero = jnp.zeros((rows, waves), f32)

    def step(block, carry):
        base = pl.multiple_of(block * CHUNK, CHUNK)
        chunk = pl.ds(base, CHUNK)
        size = CHUNK // 2
        select = select_ref[pl.ds(pl.multiple_of(block * size, size), size), :]
        for pair in range(CHUNK // 2):
            start = pl.multiple_of((base // 2 + pair) * rows, rows)
            applied = applied_ref[pl.ds(start, rows), :].astype(f32)
            mask = select[pair : pair + 1, :]
            is_first = low * mask + (1.0 - low) * (1.0 - mask)
            kept, other = applied * is_first, applied * (1.0 - is_first)
            top = slice(2 * pair * rows, (2 * pair + 1) * rows)
            bottom = slice((2 * pair + 1) * rows, (2 * pair + 2) * rows)
            stack_ref[top, :128] = (kept * low).astype(bf16)
            stack_ref[top, 128:] = (other * low).astype(bf16)
            stack_ref[bottom, :128] = (kept * (1.0 - low)).astype(bf16)
            stack_ref[bottom, 128:] = (other * (1.0 - low)).astype(bf16)
        sums = []
        for side, (cosines, sines) in enumerate(((own_cos_ref, own_sin_ref), (cos_ref, sin_ref))):
            straight, turned = carry[side]
            cosine, sine = cosines[chunk, :], sines[chunk, :]
            images = dot(stack_ref[...], weights[side], NN)
            for atom in range(CHUNK):
                image = images[atom * rows : (atom + 1) * rows, :]
                straight = straight + cosine[atom : atom + 1, :] * image
                turned = turned + sine[atom : atom + 1, :] * image
            sums.append((straight, turned))
        return tuple(sums)

    sums = lax.fori_loop(0, atoms // CHUNK, step, ((zero, zero), (zero, zero)))
    for side, (straight, turned) in enumerate(sums):
        out_ref[side, :half, :] = straight[:half, :] + turned[half:, :]
        out_ref[side, half:, :] = straight[half:, :] - turned[:half, :]


def vmem(count):
    return [pl.BlockSpec(memory_space=pltpu.VMEM)] * count


def smem(count):
    return [pl.BlockSpec(memory_space=pltpu.SMEM)] * count


def shape(dims, dtype):
    return jax.ShapeDtypeStruct(dims, dtype)


def flip(array, *axes):
    pairs = [(place, 2 ** len(axes) - 1 - place) for place in range(2 ** len(axes))]
    return lax.ppermute(array, axes, pairs)


def per_device(bands_in, template, potential, miller, positions, species, atom_order, reciprocal):
    plane = lax.axis_size("zx")
    groups = lax.axis_size("yh") * lax.axis_size("core")
    slot_dev = potential.shape[0]
    atoms = slot_dev * plane
    species_count, harmonics, waves = template.shape
    rows = 2 * bands_in.shape[1]
    pairs = slot_dev // 2
    message = pairs * rows
    width = 2 * harmonics
    template = template.reshape(species_count * harmonics, waves)
    fields = bands_in.reshape(rows, waves)
    matrices = potential.reshape(pairs, 2, 2, harmonics, harmonics)
    matrices = matrices.transpose(0, 2, 3, 1, 4).reshape(pairs, 2, harmonics, width)
    group = (lax.axis_index("yl") * plane * groups + lax.axis_index(("yh", "core"))).reshape(1)
    coefs_shape = shape((atoms // 2 * rows, width), bf16)
    fields_shape = shape((rows, waves), f32)
    phase_shape = shape((atoms, waves), f32)
    wave_scratch = pltpu.VMEM((2, CHUNK * rows, waves), bf16)

    other_miller = flip(miller, "yl")
    other_fields = flip(fields, "yl")
    other_template = flip(template, "yl")
    own_cos, own_sin, select, table = pl.pallas_call(
        functools.partial(prepare_kernel, groups, slot_dev),
        in_specs=smem(1) + vmem(4),
        out_specs=tuple(vmem(4)),
        out_shape=(
            phase_shape, phase_shape, shape((atoms // 2, 128), f32), shape((atoms, 16), f32)
        ),
        name="prepare",
    )(
        group.astype(jnp.int32), miller, positions, species.reshape(1, -1),
        atom_order.reshape(1, -1),
    )
    coefs, other_cos, other_sin = pl.pallas_call(
        first_kernel,
        in_specs=vmem(9),
        out_specs=tuple(vmem(3)),
        out_shape=(coefs_shape, phase_shape, phase_shape),
        scratch_shapes=[wave_scratch],
        name="first",
    )(
        table, other_miller, fields, other_fields, template, other_template, own_cos, own_sin,
        select,
    )
    fixed = (template, other_template, own_cos, own_sin, other_cos, other_sin, select)

    def return_fields(coefs):
        parts = lax.all_to_all(coefs.reshape(plane, message, width), "zx", 0, 0, tiled=True)
        applied = pl.pallas_call(
            potential_kernel,
            in_specs=vmem(2),
            out_specs=vmem(1)[0],
            out_shape=shape((plane, message, width), bf16),
            name="potential",
        )(parts, matrices)
        applied = lax.all_to_all(applied, "zx", 0, 0, tiled=True)
        own = pl.pallas_call(
            return_kernel,
            in_specs=vmem(8),
            out_specs=vmem(1)[0],
            out_shape=shape((2, rows, waves), f32),
            scratch_shapes=[pltpu.VMEM((CHUNK * rows, 2 * width), bf16)],
            name="back",
        )(applied.reshape(atoms // 2 * rows, width), *fixed)
        return own + flip(own, "core")

    mine = return_fields(coefs)
    once, coefs = pl.pallas_call(
        next_kernel,
        in_specs=smem(1) + vmem(15),
        out_specs=tuple(vmem(2)),
        out_shape=(fields_shape, coefs_shape),
        scratch_shapes=[wave_scratch],
        name="next",
    )(
        reciprocal, miller, other_miller, fields, other_fields, mine, flip(mine, "yl"),
        flip(mine, "yh"), flip(mine, "yl", "yh"), *fixed,
    )
    mine = return_fields(coefs)
    twice = pl.pallas_call(
        last_kernel,
        in_specs=smem(1) + vmem(6),
        out_specs=vmem(1)[0],
        out_shape=fields_shape,
        name="last",
    )(
        reciprocal, miller, once, mine, flip(mine[1], "yl"), flip(mine[0], "yh"),
        flip(mine[1], "yl", "yh"),
    )
    return once.reshape(bands_in.shape), twice.reshape(bands_in.shape)


def solution(mesh):
    pw, groups = mesh.devices.shape
    fine = Mesh(mesh.devices.reshape(2, pw // 2, 2, groups // 2), ("yl", "zx", "yh", "core"))
    waves, slots = ("yl", "zx"), ("yl", "zx", "yh", "core")
    in_specs = (
        P(None, None, waves),
        P(None, None, waves),
        P(slots, None),
        P(None, waves),
        P(),
        P(),
        P(),
        P(),
    )
    out_specs = (P(None, None, waves), P(None, None, waves))
    return jax.shard_map(
        per_device, mesh=fine, in_specs=in_specs, out_specs=out_specs, check_vma=False
    )
```

time: 153 us -> 131 us (0.86)
  blocking collectives: 66.3 us -> 45.7 us
  Pallas kernels: 33.4 us -> 28.8 us
  starting transfers between devices: 26.2 us -> 30.3 us
  waiting for transfers between devices: 21.7 us -> 17.7 us
  other arithmetic: 0 us -> 1.7 us
    all_to_all x3, blocking collectives: 66.3 us -> 45.7 us  [the longest x2 30.6 us: return_fields(): applied = lax.all_to_all(applied, 'zx', 0, 0, tiled=True)]
    ppermute x6 -> x11, starting transfers between devices: 12.6 us -> 19.1 us  [flip(): return lax.ppermute(array, axes, pairs)]
    all_to_all x1, waiting for transfers between devices: 15.1 us -> 9.34 us  [return_fields(): lax.all_to_all(coefs.reshape(plane, message, width), 'zx', 0, 0, tiled=True)]
    pallas_call x4 -> x5, Pallas kernels: 27.7 us -> 23.6 us  [the longest x2 9.15 us: return_fields(): pl.pallas_call(return_kernel, in_specs=vmem(8), out_specs=vmem(1)[0], out...]
    all_to_all x1, starting transfers between devices: 13.6 us -> 11.2 us  [return_fields(): lax.all_to_all(coefs.reshape(plane, message, width), 'zx', 0, 0, tiled=True)]
    ppermute x6 -> x11, waiting for transfers between devices: 6.62 us -> 8.36 us  [flip(): return lax.ppermute(array, axes, pairs)]
    add x0 -> x2, other arithmetic: none -> 1.7 us  [return_fields(): return own + flip(own, 'core')]
    unnamed x16 -> x26, local copies, waits for them, and re-layouts: 2.64 us -> 3.77 us
  transfers between devices with their start and end apart: 7 -> 12, of which waited for: 4 -> 7; matrix products, arithmetic and copies ran while one was open for 1% -> 1% of each run, Pallas kernels for 0% -> 3%
where the time goes in v2:
time: 131 us; the launch traced here: 130 us
  blocking collectives  45.7 us (35%)
  starting transfers between devices  30.3 us (23%)
  Pallas kernels  28.8 us (22%)
  waiting for transfers between devices  17.7 us (14%)
  local copies, waits for them, and re-layouts  4.82 us (4%)
  other arithmetic  1.7 us (1%)
    all_to_all x2, blocking collectives, return_fields(): applied = lax.all_to_all(applied, 'zx', 0, 0, tiled=True)  30.6 us
    ppermute x11, starting transfers between devices, flip(): return lax.ppermute(array, axes, pairs)  19.1 us
    all_to_all x1, blocking collectives, return_fields(): lax.all_to_all(coefs.reshape(plane, message, width), 'zx', 0, 0, tiled=True)  15.1 us
    all_to_all x1, starting transfers between devices, return_fields(): lax.all_to_all(coefs.reshape(plane, message, width), 'zx', 0, 0, tiled=True)  11.2 us
    all_to_all x1, waiting for transfers between devices, return_fields(): lax.all_to_all(coefs.reshape(plane, message, width), 'zx', 0, 0, tiled=True)  9.34 us
    pallas_call x2, Pallas kernels, return_fields(): pl.pallas_call(return_kernel, in_specs=vmem(8), out_specs=vmem(1)[0], out...  9.15 us
    ppermute x11, waiting for transfers between devices, flip(): return lax.ppermute(array, axes, pairs)  8.36 us
    pallas_call x1, Pallas kernels, per_device(): pl.pallas_call(first_kernel, in_specs=vmem(9), out_specs=tuple(vmem(3)),...  5.7 us
  transfers between devices with their start and end apart: 12, of which 7 were waited for; matrix products, arithmetic and copies ran while one was open for 1% of the time, Pallas kernels for 3%

profile of v2, /device:TPU:1, one launch (start us, length us, event | category | flops | bytes accessed | tf_op | source)
XLA Modules:
  0.0 129.8 jit_solution(17898586137064512896)
XLA Ops:
  0.6 2.2 %collective-permute-start.2 = (bf16[128,512]{1,0:T(8,128)(2,1)}, bf16[128,512]{1,0:T(8,128)(2,1)S(1)}, u32[]{:S(2)}, u32[]{:S(2)}) collective-permute-start(bf16[128,512]{1,0:T(8,128)(2,1)} %bitcast.18), channel_id=1, source_target_pairs={{0,128},{128,0},{1,129},{129,1},{2,130},{130,2},{3,131},{131,3},{4... | collective-permute-start | bytes 393224 | tf_op jit(solution)/shard_map/ppermute | solution.py:303
  2.9 1.4 %collective-permute-start = (s32[3,512]{1,0:T(4,128)}, s32[3,512]{1,0:T(4,128)S(1)}, u32[]{:S(2)}, u32[]{:S(2)}) collective-permute-start(s32[3,512]{1,0:T(4,128)} %miller_ref.3), channel_id=1, source_target_pairs={{0,128},{128,0},{1,129},{129,1},{2,130},{130,2},{3,131},{131,3},{4... | collective-permute-start | bytes 18440 | tf_op jit(solution)/shard_map/ppermute | solution.py:303
  4.3 3.7 %prepare.1 = (f32[128,512]{1,0:T(8,128)}, f32[128,512]{1,0:T(8,128)}, f32[64,128]{1,0:T(8,128)}, f32[128,16]{1,0:T(8,128)}) custom-call(s32[1]{0:T(128)} %bitcast.1.group_ref, s32[3,512]{1,0:T(4,128)} %miller_ref.3, f32[3,1024]{1,0:T(4,128)} %positions_ref.1, s32[1,1024]{1,0:T(1,128)} %bitcast.33, s32[1,1024]{1,0:T(1,128)} %bitcast.34), custom_call_target="tpu_custom_call" | custom-call | tf_op jit(solution)/shard_map/prepare/pallas_call | solution.py:329
  8.7 5.7 %first.1 = (bf16[1024,128]{1,0:T(8,128)(2,1)}, f32[128,512]{1,0:T(8,128)}, f32[128,512]{1,0:T(8,128)}) custom-call(f32[128,16]{1,0:T(8,128)} %get-tuple-element.11.table_ref, s32[3,512]{1,0:T(4,128)} %copy-done.9, f32[16,512]{1,0:T(8,128)} %bitcast.29, f32[16,512]{1,0:T(8,128)} %copy-done.4, bf16[128,512]{1,0:T(8,128)(2,1)} %bitcast.19, ...), custom_call_target="tpu_custom_call" | custom-call | tf_op jit(solution)/shard_map/first/pallas_call | solution.py:341
  14.4 11.2 %all-to-all-start = ((bf16[32,32,128]{2,1,0:T(8,128)(2,1)}), bf16[32,32,128]{2,1,0:T(8,128)(2,1)S(1)}, u32[]{:S(2)}, u32[]{:S(2)}) async-start(bf16[32,32,128]{2,1,0:T(8,128)(2,1)} %bitcast.26), calls=%async_computation | async-start | bytes 524288 | tf_op jit(solution)/shard_map/all_to_all | solution.py:355
  25.9 0.7 reshape.50.potential_ref
  26.6 9.3 %all-to-all-done.parts_ref = bf16[32,32,128]{2,1,0:T(8,128)(2,1)S(1)} async-done(((bf16[32,32,128]{2,1,0:T(8,128)(2,1)}), bf16[32,32,128]{2,1,0:T(8,128)(2,1)S(1)}, u32[]{:S(2)}, u32[]{:S(2)}) %all-to-all-start) | async-done | bytes 262176 | tf_op jit(solution)/shard_map/all_to_all | solution.py:355
  35.9 0.7 copy-done.1
  36.6 1.9 %potential.2 = bf16[32,32,128]{2,1,0:T(8,128)(2,1)} custom-call(bf16[32,32,128]{2,1,0:T(8,128)(2,1)} %copy-done.1, bf16[2,2,64,128]{3,2,1,0:T(8,128)(2,1)} %reshape.50.potential_ref), custom_call_target="tpu_custom_call" | custom-call | tf_op jit(solution)/shard_map/potential/pallas_call | solution.py:356
  38.5 15.4 %all_to_all.20 = bf16[32,32,128]{2,1,0:T(8,128)(2,1)} all-to-all(bf16[32,32,128]{2,1,0:T(8,128)(2,1)} %potential.2), channel_id=1, replica_groups=mesh['yl'=2,'zx'=32,'yh'=2,'core'=2] {'zx'}, dimensions={0} | all-to-all | bytes 524288 | tf_op jit(solution)/shard_map/all_to_all | solution.py:363
  53.9 4.6 %back.2 = f32[2,16,512]{2,1,0:T(8,128)} custom-call(bf16[1024,128]{1,0:T(8,128)(2,1)} %bitcast.24, bf16[128,512]{1,0:T(8,128)(2,1)} %bitcast.20, bf16[128,512]{1,0:T(8,128)(2,1)} %copy-done, f32[128,512]{1,0:T(8,128)} %get-tuple-element.12.own_cos_ref, f32[128,512]{1,0:T(8,128)} %get-tuple-element.13.own_sin_ref, f32[128,512]{1,0:T(8,128)} %get-tuple-element.16.cos_ref, ...), custom_call_target="tpu_custom_call" | custom-call | tf_op jit(solution)/shard_map/back/pallas_call | solution.py:364
  58.5 4.6 %collective-permute-start.3 = (f32[2,16,512]{2,1,0:T(8,128)}, f32[2,16,512]{2,1,0:T(8,128)S(1)}, u32[]{:S(2)}, u32[]{:S(2)}) collective-permute-start(f32[2,16,512]{2,1,0:T(8,128)} %back.2), channel_id=1, source_target_pairs={{0,1},{1,0},{2,3},{3,2},{4,5},{5,4},{6,7},{7,6},{8,9},{9,8},{10,11... | collective-permute-start | bytes 196616 | tf_op jit(solution)/shard_map/ppermute | solution.py:303
  63.1 1.1 collective-permute-done.3
  64.2 0.9 add.14.mine_ref
  65.1 2.0 %collective-permute-start.6 = (f32[2,16,512]{2,1,0:T(8,128)S(1)}, f32[2,16,512]{2,1,0:T(8,128)S(1)}, u32[]{:S(2)}, u32[]{:S(2)}) collective-permute-start(f32[2,16,512]{2,1,0:T(8,128)S(1)} %add.14.mine_ref), channel_id=1, source_target_pairs={{0,130},{2,128},{128,2},{130,0},{1,131},{3,129},{129,3},{131,1},{4... | collective-permute-start | bytes 196616 | tf_op jit(solution)/shard_map/ppermute | solution.py:303
  67.1 0.8 collective-permute-start.5
  68.4 1.1 collective-permute-done.6.both_ref
  69.5 2.2 %collective-permute-done.5.high_ref = f32[2,16,512]{2,1,0:T(8,128)S(1)} collective-permute-done((f32[2,16,512]{2,1,0:T(8,128)S(1)}, f32[2,16,512]{2,1,0:T(8,128)S(1)}, u32[]{:S(2)}, u32[]{:S(2)}) %collective-permute-start.5) | collective-permute-done | bytes 65568 | tf_op jit(solution)/shard_map/ppermute | solution.py:303
  72.3 0.6 copy-done.8
  72.9 5.0 %next.1 = (f32[16,512]{1,0:T(8,128)}, bf16[1024,128]{1,0:T(8,128)(2,1)}) custom-call(f32[3]{0:T(128)} %lengths_ref.3, s32[3,512]{1,0:T(4,128)} %miller_ref.3, s32[3,512]{1,0:T(4,128)} %copy-done.9, f32[16,512]{1,0:T(8,128)} %bitcast.30, f32[16,512]{1,0:T(8,128)} %copy-done.4, f32[2,16,512]{2,1,0:T(8,128)} %copy-done.3, f32[2,16,512]{2,1,0:T(8,128)} %copy-done.8, ...), custom_call_target="tpu_custom_call" | custom-call | tf_op jit(solution)/shard_map/next/pallas_call | solution.py:375
  78.0 15.1 %all_to_all.21.parts_ref = bf16[32,32,128]{2,1,0:T(8,128)(2,1)} all-to-all(bf16[32,32,128]{2,1,0:T(8,128)(2,1)} %bitcast.27), channel_id=1, replica_groups=mesh['yl'=2,'zx'=32,'yh'=2,'core'=2] {'zx'}, dimensions={0} | all-to-all | bytes 524288 | tf_op jit(solution)/shard_map/all_to_all | solution.py:355
  93.1 1.9 %potential.3 = bf16[32,32,128]{2,1,0:T(8,128)(2,1)} custom-call(bf16[32,32,128]{2,1,0:T(8,128)(2,1)} %all_to_all.21.parts_ref, bf16[2,2,64,128]{3,2,1,0:T(8,128)(2,1)} %reshape.50.potential_ref), custom_call_target="tpu_custom_call" | custom-call | tf_op jit(solution)/shard_map/potential/pallas_call | solution.py:356
  95.0 15.1 %all_to_all.22 = bf16[32,32,128]{2,1,0:T(8,128)(2,1)} all-to-all(bf16[32,32,128]{2,1,0:T(8,128)(2,1)} %potential.3), channel_id=1, replica_groups=mesh['yl'=2,'zx'=32,'yh'=2,'core'=2] {'zx'}, dimensions={0} | all-to-all | bytes 524288 | tf_op jit(solution)/shard_map/all_to_all | solution.py:363
  110.1 4.6 %back.3 = f32[2,16,512]{2,1,0:T(8,128)} custom-call(bf16[1024,128]{1,0:T(8,128)(2,1)} %bitcast.23, bf16[128,512]{1,0:T(8,128)(2,1)} %bitcast.22, bf16[128,512]{1,0:T(8,128)(2,1)} %copy-done, f32[128,512]{1,0:T(8,128)} %get-tuple-element.12.own_cos_ref, f32[128,512]{1,0:T(8,128)} %get-tuple-element.13.own_sin_ref, f32[128,512]{1,0:T(8,128)} %get-tuple-element.16.cos_ref, ...), custom_call_target="tpu_custom_call" | custom-call | tf_op jit(solution)/shard_map/back/pallas_call | solution.py:364
  114.7 4.9 %collective-permute-start.7 = (f32[2,16,512]{2,1,0:T(8,128)}, f32[2,16,512]{2,1,0:T(8,128)S(1)}, u32[]{:S(2)}, u32[]{:S(2)}) collective-permute-start(f32[2,16,512]{2,1,0:T(8,128)} %back.3), channel_id=1, source_target_pairs={{0,1},{1,0},{2,3},{3,2},{4,5},{5,4},{6,7},{7,6},{8,9},{9,8},{10,11... | collective-permute-start | bytes 196616 | tf_op jit(solution)/shard_map/ppermute | solution.py:303
  119.5 1.1 collective-permute-done.7
  120.7 0.9 add.15.mine_ref
  122.1 1.5 %collective-permute-start.9 = (f32[16,512]{1,0:T(8,128)S(1)}, f32[16,512]{1,0:T(8,128)S(1)}, u32[]{:S(2)}, u32[]{:S(2)}) collective-permute-start(f32[16,512]{1,0:T(8,128)S(1)} %get-tuple-element.20), channel_id=1, source_target_pairs={{0,2},{2,0},{1,3},{3,1},{4,6},{6,4},{5,7},{7,5},{8,10},{10,8},{9,1... | collective-permute-start | bytes 98312 | tf_op jit(solution)/shard_map/ppermute | solution.py:303
  123.7 1.1 collective-permute-start.10
  124.8 1.6 %collective-permute-done.9.high_ref = f32[16,512]{1,0:T(8,128)S(1)} collective-permute-done((f32[16,512]{1,0:T(8,128)S(1)}, f32[16,512]{1,0:T(8,128)S(1)}, u32[]{:S(2)}, u32[]{:S(2)}) %collective-permute-start.9) | collective-permute-done | bytes 32800 | tf_op jit(solution)/shard_map/ppermute | solution.py:303
  126.4 1.2 collective-permute-done.10.both_ref
  128.3 1.5 %last.1 = f32[16,512]{1,0:T(8,128)} custom-call(f32[3]{0:T(128)} %lengths_ref.3, s32[3,512]{1,0:T(4,128)} %miller_ref.3, f32[16,512]{1,0:T(8,128)} %get-tuple-element.18.fields_ref, f32[2,16,512]{2,1,0:T(8,128)} %copy-done.2, f32[16,512]{1,0:T(8,128)} %copy-done.12, f32[16,512]{1,0:T(8,128)} %copy-done.10, f32[16,512]{1,0:T(8,128)} %copy-done.11), custom_call_target="tpu_custom_call" | custom-call | tf_op jit(solution)/shard_map/last/pallas_call | solution.py:387
  (35 shorter events, 3.4 us)
Async XLA Ops:
  0.6 7.4 %collective-permute-start.2 = (bf16[128,512]{1,0:T(8,128)(2,1)}, bf16[128,512]{1,0:T(8,128)(2,1)S(1)}, u32[]{:S(2)}, u32[]{:S(2)}) collective-permute-start(bf16[128,512]{1,0:T(8,128)(2,1)} %bitcast.18), channel_id=1, source_target_pairs={{0,128},{128,0},{1,129},{129,1},{2,130},{130,2},{3,131},{131,3},{4... | collective-permute-start | bytes 393224 | tf_op jit(solution)/shard_map/ppermute | solution.py:303
  2.8 5.1 %collective-permute-start.1 = (f32[16,512]{1,0:T(8,128)}, f32[16,512]{1,0:T(8,128)S(1)}, u32[]{:S(2)}, u32[]{:S(2)}) collective-permute-start(f32[16,512]{1,0:T(8,128)} %bitcast.28), channel_id=1, source_target_pairs={{0,128},{128,0},{1,129},{129,1},{2,130},{130,2},{3,131},{131,3},{4... | collective-permute-start | bytes 98312 | tf_op jit(solution)/shard_map/ppermute | solution.py:303
  2.9 5.0 %collective-permute-start = (s32[3,512]{1,0:T(4,128)}, s32[3,512]{1,0:T(4,128)S(1)}, u32[]{:S(2)}, u32[]{:S(2)}) collective-permute-start(s32[3,512]{1,0:T(4,128)} %miller_ref.3), channel_id=1, source_target_pairs={{0,128},{128,0},{1,129},{129,1},{2,130},{130,2},{3,131},{131,3},{4... | collective-permute-start | bytes 18440 | tf_op jit(solution)/shard_map/ppermute | solution.py:303
  8.0 0.6 copy-start.9
  8.0 0.6 copy-start.4
  8.0 0.6 copy-start
  14.4 11.2 %copy-start.5 = (bf16[4,8192]{1,0:T(4,128)(2,1)S(1)}, bf16[4,8192]{1,0:T(4,128)(2,1)}, u32[]{:S(2)}) copy-start(bf16[4,8192]{1,0:T(4,128)(2,1)} %param.10) | copy-start | bytes 196612
  14.4 21.6 %all-to-all-start = ((bf16[32,32,128]{2,1,0:T(8,128)(2,1)}), bf16[32,32,128]{2,1,0:T(8,128)(2,1)S(1)}, u32[]{:S(2)}, u32[]{:S(2)}) async-start(bf16[32,32,128]{2,1,0:T(8,128)(2,1)} %bitcast.26), calls=%async_computation | async-start | bytes 524288 | tf_op jit(solution)/shard_map/all_to_all | solution.py:355
  35.9 0.7 copy-start.1
  58.5 5.7 %collective-permute-start.3 = (f32[2,16,512]{2,1,0:T(8,128)}, f32[2,16,512]{2,1,0:T(8,128)S(1)}, u32[]{:S(2)}, u32[]{:S(2)}) collective-permute-start(f32[2,16,512]{2,1,0:T(8,128)} %back.2), channel_id=1, source_target_pairs={{0,1},{1,0},{2,3},{3,2},{4,5},{5,4},{6,7},{7,6},{8,9},{9,8},{10,11... | collective-permute-start | bytes 196616 | tf_op jit(solution)/shard_map/ppermute | solution.py:303
  65.1 6.6 %copy-start.3 = (f32[2,16,512]{2,1,0:T(8,128)}, f32[2,16,512]{2,1,0:T(8,128)S(1)}, u32[]{:S(2)}) copy-start(f32[2,16,512]{2,1,0:T(8,128)S(1)} %add.14.mine_ref) | copy-start | bytes 196612
  65.1 4.4 %collective-permute-start.6 = (f32[2,16,512]{2,1,0:T(8,128)S(1)}, f32[2,16,512]{2,1,0:T(8,128)S(1)}, u32[]{:S(2)}, u32[]{:S(2)}) collective-permute-start(f32[2,16,512]{2,1,0:T(8,128)S(1)} %add.14.mine_ref), channel_id=1, source_target_pairs={{0,130},{2,128},{128,2},{130,0},{1,131},{3,129},{129,3},{131,1},{4... | collective-permute-start | bytes 196616 | tf_op jit(solution)/shard_map/ppermute | solution.py:303
  67.1 4.6 %collective-permute-start.5 = (f32[2,16,512]{2,1,0:T(8,128)S(1)}, f32[2,16,512]{2,1,0:T(8,128)S(1)}, u32[]{:S(2)}, u32[]{:S(2)}) collective-permute-start(f32[2,16,512]{2,1,0:T(8,128)S(1)} %add.14.mine_ref), channel_id=1, source_target_pairs={{0,2},{2,0},{1,3},{3,1},{4,6},{6,4},{5,7},{7,5},{8,10},{10,8},{9,1... | collective-permute-start | bytes 196616 | tf_op jit(solution)/shard_map/ppermute | solution.py:303
  67.9 3.8 %collective-permute-start.4 = (f32[2,16,512]{2,1,0:T(8,128)S(1)}, f32[2,16,512]{2,1,0:T(8,128)S(1)}, u32[]{:S(2)}, u32[]{:S(2)}) collective-permute-start(f32[2,16,512]{2,1,0:T(8,128)S(1)} %add.14.mine_ref), channel_id=1, source_target_pairs={{0,128},{128,0},{1,129},{129,1},{2,130},{130,2},{3,131},{131,3},{4... | collective-permute-start | bytes 196616 | tf_op jit(solution)/shard_map/ppermute | solution.py:303
  69.5 2.2 %copy-start.6 = (f32[2,16,512]{2,1,0:T(8,128)}, f32[2,16,512]{2,1,0:T(8,128)S(1)}, u32[]{:S(2)}) copy-start(f32[2,16,512]{2,1,0:T(8,128)S(1)} %collective-permute-done.6.both_ref) | copy-start | bytes 196612
  71.7 0.6 copy-start.7
  72.3 0.6 copy-start.8
  114.7 6.0 %collective-permute-start.7 = (f32[2,16,512]{2,1,0:T(8,128)}, f32[2,16,512]{2,1,0:T(8,128)S(1)}, u32[]{:S(2)}, u32[]{:S(2)}) collective-permute-start(f32[2,16,512]{2,1,0:T(8,128)} %back.3), channel_id=1, source_target_pairs={{0,1},{1,0},{2,3},{3,2},{4,5},{5,4},{6,7},{7,6},{8,9},{9,8},{10,11... | collective-permute-start | bytes 196616 | tf_op jit(solution)/shard_map/ppermute | solution.py:303
  121.5 0.6 copy-start.2
  122.1 4.3 %collective-permute-start.9 = (f32[16,512]{1,0:T(8,128)S(1)}, f32[16,512]{1,0:T(8,128)S(1)}, u32[]{:S(2)}, u32[]{:S(2)}) collective-permute-start(f32[16,512]{1,0:T(8,128)S(1)} %get-tuple-element.20), channel_id=1, source_target_pairs={{0,2},{2,0},{1,3},{3,1},{4,6},{6,4},{5,7},{7,5},{8,10},{10,8},{9,1... | collective-permute-start | bytes 98312 | tf_op jit(solution)/shard_map/ppermute | solution.py:303
  123.7 4.0 %collective-permute-start.10 = (f32[16,512]{1,0:T(8,128)S(1)}, f32[16,512]{1,0:T(8,128)S(1)}, u32[]{:S(2)}, u32[]{:S(2)}) collective-permute-start(f32[16,512]{1,0:T(8,128)S(1)} %get-tuple-element.21), channel_id=1, source_target_pairs={{0,130},{2,128},{128,2},{130,0},{1,131},{3,129},{129,3},{131,1},{4... | collective-permute-start | bytes 98312 | tf_op jit(solution)/shard_map/ppermute | solution.py:303
  124.8 2.9 %collective-permute-start.8 = (f32[16,512]{1,0:T(8,128)S(1)}, f32[16,512]{1,0:T(8,128)S(1)}, u32[]{:S(2)}, u32[]{:S(2)}) collective-permute-start(f32[16,512]{1,0:T(8,128)S(1)} %get-tuple-element.21), channel_id=1, source_target_pairs={{0,128},{128,0},{1,129},{129,1},{2,130},{130,2},{3,131},{131,3},{4... | collective-permute-start | bytes 98312 | tf_op jit(solution)/shard_map/ppermute | solution.py:303
  126.4 1.2 copy-start.10
  127.6 0.6 copy-start.11
  127.6 0.6 copy-start.12

commit v3 on v2

--- a/solution.py
+++ b/solution.py
@@ -32,6 +32,7 @@
 NT = (((1,), (1,)), ((), ()))
 NN = (((1,), (0,)), ((), ()))
 CHUNK = 16
+LIMIT = pltpu.CompilerParams(vmem_limit_bytes=12 * 2**20)
 
 
 def dot(left, right, dims):
@@ -333,6 +334,7 @@
         out_shape=(
             phase_shape, phase_shape, shape((atoms // 2, 128), f32), shape((atoms, 16), f32)
         ),
+        compiler_params=LIMIT,
         name="prepare",
     )(
         group.astype(jnp.int32), miller, positions, species.reshape(1, -1),
@@ -344,6 +346,7 @@
         out_specs=tuple(vmem(3)),
         out_shape=(coefs_shape, phase_shape, phase_shape),
         scratch_shapes=[wave_scratch],
+        compiler_params=LIMIT,
         name="first",
     )(
         table, other_miller, fields, other_fields, template, other_template, own_cos, own_sin,
@@ -358,7 +361,8 @@
             in_specs=vmem(2),
             out_specs=vmem(1)[0],
             out_shape=shape((plane, message, width), bf16),
-            name="potential",
+            compiler_params=LIMIT,
+        name="potential",
         )(parts, matrices)
         applied = lax.all_to_all(applied, "zx", 0, 0, tiled=True)
         own = pl.pallas_call(
@@ -367,7 +371,8 @@
             out_specs=vmem(1)[0],
             out_shape=shape((2, rows, waves), f32),
             scratch_shapes=[pltpu.VMEM((CHUNK * rows, 2 * width), bf16)],
-            name="back",
+            compiler_params=LIMIT,
+        name="back",
         )(applied.reshape(atoms // 2 * rows, width), *fixed)
         return own + flip(own, "core")
 
@@ -378,6 +383,7 @@
         out_specs=tuple(vmem(2)),
         out_shape=(fields_shape, coefs_shape),
         scratch_shapes=[wave_scratch],
+        compiler_params=LIMIT,
         name="next",
     )(
         reciprocal, miller, other_miller, fields, other_fields, mine, flip(mine, "yl"),
@@ -389,6 +395,7 @@
         in_specs=smem(1) + vmem(6),
         out_specs=vmem(1)[0],
         out_shape=fields_shape,
+        compiler_params=LIMIT,
         name="last",
     )(
         reciprocal, miller, once, mine, flip(mine[1], "yl"), flip(mine[0], "yh"),

time: 131 us -> 112 us (0.85)
  Pallas kernels: 28.8 us -> 17.1 us
  blocking collectives: 45.7 us -> 42.8 us
  local copies, waits for them, and re-layouts: 4.82 us -> 2.07 us
  other arithmetic: 1.7 us -> 0.02 us
    pallas_call x2, Pallas kernels: 9.15 us -> 5.11 us  [return_fields(): pl.pallas_call(return_kernel, in_specs=vmem(8), out_specs=vmem(1)[0], out...]
    pallas_call x2, Pallas kernels: 3.73 us -> 0.4 us  [return_fields(): pl.pallas_call(potential_kernel, in_specs=vmem(2), out_specs=vmem(1)[0],...]
    unnamed x26 -> x20, local copies, waits for them, and re-layouts: 3.77 us -> 1.65 us
    add x2, other arithmetic: 1.7 us -> 0.02 us  [return_fields(): return own + flip(own, 'core')]
    all_to_all x1, blocking collectives: 15.1 us -> 13.6 us  [return_fields(): lax.all_to_all(coefs.reshape(plane, message, width), 'zx', 0, 0, tiled=True)]
    pallas_call x1, Pallas kernels: 3.67 us -> 2.12 us  [per_device(): pl.pallas_call(functools.partial(prepare_kernel, groups, slot_dev), in_sp...]
    pallas_call x1, Pallas kernels: 5.7 us -> 4.3 us  [per_device(): pl.pallas_call(first_kernel, in_specs=vmem(9), out_specs=tuple(vmem(3)),...]
  transfers between devices with their start and end apart: 12 -> 12, of which waited for: 7 -> 7; matrix products, arithmetic and copies ran while one was open for 1% -> 0% of each run, Pallas kernels for 3% -> 2%
where the time goes in v3:
time: 112 us; the launch traced here: 111 us
  blocking collectives  42.8 us (38%)
  starting transfers between devices  29.8 us (27%)
  waiting for transfers between devices  18.9 us (17%)
  Pallas kernels  17.1 us (15%)
  local copies, waits for them, and re-layouts  2.07 us (2%)
    all_to_all x2, blocking collectives, return_fields(): applied = lax.all_to_all(applied, 'zx', 0, 0, tiled=True)  29.3 us
    ppermute x11, starting transfers between devices, flip(): return lax.ppermute(array, axes, pairs)  18.6 us
    all_to_all x1, blocking collectives, return_fields(): lax.all_to_all(coefs.reshape(plane, message, width), 'zx', 0, 0, tiled=True)  13.6 us
    all_to_all x1, starting transfers between devices, return_fields(): lax.all_to_all(coefs.reshape(plane, message, width), 'zx', 0, 0, tiled=True)  11.2 us
    all_to_all x1, waiting for transfers between devices, return_fields(): lax.all_to_all(coefs.reshape(plane, message, width), 'zx', 0, 0, tiled=True)  9.96 us
    ppermute x11, waiting for transfers between devices, flip(): return lax.ppermute(array, axes, pairs)  8.94 us
    pallas_call x2, Pallas kernels, return_fields(): pl.pallas_call(return_kernel, in_specs=vmem(8), out_specs=vmem(1)[0], out...  5.11 us
    pallas_call x1, Pallas kernels, per_device(): pl.pallas_call(first_kernel, in_specs=vmem(9), out_specs=tuple(vmem(3)),...  4.3 us
  transfers between devices with their start and end apart: 12, of which 7 were waited for; matrix products, arithmetic and copies ran while one was open for 0% of the time, Pallas kernels for 2%

profile of v3, /device:TPU:1, one launch (start us, length us, event | category | flops | bytes accessed | tf_op | source)
XLA Modules:
  0.0 111.5 jit_solution(4168332010321696420)
XLA Ops:
  0.6 2.2 %collective-permute-start.2 = (bf16[128,512]{1,0:T(8,128)(2,1)}, bf16[128,512]{1,0:T(8,128)(2,1)S(1)}, u32[]{:S(2)}, u32[]{:S(2)}) collective-permute-start(bf16[128,512]{1,0:T(8,128)(2,1)} %bitcast.18), channel_id=1, source_target_pairs={{0,128},{128,0},{1,129},{129,1},{2,130},{130,2},{3,131},{131,3},{4... | collective-permute-start | bytes 393224 | tf_op jit(solution)/shard_map/ppermute | solution.py:304
  2.9 1.4 %collective-permute-start = (s32[3,512]{1,0:T(4,128)}, s32[3,512]{1,0:T(4,128)S(1)}, u32[]{:S(2)}, u32[]{:S(2)}) collective-permute-start(s32[3,512]{1,0:T(4,128)} %miller_ref.3), channel_id=1, source_target_pairs={{0,128},{128,0},{1,129},{129,1},{2,130},{130,2},{3,131},{131,3},{4... | collective-permute-start | bytes 18440 | tf_op jit(solution)/shard_map/ppermute | solution.py:304
  4.3 0.7 copy-done.3
  5.0 2.1 %prepare.1 = (f32[128,512]{1,0:T(8,128)S(1)}, f32[128,512]{1,0:T(8,128)S(1)}, f32[64,128]{1,0:T(8,128)S(1)}, f32[128,16]{1,0:T(8,128)S(1)}) custom-call(s32[1]{0:T(128)} %bitcast.1.group_ref, s32[3,512]{1,0:T(4,128)S(1)} %copy-done.3, f32[3,1024]{1,0:T(4,128)S(1)} %copy-done.5, s32[1,1024]{1,0:T(1,128)S(1)} %bitcast.30, s32[1,1024]{1,0:T(1,128)S(1)} %bitcast.31), custom_call_target="tpu_custom_call" | custom-call | tf_op jit(solution)/shard_map/prepare/pallas_call | solution.py:330
  7.2 0.9 copy-done
  8.1 4.3 %first.1 = (bf16[1024,128]{1,0:T(8,128)(2,1)}, f32[128,512]{1,0:T(8,128)S(1)}, f32[128,512]{1,0:T(8,128)S(1)}) custom-call(f32[128,16]{1,0:T(8,128)S(1)} %get-tuple-element.11.table_ref, s32[3,512]{1,0:T(4,128)S(1)} %collective-permute-done.miller_ref, f32[16,512]{1,0:T(8,128)S(1)} %bitcast.27, f32[16,512]{1,0:T(8,128)S(1)} %collective-permute-done.1.fields_ref, ...), custom_call_target="tpu_custom_call" | custom-call | tf_op jit(solution)/shard_map/first/pallas_call | solution.py:343
  12.4 11.2 %all-to-all-start = ((bf16[32,32,128]{2,1,0:T(8,128)(2,1)}), bf16[32,32,128]{2,1,0:T(8,128)(2,1)S(1)}, u32[]{:S(2)}, u32[]{:S(2)}) async-start(bf16[32,32,128]{2,1,0:T(8,128)(2,1)} %bitcast.5), calls=%async_computation | async-start | bytes 524288 | tf_op jit(solution)/shard_map/all_to_all | solution.py:358
  23.6 0.2 reshape.49
  24.0 10.0 %all-to-all-done.parts_ref = bf16[32,32,128]{2,1,0:T(8,128)(2,1)S(1)} async-done(((bf16[32,32,128]{2,1,0:T(8,128)(2,1)}), bf16[32,32,128]{2,1,0:T(8,128)(2,1)S(1)}, u32[]{:S(2)}, u32[]{:S(2)}) %all-to-all-start) | async-done | bytes 262176 | tf_op jit(solution)/shard_map/all_to_all | solution.py:358
  34.0 0.2 potential.2
  34.2 15.2 %all_to_all.20 = bf16[32,32,128]{2,1,0:T(8,128)(2,1)S(1)} all-to-all(bf16[32,32,128]{2,1,0:T(8,128)(2,1)S(1)} %potential.2), channel_id=1, replica_groups=mesh['yl'=2,'zx'=32,'yh'=2,'core'=2] {'zx'}, dimensions={0} | all-to-all | bytes 524288 | tf_op jit(solution)/shard_map/all_to_all | solution.py:367
  49.5 2.6 %back.2 = f32[2,16,512]{2,1,0:T(8,128)S(1)} custom-call(bf16[1024,128]{1,0:T(8,128)(2,1)S(1)} %bitcast.24, bf16[128,512]{1,0:T(8,128)(2,1)S(1)} %bitcast.20, bf16[128,512]{1,0:T(8,128)(2,1)S(1)} %collective-permute-done.2.template_ref, f32[128,512]{1,0:T(8,128)S(1)} %get-tuple-element.12.own_cos_ref, f32[128,512]{1,0:T(8,128)S(1)} %get-tuple-element.13.own_sin_ref, ...), custom_call_target="tpu_custom_call" | custom-call | tf_op jit(solution)/shard_map/back/pallas_call | solution.py:368
  52.0 3.8 %collective-permute-start.3 = (f32[2,16,512]{2,1,0:T(8,128)S(1)}, f32[2,16,512]{2,1,0:T(8,128)S(1)}, u32[]{:S(2)}, u32[]{:S(2)}) collective-permute-start(f32[2,16,512]{2,1,0:T(8,128)S(1)} %back.2), channel_id=1, source_target_pairs={{0,1},{1,0},{2,3},{3,2},{4,5},{5,4},{6,7},{7,6},{8,9},{9,8},{10,11... | collective-permute-start | bytes 196616 | tf_op jit(solution)/shard_map/ppermute | solution.py:304
  55.9 0.9 collective-permute-done.3
  56.8 2.6 %collective-permute-start.6 = (f32[2,16,512]{2,1,0:T(8,128)S(1)}, f32[2,16,512]{2,1,0:T(8,128)S(1)}, u32[]{:S(2)}, u32[]{:S(2)}) collective-permute-start(f32[2,16,512]{2,1,0:T(8,128)S(1)} %add.14.mine_ref), channel_id=1, source_target_pairs={{0,130},{2,128},{128,2},{130,0},{1,131},{3,129},{129,3},{131,1},{4... | collective-permute-start | bytes 196616 | tf_op jit(solution)/shard_map/ppermute | solution.py:304
  59.4 0.3 collective-permute-start.5
  59.7 0.4 collective-permute-start.4
  60.1 1.1 collective-permute-done.6.both_ref
  61.2 2.8 %collective-permute-done.5.high_ref = f32[2,16,512]{2,1,0:T(8,128)S(1)} collective-permute-done((f32[2,16,512]{2,1,0:T(8,128)S(1)}, f32[2,16,512]{2,1,0:T(8,128)S(1)}, u32[]{:S(2)}, u32[]{:S(2)}) %collective-permute-start.5) | collective-permute-done | bytes 65568 | tf_op jit(solution)/shard_map/ppermute | solution.py:304
  64.0 4.0 %next.1 = (f32[16,512]{1,0:T(8,128)}, bf16[1024,128]{1,0:T(8,128)(2,1)S(1)}) custom-call(f32[3]{0:T(128)S(1)} %copy-done.8, s32[3,512]{1,0:T(4,128)S(1)} %copy-done.3, s32[3,512]{1,0:T(4,128)S(1)} %collective-permute-done.miller_ref, f32[16,512]{1,0:T(8,128)S(1)} %bitcast.28, f32[16,512]{1,0:T(8,128)S(1)} %collective-permute-done.1.fields_ref, ...), custom_call_target="tpu_custom_call" | custom-call | tf_op jit(solution)/shard_map/next/pallas_call | solution.py:380
  67.9 13.6 %all_to_all.21.parts_ref = bf16[32,32,128]{2,1,0:T(8,128)(2,1)S(1)} all-to-all(bf16[32,32,128]{2,1,0:T(8,128)(2,1)S(1)} %bitcast.25), channel_id=1, replica_groups=mesh['yl'=2,'zx'=32,'yh'=2,'core'=2] {'zx'}, dimensions={0} | all-to-all | bytes 524288 | tf_op jit(solution)/shard_map/all_to_all | solution.py:358
  81.5 0.2 potential.3
  81.7 14.0 %all_to_all.22 = bf16[32,32,128]{2,1,0:T(8,128)(2,1)S(1)} all-to-all(bf16[32,32,128]{2,1,0:T(8,128)(2,1)S(1)} %potential.3), channel_id=1, replica_groups=mesh['yl'=2,'zx'=32,'yh'=2,'core'=2] {'zx'}, dimensions={0} | all-to-all | bytes 524288 | tf_op jit(solution)/shard_map/all_to_all | solution.py:367
  95.7 2.6 %back.3 = f32[2,16,512]{2,1,0:T(8,128)S(1)} custom-call(bf16[1024,128]{1,0:T(8,128)(2,1)S(1)} %bitcast.23, bf16[128,512]{1,0:T(8,128)(2,1)S(1)} %bitcast.22, bf16[128,512]{1,0:T(8,128)(2,1)S(1)} %collective-permute-done.2.template_ref, f32[128,512]{1,0:T(8,128)S(1)} %get-tuple-element.12.own_cos_ref, f32[128,512]{1,0:T(8,128)S(1)} %get-tuple-element.13.own_sin_ref, ...), custom_call_target="tpu_custom_call" | custom-call | tf_op jit(solution)/shard_map/back/pallas_call | solution.py:368
  98.3 5.0 %collective-permute-start.7 = (f32[2,16,512]{2,1,0:T(8,128)S(1)}, f32[2,16,512]{2,1,0:T(8,128)S(1)}, u32[]{:S(2)}, u32[]{:S(2)}) collective-permute-start(f32[2,16,512]{2,1,0:T(8,128)S(1)} %back.3), channel_id=1, source_target_pairs={{0,1},{1,0},{2,3},{3,2},{4,5},{5,4},{6,7},{7,6},{8,9},{9,8},{10,11... | collective-permute-start | bytes 196616 | tf_op jit(solution)/shard_map/ppermute | solution.py:304
  103.3 0.9 collective-permute-done.7
  104.3 2.0 %collective-permute-start.9 = (f32[16,512]{1,0:T(8,128)S(1)}, f32[16,512]{1,0:T(8,128)S(1)}, u32[]{:S(2)}, u32[]{:S(2)}) collective-permute-start(f32[16,512]{1,0:T(8,128)S(1)} %get-tuple-element.20), channel_id=1, source_target_pairs={{0,2},{2,0},{1,3},{3,1},{4,6},{6,4},{5,7},{7,5},{8,10},{10,8},{9,1... | collective-permute-start | bytes 98312 | tf_op jit(solution)/shard_map/ppermute | solution.py:304
  106.3 0.2 collective-permute-start.10
  106.5 0.5 collective-permute-start.8
  107.0 1.6 %collective-permute-done.9.high_ref = f32[16,512]{1,0:T(8,128)S(1)} collective-permute-done((f32[16,512]{1,0:T(8,128)S(1)}, f32[16,512]{1,0:T(8,128)S(1)}, u32[]{:S(2)}, u32[]{:S(2)}) %collective-permute-start.9) | collective-permute-done | bytes 32800 | tf_op jit(solution)/shard_map/ppermute | solution.py:304
  108.6 1.7 %collective-permute-done.10.both_ref = f32[16,512]{1,0:T(8,128)S(1)} collective-permute-done((f32[16,512]{1,0:T(8,128)S(1)}, f32[16,512]{1,0:T(8,128)S(1)}, u32[]{:S(2)}, u32[]{:S(2)}) %collective-permute-start.10) | collective-permute-done | bytes 32800 | tf_op jit(solution)/shard_map/ppermute | solution.py:304
  110.3 1.2 %last.1 = f32[16,512]{1,0:T(8,128)} custom-call(f32[3]{0:T(128)S(1)} %copy-done.8, s32[3,512]{1,0:T(4,128)S(1)} %copy-done.3, f32[16,512]{1,0:T(8,128)S(1)} %copy-done.4, f32[2,16,512]{2,1,0:T(8,128)S(1)} %add.15.mine_ref, f32[16,512]{1,0:T(8,128)S(1)} %collective-permute-done.8.low_ref, f32[16,512]{1,0:T(8,128)S(1)} %collective-permute-done.9.high_ref, ...), custom_call_target="tpu_custom_call" | custom-call | tf_op jit(solution)/shard_map/last/pallas_call | solution.py:393
  (29 shorter events, 0.4 us)
Async XLA Ops:
  0.6 3.7 %copy-start.5 = (f32[3,1024]{1,0:T(4,128)S(1)}, f32[3,1024]{1,0:T(4,128)}, u32[]{:S(2)}) copy-start(f32[3,1024]{1,0:T(4,128)} %positions_ref.1) | copy-start | bytes 36868
  0.6 6.6 %collective-permute-start.2 = (bf16[128,512]{1,0:T(8,128)(2,1)}, bf16[128,512]{1,0:T(8,128)(2,1)S(1)}, u32[]{:S(2)}, u32[]{:S(2)}) collective-permute-start(bf16[128,512]{1,0:T(8,128)(2,1)} %bitcast.18), channel_id=1, source_target_pairs={{0,128},{128,0},{1,129},{129,1},{2,130},{130,2},{3,131},{131,3},{4... | collective-permute-start | bytes 393224 | tf_op jit(solution)/shard_map/ppermute | solution.py:304
  2.8 4.3 %collective-permute-start.1 = (f32[16,512]{1,0:T(8,128)}, f32[16,512]{1,0:T(8,128)S(1)}, u32[]{:S(2)}, u32[]{:S(2)}) collective-permute-start(f32[16,512]{1,0:T(8,128)} %bitcast.26), channel_id=1, source_target_pairs={{0,128},{128,0},{1,129},{129,1},{2,130},{130,2},{3,131},{131,3},{4... | collective-permute-start | bytes 98312 | tf_op jit(solution)/shard_map/ppermute | solution.py:304
  2.9 4.2 %collective-permute-start = (s32[3,512]{1,0:T(4,128)}, s32[3,512]{1,0:T(4,128)S(1)}, u32[]{:S(2)}, u32[]{:S(2)}) collective-permute-start(s32[3,512]{1,0:T(4,128)} %miller_ref.3), channel_id=1, source_target_pairs={{0,128},{128,0},{1,129},{129,1},{2,130},{130,2},{3,131},{131,3},{4... | collective-permute-start | bytes 18440 | tf_op jit(solution)/shard_map/ppermute | solution.py:304
  4.3 0.7 copy-start.3
  4.3 0.7 copy-start.6
  4.3 0.7 copy-start.7
  4.3 2.9 %copy-start.2 = (f32[2,8,512]{2,1,0:T(8,128)S(1)}, f32[2,8,512]{2,1,0:T(8,128)}, u32[]{:S(2)}) copy-start(f32[2,8,512]{2,1,0:T(8,128)} %param.8) | copy-start | bytes 98308
  7.2 0.9 copy-start
  12.4 11.2 %copy-start.9 = (bf16[4,8192]{1,0:T(4,128)(2,1)S(1)}, bf16[4,8192]{1,0:T(4,128)(2,1)}, u32[]{:S(2)}) copy-start(bf16[4,8192]{1,0:T(4,128)(2,1)} %param.10) | copy-start | bytes 196612
  12.4 21.6 %all-to-all-start = ((bf16[32,32,128]{2,1,0:T(8,128)(2,1)}), bf16[32,32,128]{2,1,0:T(8,128)(2,1)S(1)}, u32[]{:S(2)}, u32[]{:S(2)}) async-start(bf16[32,32,128]{2,1,0:T(8,128)(2,1)} %bitcast.5), calls=%async_computation | async-start | bytes 524288 | tf_op jit(solution)/shard_map/all_to_all | solution.py:358
  34.2 15.2 %copy-start.1 = (bf16[2,64,512]{2,1,0:T(8,128)(2,1)S(1)}, bf16[2,64,512]{2,1,0:T(8,128)(2,1)}, u32[]{:S(2)}) copy-start(bf16[2,64,512]{2,1,0:T(8,128)(2,1)} %param.9) | copy-start | bytes 393220
  52.0 12.0 %copy-start.8 = (f32[3]{0:T(128)S(1)}, f32[3]{0:T(128)}, u32[]{:S(2)}) copy-start(f32[3]{0:T(128)} %lengths_ref.3) | copy-start | bytes 40
  52.0 4.7 %collective-permute-start.3 = (f32[2,16,512]{2,1,0:T(8,128)S(1)}, f32[2,16,512]{2,1,0:T(8,128)S(1)}, u32[]{:S(2)}, u32[]{:S(2)}) collective-permute-start(f32[2,16,512]{2,1,0:T(8,128)S(1)} %back.2), channel_id=1, source_target_pairs={{0,1},{1,0},{2,3},{3,2},{4,5},{5,4},{6,7},{7,6},{8,9},{9,8},{10,11... | collective-permute-start | bytes 196616 | tf_op jit(solution)/shard_map/ppermute | solution.py:304
  56.8 4.4 %collective-permute-start.6 = (f32[2,16,512]{2,1,0:T(8,128)S(1)}, f32[2,16,512]{2,1,0:T(8,128)S(1)}, u32[]{:S(2)}, u32[]{:S(2)}) collective-permute-start(f32[2,16,512]{2,1,0:T(8,128)S(1)} %add.14.mine_ref), channel_id=1, source_target_pairs={{0,130},{2,128},{128,2},{130,0},{1,131},{3,129},{129,3},{131,1},{4... | collective-permute-start | bytes 196616 | tf_op jit(solution)/shard_map/ppermute | solution.py:304
  59.4 4.6 %collective-permute-start.5 = (f32[2,16,512]{2,1,0:T(8,128)S(1)}, f32[2,16,512]{2,1,0:T(8,128)S(1)}, u32[]{:S(2)}, u32[]{:S(2)}) collective-permute-start(f32[2,16,512]{2,1,0:T(8,128)S(1)} %add.14.mine_ref), channel_id=1, source_target_pairs={{0,2},{2,0},{1,3},{3,1},{4,6},{6,4},{5,7},{7,5},{8,10},{10,8},{9,1... | collective-permute-start | bytes 196616 | tf_op jit(solution)/shard_map/ppermute | solution.py:304
  59.7 4.3 %collective-permute-start.4 = (f32[2,16,512]{2,1,0:T(8,128)S(1)}, f32[2,16,512]{2,1,0:T(8,128)S(1)}, u32[]{:S(2)}, u32[]{:S(2)}) collective-permute-start(f32[2,16,512]{2,1,0:T(8,128)S(1)} %add.14.mine_ref), channel_id=1, source_target_pairs={{0,128},{128,0},{1,129},{129,1},{2,130},{130,2},{3,131},{131,3},{4... | collective-permute-start | bytes 196616 | tf_op jit(solution)/shard_map/ppermute | solution.py:304
  98.3 5.9 %collective-permute-start.7 = (f32[2,16,512]{2,1,0:T(8,128)S(1)}, f32[2,16,512]{2,1,0:T(8,128)S(1)}, u32[]{:S(2)}, u32[]{:S(2)}) collective-permute-start(f32[2,16,512]{2,1,0:T(8,128)S(1)} %back.3), channel_id=1, source_target_pairs={{0,1},{1,0},{2,3},{3,2},{4,5},{5,4},{6,7},{7,6},{8,9},{9,8},{10,11... | collective-permute-start | bytes 196616 | tf_op jit(solution)/shard_map/ppermute | solution.py:304
  104.2 6.0 %copy-start.4 = (f32[16,512]{1,0:T(8,128)S(1)}, f32[16,512]{1,0:T(8,128)}, u32[]{:S(2)}) copy-start(f32[16,512]{1,0:T(8,128)} %get-tuple-element.18.fields_ref) | copy-start | bytes 98308
  104.3 4.4 %collective-permute-start.9 = (f32[16,512]{1,0:T(8,128)S(1)}, f32[16,512]{1,0:T(8,128)S(1)}, u32[]{:S(2)}, u32[]{:S(2)}) collective-permute-start(f32[16,512]{1,0:T(8,128)S(1)} %get-tuple-element.20), channel_id=1, source_target_pairs={{0,2},{2,0},{1,3},{3,1},{4,6},{6,4},{5,7},{7,5},{8,10},{10,8},{9,1... | collective-permute-start | bytes 98312 | tf_op jit(solution)/shard_map/ppermute | solution.py:304
  106.3 4.0 %collective-permute-start.10 = (f32[16,512]{1,0:T(8,128)S(1)}, f32[16,512]{1,0:T(8,128)S(1)}, u32[]{:S(2)}, u32[]{:S(2)}) collective-permute-start(f32[16,512]{1,0:T(8,128)S(1)} %get-tuple-element.21), channel_id=1, source_target_pairs={{0,130},{2,128},{128,2},{130,0},{1,131},{3,129},{129,3},{131,1},{4... | collective-permute-start | bytes 98312 | tf_op jit(solution)/shard_map/ppermute | solution.py:304
  106.5 3.8 %collective-permute-start.8 = (f32[16,512]{1,0:T(8,128)S(1)}, f32[16,512]{1,0:T(8,128)S(1)}, u32[]{:S(2)}, u32[]{:S(2)}) collective-permute-start(f32[16,512]{1,0:T(8,128)S(1)} %get-tuple-element.21), channel_id=1, source_target_pairs={{0,128},{128,0},{1,129},{129,1},{2,130},{130,2},{3,131},{131,3},{4... | collective-permute-start | bytes 98312 | tf_op jit(solution)/shard_map/ppermute | solution.py:304

commit v4 on v2

v4 whole, which is shorter than its diff:
```python
import functools

import jax
import jax.numpy as jnp
from jax import lax
from jax.experimental import pallas as pl
from jax.experimental.pallas import tpu as pltpu
from jax.sharding import Mesh
from jax.sharding import PartitionSpec as P

f32 = jnp.float32
bf16 = jnp.bfloat16

COS_TURN = (
    0.9999999890590225,
    -19.739204499453912,
    64.93911745989556,
    -85.45013953088248,
    60.167630950949295,
    -25.96759924849463,
    6.528658161366808,
)
SIN_TURN = (
    6.283185302511503,
    -41.34170040531749,
    81.60513138579344,
    -76.70301535379849,
    42.02592698556796,
    -14.899846667364866,
    3.238137509743233,
)
NT = (((1,), (1,)), ((), ()))
NN = (((1,), (0,)), ((), ()))
CHUNK = 128
STEP = 128
LIMIT = pltpu.CompilerParams(vmem_limit_bytes=12 * 2**20)


def dot(left, right, dims):
    return lax.dot_general(left, right, dims, preferred_element_type=f32)


def horner(coefs, arg):
    total = jnp.full_like(arg, coefs[-1])
    for coef in coefs[-2::-1]:
        total = total * arg + coef
    return total


def three_parts(values):
    high = values.astype(bf16)
    rest = values - high.astype(f32)
    middle = rest.astype(bf16)
    low = (rest - middle.astype(f32)).astype(bf16)
    return high, middle, low


def atom_table(positions, species, order, first_slot, core, rows, stride, slot_dev):
    atoms = order.shape[1]
    row = lax.broadcasted_iota(jnp.int32, (rows, 1), 0)
    pair = 2 * slot_dev
    side = (row % pair // slot_dev) ^ core
    slot = first_slot + row // pair * stride + side * slot_dev + row % slot_dev
    lane = lax.broadcasted_iota(jnp.int32, (rows, atoms), 1)
    pick_slot = jnp.where(lane == slot, 1.0, 0.0).astype(bf16)
    coarse, fine = order // 128, order % 128
    pad = jnp.zeros((14, atoms), f32)
    digits = jnp.concatenate([coarse.astype(f32), fine.astype(f32), pad], axis=0).astype(bf16)
    found = dot(pick_slot, digits, NT)
    atom = (found[:, 0:1] * 128.0 + found[:, 1:2]).astype(jnp.int32)
    pick_atom = jnp.where(lane == atom, 1.0, 0.0).astype(bf16)
    high, middle, low = three_parts(positions)
    pad = jnp.zeros((6, atoms), bf16)
    facts = jnp.concatenate([high, middle, low, species.astype(f32).astype(bf16), pad], axis=0)
    return dot(pick_atom, facts, NT)


def field_pair(fields):
    half = fields.shape[0] // 2
    return fields, jnp.concatenate([-fields[half:, :], fields[:half, :]], axis=0)


def core_bands(fields_ref, core):
    quarter = fields_ref.shape[0] // 4
    parts = [fields_ref[part * quarter : (part + 1) * quarter, :] for part in range(4)]
    first = jnp.concatenate([parts[0], parts[2]], axis=0)
    second = jnp.concatenate([parts[1], parts[3]], axis=0)
    return jnp.where(core == 0, first, second)


def phases_of(table, miller):
    turns = jnp.zeros((table.shape[0], miller.shape[1]), f32)
    for axis in range(3):
        centre = table[:, axis : axis + 1] + table[:, 3 + axis : 4 + axis]
        centre = centre + table[:, 6 + axis : 7 + axis]
        turns = turns + centre * miller[axis : axis + 1, :]
    turns = turns - jnp.round(turns)
    square = turns * turns
    return horner(COS_TURN, square), turns * horner(SIN_TURN, square)


def kinetic_of(miller, lengths):
    total = jnp.zeros((1, miller.shape[1]), f32)
    for axis in range(3):
        wave_number = lengths[:, axis : axis + 1] * miller[axis : axis + 1, :]
        total = total + wave_number * wave_number
    return 0.5 * total


def both_weights(template):
    low, high = template[:64, :], template[64:, :]
    return jnp.concatenate([low, high, high, low], axis=0)


def double_weights(template):
    low, high = template[:64, :], template[64:, :]
    return jnp.concatenate([low, low, high, high], axis=0)


def prepare_kernel(
    stride, slot_dev, place_ref, lengths_ref, miller_ref, positions_ref, species_ref, order_ref,
    fields_ref, template_ref, cos_ref, sin_ref, select_ref, table_ref, own_ref, kinetic_ref,
    both_ref, double_ref,
):
    atoms = cos_ref.shape[0]
    core = place_ref[:, 1:2]
    table_ref[...] = atom_table(
        positions_ref[...], species_ref[...], order_ref[...], place_ref[:, 0:1], core, atoms,
        stride, slot_dev,
    )
    miller = miller_ref[...].astype(f32)
    kinetic_ref[...] = kinetic_of(miller, lengths_ref[...])
    own_ref[...] = core_bands(fields_ref, core)
    both_ref[...] = both_weights(template_ref[...])
    double_ref[...] = double_weights(template_ref[...])
    low = lax.broadcasted_iota(jnp.int32, (1, 128), 1) < 64

    def step(block, carry):
        base = pl.multiple_of(block * STEP, STEP)
        table = table_ref[pl.ds(base, STEP), :]
        cosine, sine = phases_of(table, miller)
        cos_ref[pl.ds(base, STEP), :] = cosine
        sin_ref[pl.ds(base, STEP), :] = sine
        kinds = table[:, 9:10]
        picked = []
        for pair in range(STEP // 2):
            even = 1.0 - kinds[2 * pair : 2 * pair + 1, :]
            odd = kinds[2 * pair + 1 : 2 * pair + 2, :]
            picked.append(jnp.where(low, even, odd))
        half = pl.ds(pl.multiple_of(block * (STEP // 2), STEP // 2), STEP // 2)
        select_ref[half, :] = jnp.concatenate(picked, axis=0)
        return carry

    lax.fori_loop(0, atoms // STEP, step, 0)


def project_chunk(base, phases, fields, weights, select, out_ref, wave_ref):
    rows = fields[0][0].shape[0]
    products = []
    for side in range(2):
        cosine, sine = phases[side]
        straight, turned = fields[side]
        for pair in range(CHUNK // 2):
            waves = [
                cosine[atom : atom + 1, :] * straight + sine[atom : atom + 1, :] * turned
                for atom in (2 * pair, 2 * pair + 1)
            ]
            two = slice(2 * pair * rows, 2 * (pair + 1) * rows)
            wave_ref[side, two, :] = jnp.concatenate(waves, axis=0).astype(bf16)
        products.append(dot(wave_ref[side], weights[side][...], NT))
    both = products[0] + products[1]
    low = lax.broadcasted_iota(jnp.int32, (rows, 128), 1) < 64
    results = []
    for pair in range(CHUNK // 2):
        even = both[2 * pair * rows : (2 * pair + 1) * rows, :]
        odd = both[(2 * pair + 1) * rows : (2 * pair + 2) * rows, :]
        first = jnp.where(low, even[:, :128], odd[:, :128])
        second = jnp.where(low, even[:, 128:], odd[:, 128:])
        results.append(jnp.where(select[pair : pair + 1, :] > 0.5, first, second))
    size = CHUNK // 2 * rows
    start = pl.multiple_of(base // 2 * rows, size)
    out_ref[pl.ds(start, size), :] = jnp.concatenate(results, axis=0).astype(bf16)


def first_kernel(
    place_ref, lengths_ref, table_ref, miller_ref, own_ref, fields_ref, own_both_ref,
    template_ref, own_cos_ref, own_sin_ref, select_ref, out_ref, cos_ref, sin_ref, other_ref,
    kinetic_ref, both_ref, double_ref, wave_ref,
):
    miller = miller_ref[...].astype(f32)
    kinetic_ref[...] = kinetic_of(miller, lengths_ref[...])
    other = core_bands(fields_ref, place_ref[:, 1:2])
    other_ref[...] = other
    fields = [field_pair(own_ref[...]), field_pair(other)]
    both_ref[...] = both_weights(template_ref[...])
    double_ref[...] = double_weights(template_ref[...])
    weights = [own_both_ref, both_ref]

    def step(block, carry):
        base = pl.multiple_of(block * CHUNK, CHUNK)
        chunk = pl.ds(base, CHUNK)
        cosine, sine = phases_of(table_ref[chunk, :], miller)
        cos_ref[chunk, :] = cosine
        sin_ref[chunk, :] = sine
        phases = [(own_cos_ref[chunk, :], own_sin_ref[chunk, :]), (cosine, sine)]
        size = CHUNK // 2
        select = select_ref[pl.ds(pl.multiple_of(block * size, size), size), :]
        project_chunk(base, phases, fields, weights, select, out_ref, wave_ref)
        return carry

    lax.fori_loop(0, cos_ref.shape[0] // CHUNK, step, 0)


def next_kernel(
    own_kinetic_ref, kinetic_ref, own_ref, other_ref, mine_ref, low_ref, high_ref, both_ref,
    own_weights_ref, weights_ref, own_cos_ref, own_sin_ref, cos_ref, sin_ref, select_ref,
    fields_out_ref, out_ref, wave_ref,
):
    own = own_kinetic_ref[...] * own_ref[...]
    own = own + ((mine_ref[0] + high_ref[0]) + (low_ref[1] + both_ref[1]))
    fields_out_ref[...] = own
    other = kinetic_ref[...] * other_ref[...]
    other = other + ((mine_ref[1] + high_ref[1]) + (low_ref[0] + both_ref[0]))
    fields = [field_pair(own), field_pair(other)]
    weights = [own_weights_ref, weights_ref]

    def step(block, carry):
        base = pl.multiple_of(block * CHUNK, CHUNK)
        chunk = pl.ds(base, CHUNK)
        phases = [
            (own_cos_ref[chunk, :], own_sin_ref[chunk, :]),
            (cos_ref[chunk, :], sin_ref[chunk, :]),
        ]
        size = CHUNK // 2
        select = select_ref[pl.ds(pl.multiple_of(block * size, size), size), :]
        project_chunk(base, phases, fields, weights, select, out_ref, wave_ref)
        return carry

    lax.fori_loop(0, cos_ref.shape[0] // CHUNK, step, 0)


def last_kernel(kinetic_ref, own_ref, mine_ref, low_ref, high_ref, both_ref, out_ref):
    total = kinetic_ref[...] * own_ref[...]
    out_ref[...] = total + ((mine_ref[0] + high_ref[...]) + (low_ref[...] + both_ref[...]))


def join_kernel(
    place_ref, once_ref, other_once_ref, twice_ref, other_twice_ref, once_out_ref, twice_out_ref
):
    core = place_ref[:, 1:2]
    for mine_ref, other_ref, out_ref in (
        (once_ref, other_once_ref, once_out_ref), (twice_ref, other_twice_ref, twice_out_ref)
    ):
        mine, other = mine_ref[...], other_ref[...]
        half = mine.shape[0] // 2
        first = jnp.where(core == 0, mine, other)
        second = jnp.where(core == 0, other, mine)
        parts = [first[:half, :], second[:half, :], first[half:, :], second[half:, :]]
        out_ref[...] = jnp.concatenate(parts, axis=0)


def potential_kernel(parts_ref, own_potential_ref, potential_ref, out_ref):
    summed = jnp.sum(parts_ref[...].astype(f32), axis=0)
    count = potential_ref.shape[0]
    rows = summed.shape[0] // (2 * count)
    half = rows // 2
    low = lax.broadcasted_iota(jnp.int32, (64, 128), 1) < 64
    results = []
    for pair in range(2 * count):
        source = own_potential_ref if pair < count else potential_ref
        blocks = []
        for part in range(2):
            matrices = source[pair % count, part].astype(f32)
            blocks.append(jnp.where(low, matrices, 0.0))
            blocks.append(jnp.where(low, 0.0, matrices))
        weights = jnp.concatenate(blocks, axis=0).astype(bf16)
        high, middle, lowest = three_parts(summed[pair * rows : (pair + 1) * rows, :])
        pieces = jnp.concatenate(
            [high.astype(f32), middle.astype(f32), lowest.astype(f32)], axis=0
        ).astype(bf16)
        product = dot(pieces, weights, NT)
        product = product[2 * rows :, :] + product[rows : 2 * rows, :] + product[:rows, :]
        real, imag = product[:, :128], product[:, 128:]
        results.append(real[:half, :] - imag[half:, :])
        results.append(real[half:, :] + imag[:half, :])
    applied = jnp.concatenate(results, axis=0).astype(bf16)
    out_ref[...] = jnp.broadcast_to(applied[None], out_ref.shape)


def return_kernel(
    applied_ref, own_weights_ref, weights_ref, own_cos_ref, own_sin_ref, cos_ref, sin_ref,
    select_ref, out_ref, stack_ref,
):
    atoms = cos_ref.shape[0]
    _, rows, waves = out_ref.shape
    half = rows // 2
    weights = [own_weights_ref, weights_ref]
    low = lax.broadcasted_iota(jnp.int32, (1, 128), 1) < 64
    zero = jnp.zeros((rows, waves), f32)

    def step(block, carry):
        base = pl.multiple_of(block * CHUNK, CHUNK)
        chunk = pl.ds(base, CHUNK)
        size = CHUNK // 2
        select = select_ref[pl.ds(pl.multiple_of(block * size, size), size), :]
        height = size * rows
        whole = applied_ref[pl.ds(pl.multiple_of(base // 2 * rows, height), height), :]
        whole = whole.astype(f32)
        for pair in range(size):
            applied = whole[pair * rows : (pair + 1) * rows, :]
            chosen = select[pair : pair + 1, :] > 0.5
            two = slice(2 * pair * rows, 2 * (pair + 1) * rows)
            for kind in range(2):
                take_even = low & chosen if kind == 0 else low & ~chosen
                take_odd = ~low & ~chosen if kind == 0 else ~low & chosen
                split = jnp.concatenate(
                    [jnp.where(take_even, applied, 0.0), jnp.where(take_odd, applied, 0.0)], axis=0
                )
                stack_ref[two, kind * 128 : (kind + 1) * 128] = split.astype(bf16)
        sums = []
        for side, (cosines, sines) in enumerate(((own_cos_ref, own_sin_ref), (cos_ref, sin_ref))):
            straight, turned = carry[side]
            cosine, sine = cosines[chunk, :], sines[chunk, :]
            images = dot(stack_ref[...], weights[side][...], NN)
            for atom in range(CHUNK):
                image = images[atom * rows : (atom + 1) * rows, :]
                straight = straight + cosine[atom : atom + 1, :] * image
                turned = turned + sine[atom : atom + 1, :] * image
            sums.append((straight, turned))
        return tuple(sums)

    sums = lax.fori_loop(0, atoms // CHUNK, step, ((zero, zero), (zero, zero)))
    for side, (straight, turned) in enumerate(sums):
        real = straight[:half, :] + turned[half:, :]
        imag = straight[half:, :] - turned[:half, :]
        out_ref[side] = jnp.concatenate([real, imag], axis=0)


def vmem(count):
    return [pl.BlockSpec(memory_space=pltpu.VMEM)] * count


def shape(dims, dtype):
    return jax.ShapeDtypeStruct(dims, dtype)


def call(kernel, args, out_shape, name, scratch_shapes=()):
    return pl.pallas_call(
        kernel,
        in_specs=vmem(len(args)),
        out_specs=tuple(vmem(len(out_shape))),
        out_shape=tuple(out_shape),
        scratch_shapes=scratch_shapes,
        compiler_params=LIMIT,
        name=name,
    )(*args)


def flip(array, *axes):
    pairs = [(place, 2 ** len(axes) - 1 - place) for place in range(2 ** len(axes))]
    return lax.ppermute(array, axes, pairs)


def per_device(bands_in, template, potential, miller, positions, species, atom_order, reciprocal):
    plane = lax.axis_size("zx")
    groups = lax.axis_size("yh") * lax.axis_size("core")
    slot_dev = potential.shape[0]
    atoms = 2 * slot_dev * plane
    species_count, harmonics, waves = template.shape
    bands = bands_in.shape[1]
    rows = bands
    pairs = slot_dev // 2
    message = 2 * pairs * rows
    width = 2 * harmonics
    template = template.reshape(species_count * harmonics, waves)
    fields = bands_in.reshape(2 * bands, waves)
    matrices = potential.reshape(pairs, 2, 2, harmonics, harmonics)
    matrices = matrices.transpose(0, 2, 3, 1, 4).reshape(pairs, 2, harmonics, width)
    core = lax.axis_index("core")
    stride = groups * slot_dev
    first_slot = lax.axis_index("yl") * plane * stride + lax.axis_index("yh") * 2 * slot_dev
    place = jnp.stack([first_slot, core]).astype(jnp.int32).reshape(1, 2)
    lengths = reciprocal.reshape(1, 3)
    coefs_shape = shape((atoms // 2 * rows, width), bf16)
    fields_shape = shape((rows, waves), f32)
    whole_shape = shape((2 * bands, waves), f32)
    phase_shape = shape((atoms, waves), f32)
    kinetic_shape = shape((1, waves), f32)
    weights_shape = shape((2 * width, waves), bf16)
    wave_scratch = pltpu.VMEM((2, CHUNK * rows, waves), bf16)

    other_miller = flip(miller, "yl")
    other_fields = flip(fields, "yl")
    other_template = flip(template, "yl")
    own_cos, own_sin, select, table, own, own_kinetic, own_both, own_double = call(
        functools.partial(prepare_kernel, stride, slot_dev),
        (
            place, lengths, miller, positions, species.reshape(1, -1), atom_order.reshape(1, -1),
            fields, template,
        ),
        (
            phase_shape, phase_shape, shape((atoms // 2, 128), f32), shape((atoms, 16), f32),
            fields_shape, kinetic_shape, weights_shape, weights_shape,
        ),
        "prepare",
    )
    coefs, other_cos, other_sin, other, other_kinetic, other_both, other_double = call(
        first_kernel,
        (
            place, lengths, table, other_miller, own, other_fields, own_both, other_template,
            own_cos, own_sin, select,
        ),
        (
            coefs_shape, phase_shape, phase_shape, fields_shape, kinetic_shape, weights_shape,
            weights_shape,
        ),
        "first",
        [wave_scratch],
    )
    other_matrices = flip(matrices, "core")
    phases = (own_cos, own_sin, other_cos, other_sin, select)

    def return_fields(coefs):
        parts = lax.all_to_all(coefs.reshape(plane, message, width), "zx", 0, 0, tiled=True)
        (applied,) = call(
            potential_kernel,
            (parts, matrices, other_matrices),
            (shape((plane, message, width), bf16),),
            "potential",
        )
        applied = lax.all_to_all(applied, "zx", 0, 0, tiled=True)
        (mine,) = call(
            return_kernel,
            (applied.reshape(atoms // 2 * rows, width), own_double, other_double) + phases,
            (shape((2, rows, waves), f32),),
            "back",
            [pltpu.VMEM((CHUNK * rows, 2 * width), bf16)],
        )
        return mine

    mine = return_fields(coefs)
    once, coefs = call(
        next_kernel,
        (
            own_kinetic, other_kinetic, own, other, mine, flip(mine, "yl"), flip(mine, "yh"),
            flip(mine, "yl", "yh"), own_both, other_both,
        )
        + phases,
        (fields_shape, coefs_shape),
        "next",
        [wave_scratch],
    )
    other_once = flip(once, "core")
    mine = return_fields(coefs)
    (twice,) = call(
        last_kernel,
        (
            own_kinetic, once, mine, flip(mine[1], "yl"), flip(mine[0], "yh"),
            flip(mine[1], "yl", "yh"),
        ),
        (fields_shape,),
        "last",
    )
    once, twice = call(
        join_kernel,
        (place, once, other_once, twice, flip(twice, "core")),
        (whole_shape, whole_shape),
        "join",
    )
    return once.reshape(bands_in.shape), twice.reshape(bands_in.shape)


def solution(mesh):
    pw, groups = mesh.devices.shape
    fine = Mesh(mesh.devices.reshape(2, pw // 2, 2, groups // 2), ("yl", "zx", "yh", "core"))
    waves, slots = ("yl", "zx"), ("yl", "zx", "yh", "core")
    in_specs = (
        P(None, None, waves),
        P(None, None, waves),
        P(slots, None),
        P(None, waves),
        P(),
        P(),
        P(),
        P(),
    )
    out_specs = (P(None, None, waves), P(None, None, waves))
    return jax.shard_map(
        per_device, mesh=fine, in_specs=in_specs, out_specs=out_specs, check_vma=False
    )
```

time: 131 us -> 108 us (0.82)
  Pallas kernels: 28.8 us -> 11.6 us
  waiting for transfers between devices: 17.7 us -> 12.1 us
  starting transfers between devices: 30.3 us -> 35.1 us
  blocking collectives: 45.7 us -> 43 us
  other arithmetic: 1.7 us -> 0.07 us
    pallas_call x8 -> x9, Pallas kernels: 28.8 us -> 11.6 us  [call(): pl.pallas_call(kernel, in_specs=vmem(len(args)), out_specs=tuple(vmem(len...]
    ppermute x11 -> x12, starting transfers between devices: 19.1 us -> 24 us  [flip(): return lax.ppermute(array, axes, pairs)]
    ppermute x11 -> x12, waiting for transfers between devices: 8.36 us -> 4.96 us  [flip(): return lax.ppermute(array, axes, pairs)]
    all_to_all x1, waiting for transfers between devices: 9.34 us -> 7.18 us  [return_fields(): lax.all_to_all(coefs.reshape(plane, message, width), 'zx', 0, 0, tiled=True)]
    add x2 -> x0, other arithmetic: 1.7 us -> none  [return_fields(): return own + flip(own, 'core')]
    all_to_all x2, blocking collectives: 30.6 us -> 29 us  [return_fields(): applied = lax.all_to_all(applied, 'zx', 0, 0, tiled=True)]
    unnamed x26 -> x20, local copies, waits for them, and re-layouts: 3.77 us -> 4.36 us
  transfers between devices with their start and end apart: 12 -> 13, of which waited for: 7 -> 5; matrix products, arithmetic and copies ran while one was open for 1% -> 0% of each run, Pallas kernels for 3% -> 2%
where the time goes in v4:
time: 108 us
  blocking collectives  43 us (40%)
  starting transfers between devices  35.1 us (32%)
  waiting for transfers between devices  12.1 us (11%)
  Pallas kernels  11.6 us (11%)
  local copies, waits for them, and re-layouts  4.78 us (4%)
    all_to_all x2, blocking collectives, return_fields(): applied = lax.all_to_all(applied, 'zx', 0, 0, tiled=True)  29 us
    ppermute x12, starting transfers between devices, flip(): return lax.ppermute(array, axes, pairs)  24 us
    all_to_all x1, blocking collectives, return_fields(): lax.all_to_all(coefs.reshape(plane, message, width), 'zx', 0, 0, tiled=True)  14 us
    pallas_call x9, Pallas kernels, call(): pl.pallas_call(kernel, in_specs=vmem(len(args)), out_specs=tuple(vmem(len...  11.6 us
    all_to_all x1, starting transfers between devices, return_fields(): lax.all_to_all(coefs.reshape(plane, message, width), 'zx', 0, 0, tiled=True)  11.2 us
    all_to_all x1, waiting for transfers between devices, return_fields(): lax.all_to_all(coefs.reshape(plane, message, width), 'zx', 0, 0, tiled=True)  7.18 us
    ppermute x12, waiting for transfers between devices, flip(): return lax.ppermute(array, axes, pairs)  4.96 us
    unnamed x20, local copies, waits for them, and re-layouts  4.36 us
  transfers between devices with their start and end apart: 13, of which 5 were waited for; matrix products, arithmetic and copies ran while one was open for 0% of the time, Pallas kernels for 2%

profile of v4, /device:TPU:1, one launch (start us, length us, event | category | flops | bytes accessed | tf_op | source)
XLA Modules:
  0.0 107.6 jit_solution(16978271707445263902)
XLA Ops:
  0.6 2.2 %collective-permute-start.2 = (bf16[128,512]{1,0:T(8,128)(2,1)}, bf16[128,512]{1,0:T(8,128)(2,1)S(1)}, u32[]{:S(2)}, u32[]{:S(2)}) collective-permute-start(bf16[128,512]{1,0:T(8,128)(2,1)} %bitcast.25), channel_id=1, source_target_pairs={{0,128},{128,0},{1,129},{129,1},{2,130},{130,2},{3,131},{131,3},{4... | collective-permute-start | bytes 393224 | tf_op jit(solution)/shard_map/ppermute | solution.py:361
  2.9 1.4 %collective-permute-start = (s32[3,512]{1,0:T(4,128)}, s32[3,512]{1,0:T(4,128)S(1)}, u32[]{:S(2)}, u32[]{:S(2)}) collective-permute-start(s32[3,512]{1,0:T(4,128)} %miller_ref.1), channel_id=1, source_target_pairs={{0,128},{128,0},{1,129},{129,1},{2,130},{130,2},{3,131},{131,3},{4... | collective-permute-start | bytes 18440 | tf_op jit(solution)/shard_map/ppermute | solution.py:361
  4.4 0.6 copy-done.6
  5.0 0.9 copy-done.2
  5.9 0.7 copy-done.4
  6.7 0.7 copy-done.5
  7.4 0.7 copy-done.7
  8.0 2.0 %prepare.1 = (f32[256,512]{1,0:T(8,128)S(1)}, f32[256,512]{1,0:T(8,128)S(1)}, f32[128,128]{1,0:T(8,128)S(1)}, f32[256,16]{1,0:T(8,128)S(1)}, f32[8,512]{1,0:T(8,...) custom-call(s32[1,2]{1,0:T(1,128)S(1)} %add_bitcast_fusion.place_ref, ...), custom_call_target="tpu_custom_call" | custom-call | tf_op jit(solution)/shard_map/prepare/pallas_call | solution.py:348
  10.1 3.3 %first.1 = (bf16[1024,128]{1,0:T(8,128)(2,1)}, f32[256,512]{1,0:T(8,128)S(1)}, f32[256,512]{1,0:T(8,128)S(1)}, f32[8,512]{1,0:T(8,128)S(1)}, f32[1,512]{1,0:T(1,...) custom-call(s32[1,2]{1,0:T(1,128)S(1)} %add_bitcast_fusion.place_ref, f32[1,3]{1,0:T(1,128)S(1)} %bitcast.32, ...), custom_call_target="tpu_custom_call" | custom-call | tf_op jit(solution)/shard_map/first/pallas_call | solution.py:348
  13.5 0.7 copy-done
  14.2 11.2 %all-to-all-start = ((bf16[32,32,128]{2,1,0:T(8,128)(2,1)}), bf16[32,32,128]{2,1,0:T(8,128)(2,1)S(1)}, u32[]{:S(2)}, u32[]{:S(2)}) async-start(bf16[32,32,128]{2,1,0:T(8,128)(2,1)} %bitcast.8), calls=%async_computation | async-start | bytes 524288 | tf_op jit(solution)/shard_map/all_to_all | solution.py:424
  25.8 1.9 %collective-permute-start.3 = (bf16[2,2,64,128]{3,2,1,0:T(8,128)(2,1)S(1)}, bf16[2,2,64,128]{3,2,1,0:T(8,128)(2,1)S(1)}, u32[]{:S(2)}, u32[]{:S(2)}) collective-permute-start(bf16[2,2,64,128]{3,2,1,0:T(8,128)(2,1)S(1)} %reshape.54.own_potential_ref), channel_id=1, source_target_pairs={{0,1},{1,0},{2,3},{3,2},{4,5},{5,4},{6,7},{7,6},{8,9},{9,8},{10,11... | collective-permute-start | bytes 196616 | tf_op jit(solution)/shard_map/ppermute | solution.py:361
  27.7 0.9 collective-permute-done.3.potential_ref
  28.6 7.2 %all-to-all-done.parts_ref = bf16[32,32,128]{2,1,0:T(8,128)(2,1)S(1)} async-done(((bf16[32,32,128]{2,1,0:T(8,128)(2,1)}), bf16[32,32,128]{2,1,0:T(8,128)(2,1)S(1)}, u32[]{:S(2)}, u32[]{:S(2)}) %all-to-all-start) | async-done | bytes 262176 | tf_op jit(solution)/shard_map/all_to_all | solution.py:424
  36.0 15.1 %all_to_all.20 = bf16[32,32,128]{2,1,0:T(8,128)(2,1)S(1)} all-to-all(bf16[32,32,128]{2,1,0:T(8,128)(2,1)S(1)} %potential.2), channel_id=1, replica_groups=mesh['yl'=2,'zx'=32,'yh'=2,'core'=2] {'zx'}, dimensions={0} | all-to-all | bytes 524288 | tf_op jit(solution)/shard_map/all_to_all | solution.py:431
  51.1 1.8 %back.2.mine_ref = f32[2,8,512]{2,1,0:T(8,128)S(1)} custom-call(bf16[1024,128]{1,0:T(8,128)(2,1)S(1)} %bitcast.23, bf16[256,512]{1,0:T(8,128)(2,1)S(1)} %get-tuple-element.31.own_weights_ref, bf16[256,512]{1,0:T(8,128)(2,1)S(1)} %get-tuple-element.32.weights_ref, f32[256,512]{1,0:T(8,128)S(1)} %get-tuple-element.25.own_cos_ref, ...), custom_call_target="tpu_custom_call" | custom-call | tf_op jit(solution)/shard_map/back/pallas_call | solution.py:348
  52.8 0.2 collective-permute-start.4
  53.1 2.9 %collective-permute-start.5 = (f32[2,8,512]{2,1,0:T(8,128)S(1)}, f32[2,8,512]{2,1,0:T(8,128)S(1)}, u32[]{:S(2)}, u32[]{:S(2)}) collective-permute-start(f32[2,8,512]{2,1,0:T(8,128)S(1)} %back.2.mine_ref), channel_id=1, source_target_pairs={{0,2},{2,0},{1,3},{3,1},{4,6},{6,4},{5,7},{7,5},{8,10},{10,8},{9,1... | collective-permute-start | bytes 98312 | tf_op jit(solution)/shard_map/ppermute | solution.py:361
  56.0 0.8 collective-permute-start.6
  56.8 0.9 collective-permute-done.5.high_ref
  57.7 2.3 %collective-permute-done.6.both_ref = f32[2,8,512]{2,1,0:T(8,128)S(1)} collective-permute-done((f32[2,8,512]{2,1,0:T(8,128)S(1)}, f32[2,8,512]{2,1,0:T(8,128)S(1)}, u32[]{:S(2)}, u32[]{:S(2)}) %collective-permute-start.6) | collective-permute-done | bytes 32800 | tf_op jit(solution)/shard_map/ppermute | solution.py:361
  60.0 1.6 %next.1 = (f32[8,512]{1,0:T(8,128)S(1)}, bf16[1024,128]{1,0:T(8,128)(2,1)S(1)}) custom-call(f32[1,512]{1,0:T(1,128)S(1)} %get-tuple-element.21.own_kinetic_ref.kinetic_ref, f32[1,512]{1,0:T(1,128)S(1)} %get-tuple-element.28.kinetic_ref, f32[8,512]{1,0:T(8,128)S(1)} %get-tuple-element.23.own_ref, f32[8,512]{1,0:T(8,128)S(1)} %get-tuple-element.29.other_ref, ...), custom_call_target="tpu_custom_call" | custom-call | tf_op jit(solution)/shard_map/next/pallas_call | solution.py:348
  61.6 14.0 %all_to_all.21.parts_ref = bf16[32,32,128]{2,1,0:T(8,128)(2,1)S(1)} all-to-all(bf16[32,32,128]{2,1,0:T(8,128)(2,1)S(1)} %bitcast.24), channel_id=1, replica_groups=mesh['yl'=2,'zx'=32,'yh'=2,'core'=2] {'zx'}, dimensions={0} | all-to-all | bytes 524288 | tf_op jit(solution)/shard_map/all_to_all | solution.py:424
  75.6 0.2 potential.3
  75.9 13.9 %all_to_all.22 = bf16[32,32,128]{2,1,0:T(8,128)(2,1)S(1)} all-to-all(bf16[32,32,128]{2,1,0:T(8,128)(2,1)S(1)} %potential.3), channel_id=1, replica_groups=mesh['yl'=2,'zx'=32,'yh'=2,'core'=2] {'zx'}, dimensions={0} | all-to-all | bytes 524288 | tf_op jit(solution)/shard_map/all_to_all | solution.py:431
  89.7 1.7 %back.3.mine_ref = f32[2,8,512]{2,1,0:T(8,128)S(1)} custom-call(bf16[1024,128]{1,0:T(8,128)(2,1)S(1)} %bitcast.22, bf16[256,512]{1,0:T(8,128)(2,1)S(1)} %get-tuple-element.31.own_weights_ref, bf16[256,512]{1,0:T(8,128)(2,1)S(1)} %get-tuple-element.32.weights_ref, f32[256,512]{1,0:T(8,128)S(1)} %get-tuple-element.25.own_cos_ref, ...), custom_call_target="tpu_custom_call" | custom-call | tf_op jit(solution)/shard_map/back/pallas_call | solution.py:348
  91.5 0.9 collective-permute-start.10
  92.4 3.1 %collective-permute-start.9 = (f32[8,512]{1,0:T(8,128)S(1)}, f32[8,512]{1,0:T(8,128)S(1)}, u32[]{:S(2)}, u32[]{:S(2)}) collective-permute-start(f32[8,512]{1,0:T(8,128)S(1)} %get-tuple-element.40), channel_id=1, source_target_pairs={{0,2},{2,0},{1,3},{3,1},{4,6},{6,4},{5,7},{7,5},{8,10},{10,8},{9,1... | collective-permute-start | bytes 49160 | tf_op jit(solution)/shard_map/ppermute | solution.py:361
  95.4 8.6 %collective-permute-start.7 = (f32[8,512]{1,0:T(8,128)S(1)}, f32[8,512]{1,0:T(8,128)S(1)}, u32[]{:S(2)}, u32[]{:S(2)}) collective-permute-start(f32[8,512]{1,0:T(8,128)S(1)} %get-tuple-element.36.own_ref.once_ref), channel_id=1, source_target_pairs={{0,1},{1,0},{2,3},{3,2},{4,5},{5,4},{6,7},{7,6},{8,9},{9,8},{10,11... | collective-permute-start | bytes 49160 | tf_op jit(solution)/shard_map/ppermute | solution.py:361
  104.1 2.0 %collective-permute-start.11 = (f32[8,512]{1,0:T(8,128)S(1)}, f32[8,512]{1,0:T(8,128)S(1)}, u32[]{:S(2)}, u32[]{:S(2)}) collective-permute-start(f32[8,512]{1,0:T(8,128)S(1)} %last.1.twice_ref), channel_id=1, source_target_pairs={{0,1},{1,0},{2,3},{3,2},{4,5},{5,4},{6,7},{7,6},{8,9},{9,8},{10,11... | collective-permute-start | bytes 49160 | tf_op jit(solution)/shard_map/ppermute | solution.py:361
  106.0 0.8 collective-permute-done.11.other_twice_ref
  106.9 0.7 join.1
  (31 shorter events, 0.9 us)
Async XLA Ops:
  0.6 3.8 %copy-start.3 = (f32[2,8,512]{2,1,0:T(8,128)S(1)}, f32[2,8,512]{2,1,0:T(8,128)}, u32[]{:S(2)}) copy-start(f32[2,8,512]{2,1,0:T(8,128)} %param.8) | copy-start | bytes 98308
  0.6 9.5 %collective-permute-start.2 = (bf16[128,512]{1,0:T(8,128)(2,1)}, bf16[128,512]{1,0:T(8,128)(2,1)S(1)}, u32[]{:S(2)}, u32[]{:S(2)}) collective-permute-start(bf16[128,512]{1,0:T(8,128)(2,1)} %bitcast.25), channel_id=1, source_target_pairs={{0,128},{128,0},{1,129},{129,1},{2,130},{130,2},{3,131},{131,3},{4... | collective-permute-start | bytes 393224 | tf_op jit(solution)/shard_map/ppermute | solution.py:361
  2.8 7.3 %collective-permute-start.1 = (f32[16,512]{1,0:T(8,128)}, f32[16,512]{1,0:T(8,128)S(1)}, u32[]{:S(2)}, u32[]{:S(2)}) collective-permute-start(f32[16,512]{1,0:T(8,128)} %bitcast.27), channel_id=1, source_target_pairs={{0,128},{128,0},{1,129},{129,1},{2,130},{130,2},{3,131},{131,3},{4... | collective-permute-start | bytes 98312 | tf_op jit(solution)/shard_map/ppermute | solution.py:361
  2.9 7.1 %collective-permute-start = (s32[3,512]{1,0:T(4,128)}, s32[3,512]{1,0:T(4,128)S(1)}, u32[]{:S(2)}, u32[]{:S(2)}) collective-permute-start(s32[3,512]{1,0:T(4,128)} %miller_ref.1), channel_id=1, source_target_pairs={{0,128},{128,0},{1,129},{129,1},{2,130},{130,2},{3,131},{131,3},{4... | collective-permute-start | bytes 18440 | tf_op jit(solution)/shard_map/ppermute | solution.py:361
  4.3 0.7 copy-start.6
  4.4 0.7 copy-start.8
  5.0 0.9 copy-start.2
  5.9 0.7 copy-start.4
  6.7 0.7 copy-start.5
  7.4 0.7 copy-start.7
  13.5 0.7 copy-start
  14.2 11.2 %copy-start.9 = (bf16[4,8192]{1,0:T(4,128)(2,1)S(1)}, bf16[4,8192]{1,0:T(4,128)(2,1)}, u32[]{:S(2)}) copy-start(bf16[4,8192]{1,0:T(4,128)(2,1)} %param.10) | copy-start | bytes 196612
  14.2 21.6 %all-to-all-start = ((bf16[32,32,128]{2,1,0:T(8,128)(2,1)}), bf16[32,32,128]{2,1,0:T(8,128)(2,1)S(1)}, u32[]{:S(2)}, u32[]{:S(2)}) async-start(bf16[32,32,128]{2,1,0:T(8,128)(2,1)} %bitcast.8), calls=%async_computation | async-start | bytes 524288 | tf_op jit(solution)/shard_map/all_to_all | solution.py:424
  25.8 2.8 %collective-permute-start.3 = (bf16[2,2,64,128]{3,2,1,0:T(8,128)(2,1)S(1)}, bf16[2,2,64,128]{3,2,1,0:T(8,128)(2,1)S(1)}, u32[]{:S(2)}, u32[]{:S(2)}) collective-permute-start(bf16[2,2,64,128]{3,2,1,0:T(8,128)(2,1)S(1)} %reshape.54.own_potential_ref), channel_id=1, source_target_pairs={{0,1},{1,0},{2,3},{3,2},{4,5},{5,4},{6,7},{7,6},{8,9},{9,8},{10,11... | collective-permute-start | bytes 196616 | tf_op jit(solution)/shard_map/ppermute | solution.py:361
  51.1 8.9 %copy-start.1 = (bf16[256,512]{1,0:T(8,128)(2,1)S(1)}, bf16[256,512]{1,0:T(8,128)(2,1)}, u32[]{:S(2)}) copy-start(bf16[256,512]{1,0:T(8,128)(2,1)} %copy-done) | copy-start | bytes 786436
  52.8 3.9 %collective-permute-start.4 = (f32[2,8,512]{2,1,0:T(8,128)S(1)}, f32[2,8,512]{2,1,0:T(8,128)S(1)}, u32[]{:S(2)}, u32[]{:S(2)}) collective-permute-start(f32[2,8,512]{2,1,0:T(8,128)S(1)} %back.2.mine_ref), channel_id=1, source_target_pairs={{0,128},{128,0},{1,129},{129,1},{2,130},{130,2},{3,131},{131,3},{4... | collective-permute-start | bytes 98312 | tf_op jit(solution)/shard_map/ppermute | solution.py:361
  53.1 4.6 %collective-permute-start.5 = (f32[2,8,512]{2,1,0:T(8,128)S(1)}, f32[2,8,512]{2,1,0:T(8,128)S(1)}, u32[]{:S(2)}, u32[]{:S(2)}) collective-permute-start(f32[2,8,512]{2,1,0:T(8,128)S(1)} %back.2.mine_ref), channel_id=1, source_target_pairs={{0,2},{2,0},{1,3},{3,1},{4,6},{6,4},{5,7},{7,5},{8,10},{10,8},{9,1... | collective-permute-start | bytes 98312 | tf_op jit(solution)/shard_map/ppermute | solution.py:361
  56.0 4.0 %collective-permute-start.6 = (f32[2,8,512]{2,1,0:T(8,128)S(1)}, f32[2,8,512]{2,1,0:T(8,128)S(1)}, u32[]{:S(2)}, u32[]{:S(2)}) collective-permute-start(f32[2,8,512]{2,1,0:T(8,128)S(1)} %back.2.mine_ref), channel_id=1, source_target_pairs={{0,130},{2,128},{128,2},{130,0},{1,131},{3,129},{129,3},{131,1},{4... | collective-permute-start | bytes 98312 | tf_op jit(solution)/shard_map/ppermute | solution.py:361
  91.5 12.5 %collective-permute-start.10 = (f32[8,512]{1,0:T(8,128)S(1)}, f32[8,512]{1,0:T(8,128)S(1)}, u32[]{:S(2)}, u32[]{:S(2)}) collective-permute-start(f32[8,512]{1,0:T(8,128)S(1)} %get-tuple-element.41), channel_id=1, source_target_pairs={{0,130},{2,128},{128,2},{130,0},{1,131},{3,129},{129,3},{131,1},{4... | collective-permute-start | bytes 49160 | tf_op jit(solution)/shard_map/ppermute | solution.py:361
  92.4 11.7 %collective-permute-start.8 = (f32[8,512]{1,0:T(8,128)S(1)}, f32[8,512]{1,0:T(8,128)S(1)}, u32[]{:S(2)}, u32[]{:S(2)}) collective-permute-start(f32[8,512]{1,0:T(8,128)S(1)} %get-tuple-element.41), channel_id=1, source_target_pairs={{0,128},{128,0},{1,129},{129,1},{2,130},{130,2},{3,131},{131,3},{4... | collective-permute-start | bytes 49160 | tf_op jit(solution)/shard_map/ppermute | solution.py:361
  92.4 11.7 %collective-permute-start.9 = (f32[8,512]{1,0:T(8,128)S(1)}, f32[8,512]{1,0:T(8,128)S(1)}, u32[]{:S(2)}, u32[]{:S(2)}) collective-permute-start(f32[8,512]{1,0:T(8,128)S(1)} %get-tuple-element.40), channel_id=1, source_target_pairs={{0,2},{2,0},{1,3},{3,1},{4,6},{6,4},{5,7},{7,5},{8,10},{10,8},{9,1... | collective-permute-start | bytes 49160 | tf_op jit(solution)/shard_map/ppermute | solution.py:361
  95.4 10.6 %collective-permute-start.7 = (f32[8,512]{1,0:T(8,128)S(1)}, f32[8,512]{1,0:T(8,128)S(1)}, u32[]{:S(2)}, u32[]{:S(2)}) collective-permute-start(f32[8,512]{1,0:T(8,128)S(1)} %get-tuple-element.36.own_ref.once_ref), channel_id=1, source_target_pairs={{0,1},{1,0},{2,3},{3,2},{4,5},{5,4},{6,7},{7,6},{8,9},{9,8},{10,11... | collective-permute-start | bytes 49160 | tf_op jit(solution)/shard_map/ppermute | solution.py:361
  104.1 2.8 %collective-permute-start.11 = (f32[8,512]{1,0:T(8,128)S(1)}, f32[8,512]{1,0:T(8,128)S(1)}, u32[]{:S(2)}, u32[]{:S(2)}) collective-permute-start(f32[8,512]{1,0:T(8,128)S(1)} %last.1.twice_ref), channel_id=1, source_target_pairs={{0,1},{1,0},{2,3},{3,2},{4,5},{5,4},{6,7},{7,6},{8,9},{9,8},{10,11... | collective-permute-start | bytes 49160 | tf_op jit(solution)/shard_map/ppermute | solution.py:361

commit v5 on v4

--- a/solution.py
+++ b/solution.py
@@ -118,10 +118,22 @@
 
 
 def prepare_kernel(
-    stride, slot_dev, place_ref, lengths_ref, miller_ref, positions_ref, species_ref, order_ref,
-    fields_ref, template_ref, cos_ref, sin_ref, select_ref, table_ref, own_ref, kinetic_ref,
-    both_ref, double_ref,
+    stride, slot_dev, place_ref, *refs,
 ):
+    sources, refs = refs[:7], refs[7:]
+    cos_ref, sin_ref, select_ref, table_ref, own_ref, kinetic_ref, both_ref, kept_ref = refs[:8]
+    targets, semaphores = refs[8:15], refs[15]
+    copies = [
+        pltpu.make_async_copy(source, target, semaphores.at[number])
+        for number, (source, target) in enumerate(zip(sources, targets))
+    ]
+    for copy in copies:
+        copy.start()
+    for copy in copies:
+        copy.wait()
+    order_ref, positions_ref, species_ref, miller_ref = targets[:4]
+    lengths_ref, fields_ref, template_ref = targets[4:]
+    kept_ref[...] = lengths_ref[...]
     atoms = cos_ref.shape[0]
     core = place_ref[:, 1:2]
     table_ref[...] = atom_table(
@@ -132,7 +144,6 @@
     kinetic_ref[...] = kinetic_of(miller, lengths_ref[...])
     own_ref[...] = core_bands(fields_ref, core)
     both_ref[...] = both_weights(template_ref[...])
-    double_ref[...] = double_weights(template_ref[...])
     low = lax.broadcasted_iota(jnp.int32, (1, 128), 1) < 64
 
     def step(block, carry):
@@ -185,7 +196,7 @@
 def first_kernel(
     place_ref, lengths_ref, table_ref, miller_ref, own_ref, fields_ref, own_both_ref,
     template_ref, own_cos_ref, own_sin_ref, select_ref, out_ref, cos_ref, sin_ref, other_ref,
-    kinetic_ref, both_ref, double_ref, wave_ref,
+    kinetic_ref, both_ref, wave_ref,
 ):
     miller = miller_ref[...].astype(f32)
     kinetic_ref[...] = kinetic_of(miller, lengths_ref[...])
@@ -193,7 +204,6 @@
     other_ref[...] = other
     fields = [field_pair(own_ref[...]), field_pair(other)]
     both_ref[...] = both_weights(template_ref[...])
-    double_ref[...] = double_weights(template_ref[...])
     weights = [own_both_ref, both_ref]
 
     def step(block, carry):
@@ -212,15 +222,15 @@
 
 
 def next_kernel(
-    own_kinetic_ref, kinetic_ref, own_ref, other_ref, mine_ref, low_ref, high_ref, both_ref,
+    own_kinetic_ref, kinetic_ref, own_ref, other_ref, near_ref, far_ref,
     own_weights_ref, weights_ref, own_cos_ref, own_sin_ref, cos_ref, sin_ref, select_ref,
     fields_out_ref, out_ref, wave_ref,
 ):
     own = own_kinetic_ref[...] * own_ref[...]
-    own = own + ((mine_ref[0] + high_ref[0]) + (low_ref[1] + both_ref[1]))
+    own = own + (near_ref[0] + far_ref[1])
     fields_out_ref[...] = own
     other = kinetic_ref[...] * other_ref[...]
-    other = other + ((mine_ref[1] + high_ref[1]) + (low_ref[0] + both_ref[0]))
+    other = other + (near_ref[1] + far_ref[0])
     fields = [field_pair(own), field_pair(other)]
     weights = [own_weights_ref, weights_ref]
 
@@ -239,19 +249,20 @@
     lax.fori_loop(0, cos_ref.shape[0] // CHUNK, step, 0)
 
 
-def last_kernel(kinetic_ref, own_ref, mine_ref, low_ref, high_ref, both_ref, out_ref):
-    total = kinetic_ref[...] * own_ref[...]
-    out_ref[...] = total + ((mine_ref[0] + high_ref[...]) + (low_ref[...] + both_ref[...]))
-
-
-def join_kernel(
-    place_ref, once_ref, other_once_ref, twice_ref, other_twice_ref, once_out_ref, twice_out_ref
-):
+def near_kernel(mine_ref, low_ref, out_ref):
+    out_ref[0] = mine_ref[0] + low_ref[1]
+    out_ref[1] = mine_ref[1] + low_ref[0]
+
+
+def last_kernel(kinetic_ref, own_ref, near_ref, far_ref, out_ref):
+    out_ref[0] = own_ref[...]
+    out_ref[1] = kinetic_ref[...] * own_ref[...] + (near_ref[0] + far_ref[...])
+
+
+def join_kernel(place_ref, mine_ref, other_ref, once_ref, twice_ref):
     core = place_ref[:, 1:2]
-    for mine_ref, other_ref, out_ref in (
-        (once_ref, other_once_ref, once_out_ref), (twice_ref, other_twice_ref, twice_out_ref)
-    ):
-        mine, other = mine_ref[...], other_ref[...]
+    for number, out_ref in enumerate((once_ref, twice_ref)):
+        mine, other = mine_ref[number], other_ref[number]
         half = mine.shape[0] // 2
         first = jnp.where(core == 0, mine, other)
         second = jnp.where(core == 0, other, mine)
@@ -288,13 +299,13 @@
 
 
 def return_kernel(
-    applied_ref, own_weights_ref, weights_ref, own_cos_ref, own_sin_ref, cos_ref, sin_ref,
+    applied_ref, own_template_ref, template_ref, own_cos_ref, own_sin_ref, cos_ref, sin_ref,
     select_ref, out_ref, stack_ref,
 ):
     atoms = cos_ref.shape[0]
     _, rows, waves = out_ref.shape
     half = rows // 2
-    weights = [own_weights_ref, weights_ref]
+    weights = [double_weights(own_template_ref[...]), double_weights(template_ref[...])]
     low = lax.broadcasted_iota(jnp.int32, (1, 128), 1) < 64
     zero = jnp.zeros((rows, waves), f32)
 
@@ -321,7 +332,7 @@
         for side, (cosines, sines) in enumerate(((own_cos_ref, own_sin_ref), (cos_ref, sin_ref))):
             straight, turned = carry[side]
             cosine, sine = cosines[chunk, :], sines[chunk, :]
-            images = dot(stack_ref[...], weights[side][...], NN)
+            images = dot(stack_ref[...], weights[side], NN)
             for atom in range(CHUNK):
                 image = images[atom * rows : (atom + 1) * rows, :]
                 straight = straight + cosine[atom : atom + 1, :] * image
@@ -344,10 +355,10 @@
     return jax.ShapeDtypeStruct(dims, dtype)
 
 
-def call(kernel, args, out_shape, name, scratch_shapes=()):
+def call(kernel, args, out_shape, name, scratch_shapes=(), unread=0):
     return pl.pallas_call(
         kernel,
-        in_specs=vmem(len(args)),
+        in_specs=vmem(len(args) - unread) + [pl.BlockSpec(memory_space=pltpu.HBM)] * unread,
         out_specs=tuple(vmem(len(out_shape))),
         out_shape=tuple(out_shape),
         scratch_shapes=scratch_shapes,
@@ -392,19 +403,24 @@
     other_miller = flip(miller, "yl")
     other_fields = flip(fields, "yl")
     other_template = flip(template, "yl")
-    own_cos, own_sin, select, table, own, own_kinetic, own_both, own_double = call(
+    inputs = (
+        atom_order.reshape(1, -1), positions, species.reshape(1, -1), miller, lengths, fields,
+        template,
+    )
+    inputs = tuple(pltpu.with_memory_space_constraint(value, pltpu.HBM) for value in inputs)
+    own_cos, own_sin, select, table, own, own_kinetic, own_both, lengths = call(
         functools.partial(prepare_kernel, stride, slot_dev),
-        (
-            place, lengths, miller, positions, species.reshape(1, -1), atom_order.reshape(1, -1),
-            fields, template,
-        ),
+        (place,) + inputs,
         (
             phase_shape, phase_shape, shape((atoms // 2, 128), f32), shape((atoms, 16), f32),
-            fields_shape, kinetic_shape, weights_shape, weights_shape,
+            fields_shape, kinetic_shape, weights_shape, shape(lengths.shape, f32),
         ),
         "prepare",
-    )
-    coefs, other_cos, other_sin, other, other_kinetic, other_both, other_double = call(
+        [pltpu.VMEM(value.shape, value.dtype) for value in inputs]
+        + [pltpu.SemaphoreType.DMA((len(inputs),))],
+        unread=len(inputs),
+    )
+    coefs, other_cos, other_sin, other, other_kinetic, other_both = call(
         first_kernel,
         (
             place, lengths, table, other_miller, own, other_fields, own_both, other_template,
@@ -412,7 +428,6 @@
         ),
         (
             coefs_shape, phase_shape, phase_shape, fields_shape, kinetic_shape, weights_shape,
-            weights_shape,
         ),
         "first",
         [wave_scratch],
@@ -431,41 +446,37 @@
         applied = lax.all_to_all(applied, "zx", 0, 0, tiled=True)
         (mine,) = call(
             return_kernel,
-            (applied.reshape(atoms // 2 * rows, width), own_double, other_double) + phases,
+            (applied.reshape(atoms // 2 * rows, width), template, other_template) + phases,
             (shape((2, rows, waves), f32),),
             "back",
             [pltpu.VMEM((CHUNK * rows, 2 * width), bf16)],
         )
-        return mine
-
-    mine = return_fields(coefs)
+        (near,) = call(
+            near_kernel, (mine, flip(mine, "yl")), (shape((2, rows, waves), f32),), "near"
+        )
+        return near
+
+    near = return_fields(coefs)
     once, coefs = call(
         next_kernel,
         (
-            own_kinetic, other_kinetic, own, other, mine, flip(mine, "yl"), flip(mine, "yh"),
-            flip(mine, "yl", "yh"), own_both, other_both,
+            own_kinetic, other_kinetic, own, other, near, flip(near, "yl", "yh"), own_both,
+            other_both,
         )
         + phases,
         (fields_shape, coefs_shape),
         "next",
         [wave_scratch],
     )
-    other_once = flip(once, "core")
-    mine = return_fields(coefs)
-    (twice,) = call(
+    near = return_fields(coefs)
+    (mine,) = call(
         last_kernel,
-        (
-            own_kinetic, once, mine, flip(mine[1], "yl"), flip(mine[0], "yh"),
-            flip(mine[1], "yl", "yh"),
-        ),
-        (fields_shape,),
+        (own_kinetic, once, near, flip(near[1], "yl", "yh")),
+        (shape((2, rows, waves), f32),),
         "last",
     )
     once, twice = call(
-        join_kernel,
-        (place, once, other_once, twice, flip(twice, "core")),
-        (whole_shape, whole_shape),
-        "join",
+        join_kernel, (place, mine, flip(mine, "core")), (whole_shape, whole_shape), "join"
     )
     return once.reshape(bands_in.shape), twice.reshape(bands_in.shape)
 

time: 108 us -> 107 us (level)
  waiting for transfers between devices: 12.1 us -> 17.9 us
  local copies, waits for them, and re-layouts: 4.78 us -> 0.43 us
  starting transfers between devices: 35.1 us -> 32 us
  Pallas kernels: 11.6 us -> 12.7 us
    ppermute x12 -> x9, waiting for transfers between devices: 4.96 us -> 10.8 us  [flip(): return lax.ppermute(array, axes, pairs)]
    unnamed x20 -> x4, local copies, waits for them, and re-layouts: 4.36 us -> 0.01 us
    ppermute x12 -> x9, starting transfers between devices: 24 us -> 20.8 us  [flip(): return lax.ppermute(array, axes, pairs)]
    pallas_call x9 -> x11, Pallas kernels: 11.6 us -> 12.7 us  [call(): pl.pallas_call(kernel, in_specs=vmem(len(args) - unread) + [pl.BlockSpec(...]
  transfers between devices with their start and end apart: 13 -> 10, of which waited for: 5 -> 7; matrix products, arithmetic and copies ran while one was open for 0% -> 0% of each run, Pallas kernels for 2% -> 3%
where the time goes in v5:
time: 107 us
  blocking collectives  43 us (40%)
  starting transfers between devices  32 us (30%)
  waiting for transfers between devices  17.9 us (17%)
  Pallas kernels  12.7 us (12%)
    all_to_all x2, blocking collectives, return_fields(): applied = lax.all_to_all(applied, 'zx', 0, 0, tiled=True)  29 us
    ppermute x9, starting transfers between devices, flip(): return lax.ppermute(array, axes, pairs)  20.8 us
    all_to_all x1, blocking collectives, return_fields(): lax.all_to_all(coefs.reshape(plane, message, width), 'zx', 0, 0, tiled=True)  14.1 us
    pallas_call x11, Pallas kernels, call(): pl.pallas_call(kernel, in_specs=vmem(len(args) - unread) + [pl.BlockSpec(...  12.7 us
    all_to_all x1, starting transfers between devices, return_fields(): lax.all_to_all(coefs.reshape(plane, message, width), 'zx', 0, 0, tiled=True)  11.2 us
    ppermute x9, waiting for transfers between devices, flip(): return lax.ppermute(array, axes, pairs)  10.8 us
    all_to_all x1, waiting for transfers between devices, return_fields(): lax.all_to_all(coefs.reshape(plane, message, width), 'zx', 0, 0, tiled=True)  7.18 us
  transfers between devices with their start and end apart: 10, of which 7 were waited for; matrix products, arithmetic and copies ran while one was open for 0% of the time, Pallas kernels for 3%

profile of v5, /device:TPU:1, one launch (start us, length us, event | category | flops | bytes accessed | tf_op | source)
XLA Modules:
  0.0 107.0 jit_solution(17627191873743708185)
XLA Ops:
  0.6 2.2 %collective-permute-start.2 = (bf16[128,512]{1,0:T(8,128)(2,1)}, bf16[128,512]{1,0:T(8,128)(2,1)S(1)}, u32[]{:S(2)}, u32[]{:S(2)}) collective-permute-start(bf16[128,512]{1,0:T(8,128)(2,1)} %bitcast.20), channel_id=1, source_target_pairs={{0,128},{128,0},{1,129},{129,1},{2,130},{130,2},{3,131},{131,3},{4... | collective-permute-start | bytes 393224 | tf_op jit(solution)/shard_map/ppermute | solution.py:372
  2.8 0.1 collective-permute-start
  2.9 1.4 %collective-permute-start.1 = (f32[16,512]{1,0:T(8,128)}, f32[16,512]{1,0:T(8,128)S(1)}, u32[]{:S(2)}, u32[]{:S(2)}) collective-permute-start(f32[16,512]{1,0:T(8,128)} %bitcast.28), channel_id=1, source_target_pairs={{0,128},{128,0},{1,129},{129,1},{2,130},{130,2},{3,131},{131,3},{4... | collective-permute-start | bytes 98312 | tf_op jit(solution)/shard_map/ppermute | solution.py:372
  4.3 0.1 add_bitcast_fusion.place_ref
  4.4 3.1 %prepare.1 = (f32[256,512]{1,0:T(8,128)S(1)}, f32[256,512]{1,0:T(8,128)S(1)}, f32[128,128]{1,0:T(8,128)S(1)}, f32[256,16]{1,0:T(8,128)S(1)}, f32[8,512]{1,0:T(8,...) custom-call(s32[1,2]{1,0:T(1,128)S(1)} %add_bitcast_fusion.place_ref, ...), custom_call_target="tpu_custom_call" | custom-call | tf_op jit(solution)/shard_map/prepare/pallas_call | solution.py:359
  7.5 3.3 %first.1 = (bf16[1024,128]{1,0:T(8,128)(2,1)}, f32[256,512]{1,0:T(8,128)S(1)}, f32[256,512]{1,0:T(8,128)S(1)}, f32[8,512]{1,0:T(8,128)S(1)}, f32[1,512]{1,0:T(1,128)S(1)}, /*index=5*/bf16[256,512]{1,0:T(8,128)(2,1)S(1)}) custom-call(s32[1,2]{1,0:T(1,128)S(1)} %add_bitcast_fusion.place_ref, f32[1,3]{1,0:T(1,128)S(1)} %get-tuple-element.21.lengths_ref, ...), custom_call_target="tpu_custom_call" | custom-call | tf_op jit(solution)/shard_map/first/pallas_call | solution.py:359
  10.8 11.2 %all-to-all-start = ((bf16[32,32,128]{2,1,0:T(8,128)(2,1)}), bf16[32,32,128]{2,1,0:T(8,128)(2,1)S(1)}, u32[]{:S(2)}, u32[]{:S(2)}) async-start(bf16[32,32,128]{2,1,0:T(8,128)(2,1)} %bitcast.8), calls=%async_computation | async-start | bytes 524288 | tf_op jit(solution)/shard_map/all_to_all | solution.py:439
  22.0 0.2 reshape.53
  22.2 0.1 copy.12
  22.4 0.1 reshape.54.own_potential_ref
  22.5 1.9 %collective-permute-start.3 = (bf16[2,2,64,128]{3,2,1,0:T(8,128)(2,1)S(1)}, bf16[2,2,64,128]{3,2,1,0:T(8,128)(2,1)S(1)}, u32[]{:S(2)}, u32[]{:S(2)}) collective-permute-start(bf16[2,2,64,128]{3,2,1,0:T(8,128)(2,1)S(1)} %reshape.54.own_potential_ref), channel_id=1, source_target_pairs={{0,1},{1,0},{2,3},{3,2},{4,5},{5,4},{6,7},{7,6},{8,9},{9,8},{10,11... | collective-permute-start | bytes 196616 | tf_op jit(solution)/shard_map/ppermute | solution.py:372
  24.4 0.9 collective-permute-done.3.potential_ref
  25.3 7.2 %all-to-all-done.parts_ref = bf16[32,32,128]{2,1,0:T(8,128)(2,1)S(1)} async-done(((bf16[32,32,128]{2,1,0:T(8,128)(2,1)}), bf16[32,32,128]{2,1,0:T(8,128)(2,1)S(1)}, u32[]{:S(2)}, u32[]{:S(2)}) %all-to-all-start) | async-done | bytes 262176 | tf_op jit(solution)/shard_map/all_to_all | solution.py:439
  32.4 0.2 potential.2
  32.7 15.2 %all_to_all.20 = bf16[32,32,128]{2,1,0:T(8,128)(2,1)S(1)} all-to-all(bf16[32,32,128]{2,1,0:T(8,128)(2,1)S(1)} %potential.2), channel_id=1, replica_groups=mesh['yl'=2,'zx'=32,'yh'=2,'core'=2] {'zx'}, dimensions={0} | all-to-all | bytes 524288 | tf_op jit(solution)/shard_map/all_to_all | solution.py:446
  47.9 1.8 %back.2.mine_ref = f32[2,8,512]{2,1,0:T(8,128)S(1)} custom-call(bf16[1024,128]{1,0:T(8,128)(2,1)S(1)} %bitcast.25, bf16[128,512]{1,0:T(8,128)(2,1)S(1)} %bitcast.22, bf16[128,512]{1,0:T(8,128)(2,1)S(1)} %collective-permute-done.2.template_ref, f32[256,512]{1,0:T(8,128)S(1)} %get-tuple-element.25.own_cos_ref, f32[256,512]{1,0:T(8,128)S(1)} %get-tuple-element.26.own_sin_ref, ...), custom_call_target="tpu_custom_call" | custom-call | tf_op jit(solution)/shard_map/back/pallas_call | solution.py:359
  49.7 0.7 collective-permute-start.4
  50.4 2.2 %collective-permute-done.4.low_ref = f32[2,8,512]{2,1,0:T(8,128)S(1)} collective-permute-done((f32[2,8,512]{2,1,0:T(8,128)S(1)}, f32[2,8,512]{2,1,0:T(8,128)S(1)}, u32[]{:S(2)}, u32[]{:S(2)}) %collective-permute-start.4) | collective-permute-done | bytes 32800 | tf_op jit(solution)/shard_map/ppermute | solution.py:372
  52.5 2.1 %collective-permute-start.5 = (f32[2,8,512]{2,1,0:T(8,128)S(1)}, f32[2,8,512]{2,1,0:T(8,128)S(1)}, u32[]{:S(2)}, u32[]{:S(2)}) collective-permute-start(f32[2,8,512]{2,1,0:T(8,128)S(1)} %near.2.near_ref), channel_id=1, source_target_pairs={{0,130},{2,128},{128,2},{130,0},{1,131},{3,129},{129,3},{131,1},{4... | collective-permute-start | bytes 98312 | tf_op jit(solution)/shard_map/ppermute | solution.py:372
  54.6 1.9 %collective-permute-done.5.far_ref = f32[2,8,512]{2,1,0:T(8,128)S(1)} collective-permute-done((f32[2,8,512]{2,1,0:T(8,128)S(1)}, f32[2,8,512]{2,1,0:T(8,128)S(1)}, u32[]{:S(2)}, u32[]{:S(2)}) %collective-permute-start.5) | collective-permute-done | bytes 32800 | tf_op jit(solution)/shard_map/ppermute | solution.py:372
  56.5 1.6 %next.1 = (f32[8,512]{1,0:T(8,128)S(1)}, bf16[1024,128]{1,0:T(8,128)(2,1)S(1)}) custom-call(f32[1,512]{1,0:T(1,128)S(1)} %get-tuple-element.20.own_kinetic_ref.kinetic_ref, f32[1,512]{1,0:T(1,128)S(1)} %get-tuple-element.28.kinetic_ref, f32[8,512]{1,0:T(8,128)S(1)} %get-tuple-element.23.own_ref, f32[8,512]{1,0:T(8,128)S(1)} %get-tuple-element.29.other_ref, ...), custom_call_target="tpu_custom_call" | custom-call | tf_op jit(solution)/shard_map/next/pallas_call | solution.py:359
  58.1 14.1 %all_to_all.21.parts_ref = bf16[32,32,128]{2,1,0:T(8,128)(2,1)S(1)} all-to-all(bf16[32,32,128]{2,1,0:T(8,128)(2,1)S(1)} %bitcast.26), channel_id=1, replica_groups=mesh['yl'=2,'zx'=32,'yh'=2,'core'=2] {'zx'}, dimensions={0} | all-to-all | bytes 524288 | tf_op jit(solution)/shard_map/all_to_all | solution.py:439
  72.2 0.2 potential.3
  72.4 13.8 %all_to_all.22 = bf16[32,32,128]{2,1,0:T(8,128)(2,1)S(1)} all-to-all(bf16[32,32,128]{2,1,0:T(8,128)(2,1)S(1)} %potential.3), channel_id=1, replica_groups=mesh['yl'=2,'zx'=32,'yh'=2,'core'=2] {'zx'}, dimensions={0} | all-to-all | bytes 524288 | tf_op jit(solution)/shard_map/all_to_all | solution.py:446
  86.1 1.8 %back.3.mine_ref = f32[2,8,512]{2,1,0:T(8,128)S(1)} custom-call(bf16[1024,128]{1,0:T(8,128)(2,1)S(1)} %bitcast.24, bf16[128,512]{1,0:T(8,128)(2,1)S(1)} %bitcast.23, bf16[128,512]{1,0:T(8,128)(2,1)S(1)} %collective-permute-done.2.template_ref, f32[256,512]{1,0:T(8,128)S(1)} %get-tuple-element.25.own_cos_ref, f32[256,512]{1,0:T(8,128)S(1)} %get-tuple-element.26.own_sin_ref, ...), custom_call_target="tpu_custom_call" | custom-call | tf_op jit(solution)/shard_map/back/pallas_call | solution.py:359
  87.9 0.1 collective-permute-start.6
  88.0 3.0 %collective-permute-done.6.low_ref = f32[2,8,512]{2,1,0:T(8,128)S(1)} collective-permute-done((f32[2,8,512]{2,1,0:T(8,128)S(1)}, f32[2,8,512]{2,1,0:T(8,128)S(1)}, u32[]{:S(2)}, u32[]{:S(2)}) %collective-permute-start.6) | collective-permute-done | bytes 32800 | tf_op jit(solution)/shard_map/ppermute | solution.py:372
  91.1 2.0 %collective-permute-start.7 = (f32[8,512]{1,0:T(8,128)S(1)}, f32[8,512]{1,0:T(8,128)S(1)}, u32[]{:S(2)}, u32[]{:S(2)}) collective-permute-start(f32[8,512]{1,0:T(8,128)S(1)} %slice_bitcast_fusion), channel_id=1, source_target_pairs={{0,130},{2,128},{128,2},{130,0},{1,131},{3,129},{129,3},{131,1},{4... | collective-permute-start | bytes 49160 | tf_op jit(solution)/shard_map/ppermute | solution.py:372
  93.1 1.9 %collective-permute-done.7.far_ref = f32[8,512]{1,0:T(8,128)S(1)} collective-permute-done((f32[8,512]{1,0:T(8,128)S(1)}, f32[8,512]{1,0:T(8,128)S(1)}, u32[]{:S(2)}, u32[]{:S(2)}) %collective-permute-start.7) | collective-permute-done | bytes 16416 | tf_op jit(solution)/shard_map/ppermute | solution.py:372
  95.0 10.4 %collective-permute-start.8 = (f32[2,8,512]{2,1,0:T(8,128)S(1)}, f32[2,8,512]{2,1,0:T(8,128)S(1)}, u32[]{:S(2)}, u32[]{:S(2)}) collective-permute-start(f32[2,8,512]{2,1,0:T(8,128)S(1)} %last.1.mine_ref), channel_id=1, source_target_pairs={{0,1},{1,0},{2,3},{3,2},{4,5},{5,4},{6,7},{7,6},{8,9},{9,8},{10,11... | collective-permute-start | bytes 98312 | tf_op jit(solution)/shard_map/ppermute | solution.py:372
  105.4 0.9 collective-permute-done.8.other_ref
  106.3 0.7 join.1
  (11 shorter events, 0.0 us)
Async XLA Ops:
  0.6 6.9 %collective-permute-start.2 = (bf16[128,512]{1,0:T(8,128)(2,1)}, bf16[128,512]{1,0:T(8,128)(2,1)S(1)}, u32[]{:S(2)}, u32[]{:S(2)}) collective-permute-start(bf16[128,512]{1,0:T(8,128)(2,1)} %bitcast.20), channel_id=1, source_target_pairs={{0,128},{128,0},{1,129},{129,1},{2,130},{130,2},{3,131},{131,3},{4... | collective-permute-start | bytes 393224 | tf_op jit(solution)/shard_map/ppermute | solution.py:372
  2.8 4.7 %collective-permute-start = (s32[3,512]{1,0:T(4,128)}, s32[3,512]{1,0:T(4,128)S(1)}, u32[]{:S(2)}, u32[]{:S(2)}) collective-permute-start(s32[3,512]{1,0:T(4,128)} %refs_3_.1), channel_id=1, source_target_pairs={{0,128},{128,0},{1,129},{129,1},{2,130},{130,2},{3,131},{131,3},{4... | collective-permute-start | bytes 18440 | tf_op jit(solution)/shard_map/ppermute | solution.py:372
  2.9 4.6 %collective-permute-start.1 = (f32[16,512]{1,0:T(8,128)}, f32[16,512]{1,0:T(8,128)S(1)}, u32[]{:S(2)}, u32[]{:S(2)}) collective-permute-start(f32[16,512]{1,0:T(8,128)} %bitcast.28), channel_id=1, source_target_pairs={{0,128},{128,0},{1,129},{129,1},{2,130},{130,2},{3,131},{131,3},{4... | collective-permute-start | bytes 98312 | tf_op jit(solution)/shard_map/ppermute | solution.py:372
  10.8 11.2 %copy-start.1 = (bf16[4,8192]{1,0:T(4,128)(2,1)S(1)}, bf16[4,8192]{1,0:T(4,128)(2,1)}, u32[]{:S(2)}) copy-start(bf16[4,8192]{1,0:T(4,128)(2,1)} %param.10) | copy-start | bytes 196612
  10.8 21.6 %all-to-all-start = ((bf16[32,32,128]{2,1,0:T(8,128)(2,1)}), bf16[32,32,128]{2,1,0:T(8,128)(2,1)S(1)}, u32[]{:S(2)}, u32[]{:S(2)}) async-start(bf16[32,32,128]{2,1,0:T(8,128)(2,1)} %bitcast.8), calls=%async_computation | async-start | bytes 524288 | tf_op jit(solution)/shard_map/all_to_all | solution.py:439
  22.5 2.8 %collective-permute-start.3 = (bf16[2,2,64,128]{3,2,1,0:T(8,128)(2,1)S(1)}, bf16[2,2,64,128]{3,2,1,0:T(8,128)(2,1)S(1)}, u32[]{:S(2)}, u32[]{:S(2)}) collective-permute-start(bf16[2,2,64,128]{3,2,1,0:T(8,128)(2,1)S(1)} %reshape.54.own_potential_ref), channel_id=1, source_target_pairs={{0,1},{1,0},{2,3},{3,2},{4,5},{5,4},{6,7},{7,6},{8,9},{9,8},{10,11... | collective-permute-start | bytes 196616 | tf_op jit(solution)/shard_map/ppermute | solution.py:372
  32.7 15.2 %copy-start = (bf16[2,64,512]{2,1,0:T(8,128)(2,1)S(1)}, bf16[2,64,512]{2,1,0:T(8,128)(2,1)}, u32[]{:S(2)}) copy-start(bf16[2,64,512]{2,1,0:T(8,128)(2,1)} %param.9) | copy-start | bytes 393220
  49.7 2.9 %collective-permute-start.4 = (f32[2,8,512]{2,1,0:T(8,128)S(1)}, f32[2,8,512]{2,1,0:T(8,128)S(1)}, u32[]{:S(2)}, u32[]{:S(2)}) collective-permute-start(f32[2,8,512]{2,1,0:T(8,128)S(1)} %back.2.mine_ref), channel_id=1, source_target_pairs={{0,128},{128,0},{1,129},{129,1},{2,130},{130,2},{3,131},{131,3},{4... | collective-permute-start | bytes 98312 | tf_op jit(solution)/shard_map/ppermute | solution.py:372
  52.5 4.0 %collective-permute-start.5 = (f32[2,8,512]{2,1,0:T(8,128)S(1)}, f32[2,8,512]{2,1,0:T(8,128)S(1)}, u32[]{:S(2)}, u32[]{:S(2)}) collective-permute-start(f32[2,8,512]{2,1,0:T(8,128)S(1)} %near.2.near_ref), channel_id=1, source_target_pairs={{0,130},{2,128},{128,2},{130,0},{1,131},{3,129},{129,3},{131,1},{4... | collective-permute-start | bytes 98312 | tf_op jit(solution)/shard_map/ppermute | solution.py:372
  87.9 3.1 %collective-permute-start.6 = (f32[2,8,512]{2,1,0:T(8,128)S(1)}, f32[2,8,512]{2,1,0:T(8,128)S(1)}, u32[]{:S(2)}, u32[]{:S(2)}) collective-permute-start(f32[2,8,512]{2,1,0:T(8,128)S(1)} %back.3.mine_ref), channel_id=1, source_target_pairs={{0,128},{128,0},{1,129},{129,1},{2,130},{130,2},{3,131},{131,3},{4... | collective-permute-start | bytes 98312 | tf_op jit(solution)/shard_map/ppermute | solution.py:372
  91.1 3.9 %collective-permute-start.7 = (f32[8,512]{1,0:T(8,128)S(1)}, f32[8,512]{1,0:T(8,128)S(1)}, u32[]{:S(2)}, u32[]{:S(2)}) collective-permute-start(f32[8,512]{1,0:T(8,128)S(1)} %slice_bitcast_fusion), channel_id=1, source_target_pairs={{0,130},{2,128},{128,2},{130,0},{1,131},{3,129},{129,3},{131,1},{4... | collective-permute-start | bytes 49160 | tf_op jit(solution)/shard_map/ppermute | solution.py:372
  95.0 11.3 %collective-permute-start.8 = (f32[2,8,512]{2,1,0:T(8,128)S(1)}, f32[2,8,512]{2,1,0:T(8,128)S(1)}, u32[]{:S(2)}, u32[]{:S(2)}) collective-permute-start(f32[2,8,512]{2,1,0:T(8,128)S(1)} %last.1.mine_ref), channel_id=1, source_target_pairs={{0,1},{1,0},{2,3},{3,2},{4,5},{5,4},{6,7},{7,6},{8,9},{9,8},{10,11... | collective-permute-start | bytes 98312 | tf_op jit(solution)/shard_map/ppermute | solution.py:372

commit v6 on v5

--- a/solution.py
+++ b/solution.py
@@ -12,27 +12,25 @@
 bf16 = jnp.bfloat16
 
 COS_TURN = (
-    0.9999999890590225,
-    -19.739204499453912,
-    64.93911745989556,
-    -85.45013953088248,
-    60.167630950949295,
-    -25.96759924849463,
-    6.528658161366808,
+    0.9999992107823212,
+    -19.738980355764024,
+    64.92865742103461,
+    -85.27162153431523,
+    58.790492120199225,
+    -21.07110562773966,
 )
 SIN_TURN = (
-    6.283185302511503,
-    -41.34170040531749,
-    81.60513138579344,
-    -76.70301535379849,
-    42.02592698556796,
-    -14.899846667364866,
-    3.238137509743233,
+    6.283184916495427,
+    -41.34158923268859,
+    81.59994332978516,
+    -76.61447253128296,
+    41.342882354732154,
+    -12.471243535293539,
 )
 NT = (((1,), (1,)), ((), ()))
 NN = (((1,), (0,)), ((), ()))
 CHUNK = 128
-STEP = 128
+STEP = 256
 LIMIT = pltpu.CompilerParams(vmem_limit_bytes=12 * 2**20)
 
 
@@ -129,7 +127,7 @@
     ]
     for copy in copies:
         copy.start()
-    for copy in copies:
+    for copy in copies[:5]:
         copy.wait()
     order_ref, positions_ref, species_ref, miller_ref = targets[:4]
     lengths_ref, fields_ref, template_ref = targets[4:]
@@ -142,8 +140,6 @@
     )
     miller = miller_ref[...].astype(f32)
     kinetic_ref[...] = kinetic_of(miller, lengths_ref[...])
-    own_ref[...] = core_bands(fields_ref, core)
-    both_ref[...] = both_weights(template_ref[...])
     low = lax.broadcasted_iota(jnp.int32, (1, 128), 1) < 64
 
     def step(block, carry):
@@ -163,6 +159,10 @@
         return carry
 
     lax.fori_loop(0, atoms // STEP, step, 0)
+    for copy in copies[5:]:
+        copy.wait()
+    own_ref[...] = core_bands(fields_ref, core)
+    both_ref[...] = both_weights(template_ref[...])
 
 
 def project_chunk(base, phases, fields, weights, select, out_ref, wave_ref):
@@ -195,7 +195,8 @@
 
 def first_kernel(
     place_ref, lengths_ref, table_ref, miller_ref, own_ref, fields_ref, own_both_ref,
-    template_ref, own_cos_ref, own_sin_ref, select_ref, out_ref, cos_ref, sin_ref, other_ref,
+    template_ref, own_cos_ref, own_sin_ref, select_ref, _matrices_ref, _other_matrices_ref,
+    out_ref, cos_ref, sin_ref, other_ref,
     kinetic_ref, both_ref, wave_ref,
 ):
     miller = miller_ref[...].astype(f32)
@@ -385,8 +386,6 @@
     width = 2 * harmonics
     template = template.reshape(species_count * harmonics, waves)
     fields = bands_in.reshape(2 * bands, waves)
-    matrices = potential.reshape(pairs, 2, 2, harmonics, harmonics)
-    matrices = matrices.transpose(0, 2, 3, 1, 4).reshape(pairs, 2, harmonics, width)
     core = lax.axis_index("core")
     stride = groups * slot_dev
     first_slot = lax.axis_index("yl") * plane * stride + lax.axis_index("yh") * 2 * slot_dev
@@ -403,6 +402,12 @@
     other_miller = flip(miller, "yl")
     other_fields = flip(fields, "yl")
     other_template = flip(template, "yl")
+
+    def matrices_of(potential):
+        matrices = potential.reshape(pairs, 2, 2, harmonics, harmonics)
+        return matrices.transpose(0, 2, 3, 1, 4).reshape(pairs, 2, harmonics, width)
+
+    matrices, other_matrices = matrices_of(potential), matrices_of(flip(potential, "core"))
     inputs = (
         atom_order.reshape(1, -1), positions, species.reshape(1, -1), miller, lengths, fields,
         template,
@@ -424,7 +429,7 @@
         first_kernel,
         (
             place, lengths, table, other_miller, own, other_fields, own_both, other_template,
-            own_cos, own_sin, select,
+            own_cos, own_sin, select, matrices, other_matrices,
         ),
         (
             coefs_shape, phase_shape, phase_shape, fields_shape, kinetic_shape, weights_shape,
@@ -432,7 +437,6 @@
         "first",
         [wave_scratch],
     )
-    other_matrices = flip(matrices, "core")
     phases = (own_cos, own_sin, other_cos, other_sin, select)
 
     def return_fields(coefs):

time: 107 us -> 110 us (1.028)
  blocking collectives: 43 us -> 66.5 us
  starting transfers between devices: 32 us -> 18.4 us
  waiting for transfers between devices: 17.9 us -> 10.5 us
  local copies, waits for them, and re-layouts: 0.43 us -> 1.68 us
    all_to_all x1 -> x2, blocking collectives: 14.1 us -> 37.8 us  [return_fields(): lax.all_to_all(coefs.reshape(plane, message, width), 'zx', 0, 0, tiled=True)]
    all_to_all x1 -> x0, starting transfers between devices: 11.2 us -> none  [return_fields(): lax.all_to_all(coefs.reshape(plane, message, width), 'zx', 0, 0, tiled=True)]
    all_to_all x1 -> x0, waiting for transfers between devices: 7.18 us -> none  [return_fields(): lax.all_to_all(coefs.reshape(plane, message, width), 'zx', 0, 0, tiled=True)]
    ppermute x9, starting transfers between devices: 20.8 us -> 18.4 us  [flip(): return lax.ppermute(array, axes, pairs)]
    reshape x3 -> x6, local copies, waits for them, and re-layouts: 0.42 us -> 1.66 us  [the longest x4 1.44 us: matrices_of(): matrices = potential.reshape(pairs, 2, 2, harmonics, harmonics)]
    pallas_call x11, Pallas kernels: 12.7 us -> 11.6 us  [call(): pl.pallas_call(kernel, in_specs=vmem(len(args) - unread) + [pl.BlockSpec(...]
  transfers between devices with their start and end apart: 10 -> 9, of which waited for: 7 -> 5; matrix products, arithmetic and copies ran while one was open for 0% -> 2% of each run, Pallas kernels for 3% -> 2%
where the time goes in v6:
time: 110 us
  blocking collectives  66.5 us (60%)
  starting transfers between devices  18.4 us (17%)
  Pallas kernels  11.6 us (11%)
  waiting for transfers between devices  10.5 us (10%)
  local copies, waits for them, and re-layouts  1.68 us (2%)
    all_to_all x2, blocking collectives, return_fields(): lax.all_to_all(coefs.reshape(plane, message, width), 'zx', 0, 0, tiled=True)  37.8 us
    all_to_all x2, blocking collectives, return_fields(): applied = lax.all_to_all(applied, 'zx', 0, 0, tiled=True)  28.7 us
    ppermute x9, starting transfers between devices, flip(): return lax.ppermute(array, axes, pairs)  18.4 us
    pallas_call x11, Pallas kernels, call(): pl.pallas_call(kernel, in_specs=vmem(len(args) - unread) + [pl.BlockSpec(...  11.6 us
    ppermute x9, waiting for transfers between devices, flip(): return lax.ppermute(array, axes, pairs)  10.5 us
  transfers between devices with their start and end apart: 9, of which 5 were waited for; matrix products, arithmetic and copies ran while one was open for 2% of the time, Pallas kernels for 2%

profile of v6, /device:TPU:1, one launch (start us, length us, event | category | flops | bytes accessed | tf_op | source)
XLA Modules:
  0.0 109.5 jit_solution(2249605536657019579)
XLA Ops:
  0.6 2.2 %collective-permute-start.2 = (bf16[128,512]{1,0:T(8,128)(2,1)}, bf16[128,512]{1,0:T(8,128)(2,1)S(1)}, u32[]{:S(2)}, u32[]{:S(2)}) collective-permute-start(bf16[128,512]{1,0:T(8,128)(2,1)} %bitcast.23), channel_id=1, source_target_pairs={{0,128},{128,0},{1,129},{129,1},{2,130},{130,2},{3,131},{131,3},{4... | collective-permute-start | bytes 393224 | tf_op jit(solution)/shard_map/ppermute | solution.py:373
  2.8 0.1 collective-permute-start
  2.9 1.4 %collective-permute-start.1 = (f32[16,512]{1,0:T(8,128)}, f32[16,512]{1,0:T(8,128)S(1)}, u32[]{:S(2)}, u32[]{:S(2)}) collective-permute-start(f32[16,512]{1,0:T(8,128)} %bitcast.33), channel_id=1, source_target_pairs={{0,128},{128,0},{1,129},{129,1},{2,130},{130,2},{3,131},{131,3},{4... | collective-permute-start | bytes 98312 | tf_op jit(solution)/shard_map/ppermute | solution.py:373
  4.3 1.7 %collective-permute-start.3 = (bf16[4,8192]{1,0:T(4,128)(2,1)}, bf16[4,8192]{1,0:T(4,128)(2,1)S(1)}, u32[]{:S(2)}, u32[]{:S(2)}) collective-permute-start(bf16[4,8192]{1,0:T(4,128)(2,1)} %param.10), channel_id=1, source_target_pairs={{0,1},{1,0},{2,3},{3,2},{4,5},{5,4},{6,7},{7,6},{8,9},{9,8},{10,11... | collective-permute-start | bytes 196616 | tf_op jit(solution)/shard_map/ppermute | solution.py:373
  6.1 1.0 reshape.58
  7.1 0.1 copy.15
  7.3 0.1 reshape.59._matrices_ref.own_potential_ref
  7.4 2.6 %prepare.1 = (f32[256,512]{1,0:T(8,128)S(1)}, f32[256,512]{1,0:T(8,128)S(1)}, f32[128,128]{1,0:T(8,128)S(1)}, f32[256,16]{1,0:T(8,128)S(1)}, f32[8,512]{1,0:T(8,...) custom-call(s32[1,2]{1,0:T(1,128)S(1)} %add_bitcast_fusion.place_ref, ...), custom_call_target="tpu_custom_call" | custom-call | tf_op jit(solution)/shard_map/prepare/pallas_call | solution.py:360
  10.0 0.2 reshape.60
  10.2 0.1 copy.14
  10.3 0.1 reshape.61._other_matrices_ref.potential_ref
  10.5 2.4 %first.1 = (bf16[1024,128]{1,0:T(8,128)(2,1)S(1)}, f32[256,512]{1,0:T(8,128)S(1)}, f32[256,512]{1,0:T(8,128)S(1)}, f32[8,512]{1,0:T(8,128)S(1)}, f32[1,512]{1,0:T(1,128)S(1)}, /*index=5*/bf16[256,512]{1,0:T(8,128)(2,1)S(1)}) custom-call(s32[1,2]{1,0:T(1,128)S(1)} %add_bitcast_fusion.place_ref, f32[1,3]{1,0:T(1,128)S(1)} %get-tuple-element.21.lengths_ref, ...), custom_call_target="tpu_custom_call" | custom-call | tf_op jit(solution)/shard_map/first/pallas_call | solution.py:360
  12.9 22.6 %all_to_all.20.parts_ref = bf16[32,32,128]{2,1,0:T(8,128)(2,1)S(1)} all-to-all(bf16[32,32,128]{2,1,0:T(8,128)(2,1)S(1)} %bitcast.29), channel_id=1, replica_groups=mesh['yl'=2,'zx'=32,'yh'=2,'core'=2] {'zx'}, dimensions={0} | all-to-all | bytes 524288 | tf_op jit(solution)/shard_map/all_to_all | solution.py:443
  35.5 0.2 potential.2
  35.7 14.8 %all_to_all.21 = bf16[32,32,128]{2,1,0:T(8,128)(2,1)S(1)} all-to-all(bf16[32,32,128]{2,1,0:T(8,128)(2,1)S(1)} %potential.2), channel_id=1, replica_groups=mesh['yl'=2,'zx'=32,'yh'=2,'core'=2] {'zx'}, dimensions={0} | all-to-all | bytes 524288 | tf_op jit(solution)/shard_map/all_to_all | solution.py:450
  50.6 1.8 %back.2.mine_ref = f32[2,8,512]{2,1,0:T(8,128)S(1)} custom-call(bf16[1024,128]{1,0:T(8,128)(2,1)S(1)} %bitcast.28, bf16[128,512]{1,0:T(8,128)(2,1)S(1)} %bitcast.25, bf16[128,512]{1,0:T(8,128)(2,1)S(1)} %collective-permute-done.2.template_ref, f32[256,512]{1,0:T(8,128)S(1)} %get-tuple-element.25.own_cos_ref, f32[256,512]{1,0:T(8,128)S(1)} %get-tuple-element.26.own_sin_ref, ...), custom_call_target="tpu_custom_call" | custom-call | tf_op jit(solution)/shard_map/back/pallas_call | solution.py:360
  52.4 0.3 collective-permute-start.4
  52.6 2.6 %collective-permute-done.4.low_ref = f32[2,8,512]{2,1,0:T(8,128)S(1)} collective-permute-done((f32[2,8,512]{2,1,0:T(8,128)S(1)}, f32[2,8,512]{2,1,0:T(8,128)S(1)}, u32[]{:S(2)}, u32[]{:S(2)}) %collective-permute-start.4) | collective-permute-done | bytes 32800 | tf_op jit(solution)/shard_map/ppermute | solution.py:373
  55.2 1.9 %collective-permute-start.5 = (f32[2,8,512]{2,1,0:T(8,128)S(1)}, f32[2,8,512]{2,1,0:T(8,128)S(1)}, u32[]{:S(2)}, u32[]{:S(2)}) collective-permute-start(f32[2,8,512]{2,1,0:T(8,128)S(1)} %near.2.near_ref), channel_id=1, source_target_pairs={{0,130},{2,128},{128,2},{130,0},{1,131},{3,129},{129,3},{131,1},{4... | collective-permute-start | bytes 98312 | tf_op jit(solution)/shard_map/ppermute | solution.py:373
  57.1 2.1 %collective-permute-done.5.far_ref = f32[2,8,512]{2,1,0:T(8,128)S(1)} collective-permute-done((f32[2,8,512]{2,1,0:T(8,128)S(1)}, f32[2,8,512]{2,1,0:T(8,128)S(1)}, u32[]{:S(2)}, u32[]{:S(2)}) %collective-permute-start.5) | collective-permute-done | bytes 32800 | tf_op jit(solution)/shard_map/ppermute | solution.py:373
  59.2 1.8 %next.1 = (f32[8,512]{1,0:T(8,128)S(1)}, bf16[1024,128]{1,0:T(8,128)(2,1)S(1)}) custom-call(f32[1,512]{1,0:T(1,128)S(1)} %get-tuple-element.20.own_kinetic_ref.kinetic_ref, f32[1,512]{1,0:T(1,128)S(1)} %get-tuple-element.28.kinetic_ref, f32[8,512]{1,0:T(8,128)S(1)} %get-tuple-element.23.own_ref, f32[8,512]{1,0:T(8,128)S(1)} %get-tuple-element.29.other_ref, ...), custom_call_target="tpu_custom_call" | custom-call | tf_op jit(solution)/shard_map/next/pallas_call | solution.py:360
  61.0 15.3 %all_to_all.22.parts_ref = bf16[32,32,128]{2,1,0:T(8,128)(2,1)S(1)} all-to-all(bf16[32,32,128]{2,1,0:T(8,128)(2,1)S(1)} %bitcast.30), channel_id=1, replica_groups=mesh['yl'=2,'zx'=32,'yh'=2,'core'=2] {'zx'}, dimensions={0} | all-to-all | bytes 524288 | tf_op jit(solution)/shard_map/all_to_all | solution.py:443
  76.3 0.2 potential.3
  76.5 13.9 %all_to_all.23 = bf16[32,32,128]{2,1,0:T(8,128)(2,1)S(1)} all-to-all(bf16[32,32,128]{2,1,0:T(8,128)(2,1)S(1)} %potential.3), channel_id=1, replica_groups=mesh['yl'=2,'zx'=32,'yh'=2,'core'=2] {'zx'}, dimensions={0} | all-to-all | bytes 524288 | tf_op jit(solution)/shard_map/all_to_all | solution.py:450
  90.4 1.8 %back.3.mine_ref = f32[2,8,512]{2,1,0:T(8,128)S(1)} custom-call(bf16[1024,128]{1,0:T(8,128)(2,1)S(1)} %bitcast.27, bf16[128,512]{1,0:T(8,128)(2,1)S(1)} %bitcast.26, bf16[128,512]{1,0:T(8,128)(2,1)S(1)} %collective-permute-done.2.template_ref, f32[256,512]{1,0:T(8,128)S(1)} %get-tuple-element.25.own_cos_ref, f32[256,512]{1,0:T(8,128)S(1)} %get-tuple-element.26.own_sin_ref, ...), custom_call_target="tpu_custom_call" | custom-call | tf_op jit(solution)/shard_map/back/pallas_call | solution.py:360
  92.1 0.1 collective-permute-start.6
  92.2 3.0 %collective-permute-done.6.low_ref = f32[2,8,512]{2,1,0:T(8,128)S(1)} collective-permute-done((f32[2,8,512]{2,1,0:T(8,128)S(1)}, f32[2,8,512]{2,1,0:T(8,128)S(1)}, u32[]{:S(2)}, u32[]{:S(2)}) %collective-permute-start.6) | collective-permute-done | bytes 32800 | tf_op jit(solution)/shard_map/ppermute | solution.py:373
  95.3 2.0 %collective-permute-start.7 = (f32[8,512]{1,0:T(8,128)S(1)}, f32[8,512]{1,0:T(8,128)S(1)}, u32[]{:S(2)}, u32[]{:S(2)}) collective-permute-start(f32[8,512]{1,0:T(8,128)S(1)} %slice_bitcast_fusion), channel_id=1, source_target_pairs={{0,130},{2,128},{128,2},{130,0},{1,131},{3,129},{129,3},{131,1},{4... | collective-permute-start | bytes 49160 | tf_op jit(solution)/shard_map/ppermute | solution.py:373
  97.3 1.9 %collective-permute-done.7.far_ref = f32[8,512]{1,0:T(8,128)S(1)} collective-permute-done((f32[8,512]{1,0:T(8,128)S(1)}, f32[8,512]{1,0:T(8,128)S(1)}, u32[]{:S(2)}, u32[]{:S(2)}) %collective-permute-start.7) | collective-permute-done | bytes 16416 | tf_op jit(solution)/shard_map/ppermute | solution.py:373
  99.2 8.7 %collective-permute-start.8 = (f32[2,8,512]{2,1,0:T(8,128)S(1)}, f32[2,8,512]{2,1,0:T(8,128)S(1)}, u32[]{:S(2)}, u32[]{:S(2)}) collective-permute-start(f32[2,8,512]{2,1,0:T(8,128)S(1)} %last.1.mine_ref), channel_id=1, source_target_pairs={{0,1},{1,0},{2,3},{3,2},{4,5},{5,4},{6,7},{7,6},{8,9},{9,8},{10,11... | collective-permute-start | bytes 98312 | tf_op jit(solution)/shard_map/ppermute | solution.py:373
  107.9 0.9 collective-permute-done.8.other_ref
  108.8 0.7 join.1
  (11 shorter events, 0.1 us)
Async XLA Ops:
  0.6 9.9 %collective-permute-start.2 = (bf16[128,512]{1,0:T(8,128)(2,1)}, bf16[128,512]{1,0:T(8,128)(2,1)S(1)}, u32[]{:S(2)}, u32[]{:S(2)}) collective-permute-start(bf16[128,512]{1,0:T(8,128)(2,1)} %bitcast.23), channel_id=1, source_target_pairs={{0,128},{128,0},{1,129},{129,1},{2,130},{130,2},{3,131},{131,3},{4... | collective-permute-start | bytes 393224 | tf_op jit(solution)/shard_map/ppermute | solution.py:373
  2.8 7.6 %collective-permute-start = (s32[3,512]{1,0:T(4,128)}, s32[3,512]{1,0:T(4,128)S(1)}, u32[]{:S(2)}, u32[]{:S(2)}) collective-permute-start(s32[3,512]{1,0:T(4,128)} %refs_3_.1), channel_id=1, source_target_pairs={{0,128},{128,0},{1,129},{129,1},{2,130},{130,2},{3,131},{131,3},{4... | collective-permute-start | bytes 18440 | tf_op jit(solution)/shard_map/ppermute | solution.py:373
  2.9 7.5 %collective-permute-start.1 = (f32[16,512]{1,0:T(8,128)}, f32[16,512]{1,0:T(8,128)S(1)}, u32[]{:S(2)}, u32[]{:S(2)}) collective-permute-start(f32[16,512]{1,0:T(8,128)} %bitcast.33), channel_id=1, source_target_pairs={{0,128},{128,0},{1,129},{129,1},{2,130},{130,2},{3,131},{131,3},{4... | collective-permute-start | bytes 98312 | tf_op jit(solution)/shard_map/ppermute | solution.py:373
  4.3 5.7 %collective-permute-start.3 = (bf16[4,8192]{1,0:T(4,128)(2,1)}, bf16[4,8192]{1,0:T(4,128)(2,1)S(1)}, u32[]{:S(2)}, u32[]{:S(2)}) collective-permute-start(bf16[4,8192]{1,0:T(4,128)(2,1)} %param.10), channel_id=1, source_target_pairs={{0,1},{1,0},{2,3},{3,2},{4,5},{5,4},{6,7},{7,6},{8,9},{9,8},{10,11... | collective-permute-start | bytes 196616 | tf_op jit(solution)/shard_map/ppermute | solution.py:373
  35.7 14.8 %copy-start = (bf16[2,64,512]{2,1,0:T(8,128)(2,1)S(1)}, bf16[2,64,512]{2,1,0:T(8,128)(2,1)}, u32[]{:S(2)}) copy-start(bf16[2,64,512]{2,1,0:T(8,128)(2,1)} %param.9) | copy-start | bytes 393220
  52.4 2.9 %collective-permute-start.4 = (f32[2,8,512]{2,1,0:T(8,128)S(1)}, f32[2,8,512]{2,1,0:T(8,128)S(1)}, u32[]{:S(2)}, u32[]{:S(2)}) collective-permute-start(f32[2,8,512]{2,1,0:T(8,128)S(1)} %back.2.mine_ref), channel_id=1, source_target_pairs={{0,128},{128,0},{1,129},{129,1},{2,130},{130,2},{3,131},{131,3},{4... | collective-permute-start | bytes 98312 | tf_op jit(solution)/shard_map/ppermute | solution.py:373
  55.2 4.0 %collective-permute-start.5 = (f32[2,8,512]{2,1,0:T(8,128)S(1)}, f32[2,8,512]{2,1,0:T(8,128)S(1)}, u32[]{:S(2)}, u32[]{:S(2)}) collective-permute-start(f32[2,8,512]{2,1,0:T(8,128)S(1)} %near.2.near_ref), channel_id=1, source_target_pairs={{0,130},{2,128},{128,2},{130,0},{1,131},{3,129},{129,3},{131,1},{4... | collective-permute-start | bytes 98312 | tf_op jit(solution)/shard_map/ppermute | solution.py:373
  92.1 3.1 %collective-permute-start.6 = (f32[2,8,512]{2,1,0:T(8,128)S(1)}, f32[2,8,512]{2,1,0:T(8,128)S(1)}, u32[]{:S(2)}, u32[]{:S(2)}) collective-permute-start(f32[2,8,512]{2,1,0:T(8,128)S(1)} %back.3.mine_ref), channel_id=1, source_target_pairs={{0,128},{128,0},{1,129},{129,1},{2,130},{130,2},{3,131},{131,3},{4... | collective-permute-start | bytes 98312 | tf_op jit(solution)/shard_map/ppermute | solution.py:373
  95.3 3.9 %collective-permute-start.7 = (f32[8,512]{1,0:T(8,128)S(1)}, f32[8,512]{1,0:T(8,128)S(1)}, u32[]{:S(2)}, u32[]{:S(2)}) collective-permute-start(f32[8,512]{1,0:T(8,128)S(1)} %slice_bitcast_fusion), channel_id=1, source_target_pairs={{0,130},{2,128},{128,2},{130,0},{1,131},{3,129},{129,3},{131,1},{4... | collective-permute-start | bytes 49160 | tf_op jit(solution)/shard_map/ppermute | solution.py:373
  99.2 9.6 %collective-permute-start.8 = (f32[2,8,512]{2,1,0:T(8,128)S(1)}, f32[2,8,512]{2,1,0:T(8,128)S(1)}, u32[]{:S(2)}, u32[]{:S(2)}) collective-permute-start(f32[2,8,512]{2,1,0:T(8,128)S(1)} %last.1.mine_ref), channel_id=1, source_target_pairs={{0,1},{1,0},{2,3},{3,2},{4,5},{5,4},{6,7},{7,6},{8,9},{9,8},{10,11... | collective-permute-start | bytes 98312 | tf_op jit(solution)/shard_map/ppermute | solution.py:373

commit v7 on v6

--- a/solution.py
+++ b/solution.py
@@ -7,6 +7,7 @@
 from jax.experimental.pallas import tpu as pltpu
 from jax.sharding import Mesh
 from jax.sharding import PartitionSpec as P
+
 
 f32 = jnp.float32
 bf16 = jnp.bfloat16
@@ -195,8 +196,7 @@
 
 def first_kernel(
     place_ref, lengths_ref, table_ref, miller_ref, own_ref, fields_ref, own_both_ref,
-    template_ref, own_cos_ref, own_sin_ref, select_ref, _matrices_ref, _other_matrices_ref,
-    out_ref, cos_ref, sin_ref, other_ref,
+    template_ref, own_cos_ref, own_sin_ref, select_ref, out_ref, cos_ref, sin_ref, other_ref,
     kinetic_ref, both_ref, wave_ref,
 ):
     miller = miller_ref[...].astype(f32)
@@ -223,15 +223,15 @@
 
 
 def next_kernel(
-    own_kinetic_ref, kinetic_ref, own_ref, other_ref, near_ref, far_ref,
-    own_weights_ref, weights_ref, own_cos_ref, own_sin_ref, cos_ref, sin_ref, select_ref,
+    own_kinetic_ref, kinetic_ref, own_ref, other_ref, mine_ref, low_ref, high_ref,
+    both_ref, own_weights_ref, weights_ref, own_cos_ref, own_sin_ref, cos_ref, sin_ref, select_ref,
     fields_out_ref, out_ref, wave_ref,
 ):
     own = own_kinetic_ref[...] * own_ref[...]
-    own = own + (near_ref[0] + far_ref[1])
+    own = own + ((mine_ref[0] + high_ref[0]) + (low_ref[1] + both_ref[1]))
     fields_out_ref[...] = own
     other = kinetic_ref[...] * other_ref[...]
-    other = other + (near_ref[1] + far_ref[0])
+    other = other + ((mine_ref[1] + high_ref[1]) + (low_ref[0] + both_ref[0]))
     fields = [field_pair(own), field_pair(other)]
     weights = [own_weights_ref, weights_ref]
 
@@ -250,14 +250,10 @@
     lax.fori_loop(0, cos_ref.shape[0] // CHUNK, step, 0)
 
 
-def near_kernel(mine_ref, low_ref, out_ref):
-    out_ref[0] = mine_ref[0] + low_ref[1]
-    out_ref[1] = mine_ref[1] + low_ref[0]
-
-
-def last_kernel(kinetic_ref, own_ref, near_ref, far_ref, out_ref):
+def last_kernel(kinetic_ref, own_ref, mine_ref, low_ref, high_ref, both_ref, out_ref):
+    total = kinetic_ref[...] * own_ref[...]
     out_ref[0] = own_ref[...]
-    out_ref[1] = kinetic_ref[...] * own_ref[...] + (near_ref[0] + far_ref[...])
+    out_ref[1] = total + ((mine_ref[0] + high_ref[...]) + (low_ref[...] + both_ref[...]))
 
 
 def join_kernel(place_ref, mine_ref, other_ref, once_ref, twice_ref):
@@ -356,7 +352,7 @@
     return jax.ShapeDtypeStruct(dims, dtype)
 
 
-def call(kernel, args, out_shape, name, scratch_shapes=(), unread=0):
+def call(kernel, args, out_shape, scratch_shapes=(), unread=0):
     return pl.pallas_call(
         kernel,
         in_specs=vmem(len(args) - unread) + [pl.BlockSpec(memory_space=pltpu.HBM)] * unread,
@@ -364,7 +360,6 @@
         out_shape=tuple(out_shape),
         scratch_shapes=scratch_shapes,
         compiler_params=LIMIT,
-        name=name,
     )(*args)
 
 
@@ -386,6 +381,8 @@
     width = 2 * harmonics
     template = template.reshape(species_count * harmonics, waves)
     fields = bands_in.reshape(2 * bands, waves)
+    matrices = potential.reshape(pairs, 2, 2, harmonics, harmonics)
+    matrices = matrices.transpose(0, 2, 3, 1, 4).reshape(pairs, 2, harmonics, width)
     core = lax.axis_index("core")
     stride = groups * slot_dev
     first_slot = lax.axis_index("yl") * plane * stride + lax.axis_index("yh") * 2 * slot_dev
@@ -402,12 +399,6 @@
     other_miller = flip(miller, "yl")
     other_fields = flip(fields, "yl")
     other_template = flip(template, "yl")
-
-    def matrices_of(potential):
-        matrices = potential.reshape(pairs, 2, 2, harmonics, harmonics)
-        return matrices.transpose(0, 2, 3, 1, 4).reshape(pairs, 2, harmonics, width)
-
-    matrices, other_matrices = matrices_of(potential), matrices_of(flip(potential, "core"))
     inputs = (
         atom_order.reshape(1, -1), positions, species.reshape(1, -1), miller, lengths, fields,
         template,
@@ -420,7 +411,6 @@
             phase_shape, phase_shape, shape((atoms // 2, 128), f32), shape((atoms, 16), f32),
             fields_shape, kinetic_shape, weights_shape, shape(lengths.shape, f32),
         ),
-        "prepare",
         [pltpu.VMEM(value.shape, value.dtype) for value in inputs]
         + [pltpu.SemaphoreType.DMA((len(inputs),))],
         unread=len(inputs),
@@ -429,14 +419,14 @@
         first_kernel,
         (
             place, lengths, table, other_miller, own, other_fields, own_both, other_template,
-            own_cos, own_sin, select, matrices, other_matrices,
+            own_cos, own_sin, select,
         ),
         (
             coefs_shape, phase_shape, phase_shape, fields_shape, kinetic_shape, weights_shape,
         ),
-        "first",
         [wave_scratch],
     )
+    other_matrices = flip(matrices, "core")
     phases = (own_cos, own_sin, other_cos, other_sin, select)
 
     def return_fields(coefs):
@@ -445,43 +435,39 @@
             potential_kernel,
             (parts, matrices, other_matrices),
             (shape((plane, message, width), bf16),),
-            "potential",
         )
         applied = lax.all_to_all(applied, "zx", 0, 0, tiled=True)
         (mine,) = call(
             return_kernel,
             (applied.reshape(atoms // 2 * rows, width), template, other_template) + phases,
             (shape((2, rows, waves), f32),),
-            "back",
             [pltpu.VMEM((CHUNK * rows, 2 * width), bf16)],
         )
-        (near,) = call(
-            near_kernel, (mine, flip(mine, "yl")), (shape((2, rows, waves), f32),), "near"
-        )
-        return near
-
-    near = return_fields(coefs)
+        return mine
+
+    def around(same, turned):
+        low = flip(turned, "yl")
+        both = flip(turned, "yl", "yh")
+        high = flip(same, "yh")
+        return low, high, both
+
+    mine = return_fields(coefs)
     once, coefs = call(
         next_kernel,
-        (
-            own_kinetic, other_kinetic, own, other, near, flip(near, "yl", "yh"), own_both,
-            other_both,
-        )
+        (own_kinetic, other_kinetic, own, other, mine)
+        + around(mine, mine)
+        + (own_both, other_both)
         + phases,
         (fields_shape, coefs_shape),
-        "next",
         [wave_scratch],
     )
-    near = return_fields(coefs)
+    mine = return_fields(coefs)
     (mine,) = call(
         last_kernel,
-        (own_kinetic, once, near, flip(near[1], "yl", "yh")),
+        (own_kinetic, once, mine) + around(mine[0], mine[1]),
         (shape((2, rows, waves), f32),),
-        "last",
-    )
-    once, twice = call(
-        join_kernel, (place, mine, flip(mine, "core")), (whole_shape, whole_shape), "join"
-    )
+    )
+    once, twice = call(join_kernel, (place, mine, flip(mine, "core")), (whole_shape, whole_shape))
     return once.reshape(bands_in.shape), twice.reshape(bands_in.shape)
 
 
@@ -500,6 +486,7 @@
         P(),
     )
     out_specs = (P(None, None, waves), P(None, None, waves))
+
     return jax.shard_map(
         per_device, mesh=fine, in_specs=in_specs, out_specs=out_specs, check_vma=False
     )

time: 110 us -> 104 us (0.945)
  blocking collectives: 66.5 us -> 43.1 us
  starting transfers between devices: 18.4 us -> 32.1 us
  waiting for transfers between devices: 10.5 us -> 15.2 us
  local copies, waits for them, and re-layouts: 1.68 us -> 0.43 us
    all_to_all x2 -> x1, blocking collectives: 37.8 us -> 14 us  [return_fields(): lax.all_to_all(coefs.reshape(plane, message, width), 'zx', 0, 0, tiled=True)]
    all_to_all x0 -> x1, starting transfers between devices: none -> 11.2 us  [return_fields(): lax.all_to_all(coefs.reshape(plane, message, width), 'zx', 0, 0, tiled=True)]
    all_to_all x0 -> x1, waiting for transfers between devices: none -> 7.18 us  [return_fields(): lax.all_to_all(coefs.reshape(plane, message, width), 'zx', 0, 0, tiled=True)]
    ppermute x9 -> x11, starting transfers between devices: 18.4 us -> 20.9 us  [flip(): return lax.ppermute(array, axes, pairs)]
    ppermute x9 -> x11, waiting for transfers between devices: 10.5 us -> 8.05 us  [flip(): return lax.ppermute(array, axes, pairs)]
    reshape x6 -> x3, local copies, waits for them, and re-layouts: 1.66 us -> 0.42 us  [the longest x2 0.3 us: per_device(): matrices = potential.reshape(pairs, 2, 2, harmonics, harmonics)]
    pallas_call x11 -> x9, Pallas kernels: 11.6 us -> 12 us  [call(): pl.pallas_call(kernel, in_specs=vmem(len(args) - unread) + [pl.BlockSpec(...]
  transfers between devices with their start and end apart: 9 -> 12, of which waited for: 5 -> 7; matrix products, arithmetic and copies ran while one was open for 2% -> 0% of each run, Pallas kernels for 2% -> 3%
where the time goes in v7:
time: 104 us
  blocking collectives  43.1 us (41%)
  starting transfers between devices  32.1 us (31%)
  waiting for transfers between devices  15.2 us (15%)
  Pallas kernels  12 us (12%)
    all_to_all x2, blocking collectives, return_fields(): applied = lax.all_to_all(applied, 'zx', 0, 0, tiled=True)  29.1 us
    ppermute x11, starting transfers between devices, flip(): return lax.ppermute(array, axes, pairs)  20.9 us
    all_to_all x1, blocking collectives, return_fields(): lax.all_to_all(coefs.reshape(plane, message, width), 'zx', 0, 0, tiled=True)  14 us
    pallas_call x9, Pallas kernels, call(): pl.pallas_call(kernel, in_specs=vmem(len(args) - unread) + [pl.BlockSpec(...  12 us
    all_to_all x1, starting transfers between devices, return_fields(): lax.all_to_all(coefs.reshape(plane, message, width), 'zx', 0, 0, tiled=True)  11.2 us
    ppermute x11, waiting for transfers between devices, flip(): return lax.ppermute(array, axes, pairs)  8.05 us
    all_to_all x1, waiting for transfers between devices, return_fields(): lax.all_to_all(coefs.reshape(plane, message, width), 'zx', 0, 0, tiled=True)  7.18 us
  transfers between devices with their start and end apart: 12, of which 7 were waited for; matrix products, arithmetic and copies ran while one was open for 0% of the time, Pallas kernels for 3%

profile of v7, /device:TPU:1, one launch (start us, length us, event | category | flops | bytes accessed | tf_op | source)
XLA Modules:
  0.0 103.6 jit_solution(14434508123195624186)
XLA Ops:
  0.6 2.2 %collective-permute-start.2 = (bf16[128,512]{1,0:T(8,128)(2,1)}, bf16[128,512]{1,0:T(8,128)(2,1)S(1)}, u32[]{:S(2)}, u32[]{:S(2)}) collective-permute-start(bf16[128,512]{1,0:T(8,128)(2,1)} %bitcast.22), channel_id=1, source_target_pairs={{0,128},{128,0},{1,129},{129,1},{2,130},{130,2},{3,131},{131,3},{4... | collective-permute-start | bytes 393224 | tf_op jit(solution)/shard_map/ppermute | solution.py:368
  2.9 1.4 %collective-permute-start.1 = (f32[16,512]{1,0:T(8,128)}, f32[16,512]{1,0:T(8,128)S(1)}, u32[]{:S(2)}, u32[]{:S(2)}) collective-permute-start(f32[16,512]{1,0:T(8,128)} %bitcast.30), channel_id=1, source_target_pairs={{0,128},{128,0},{1,129},{129,1},{2,130},{130,2},{3,131},{131,3},{4... | collective-permute-start | bytes 98312 | tf_op jit(solution)/shard_map/ppermute | solution.py:368
  4.4 2.6 %shard_map.95 = (f32[256,512]{1,0:T(8,128)S(1)}, f32[256,512]{1,0:T(8,128)S(1)}, f32[128,128]{1,0:T(8,128)S(1)}, f32[256,16]{1,0:T(8,128)S(1)}, f32[8,512]{1,0:T...) custom-call(s32[1,2]{1,0:T(1,128)S(1)} %add_bitcast_fusion.place_ref, ...), custom_call_target="tpu_custom_call" | custom-call | tf_op jit(solution)/shard_map/pallas_call | solution.py:356
  7.0 3.1 %shard_map.96 = (bf16[1024,128]{1,0:T(8,128)(2,1)}, f32[256,512]{1,0:T(8,128)S(1)}, f32[256,512]{1,0:T(8,128)S(1)}, f32[8,512]{1,0:T(8,128)S(1)}, f32[1,512]{1,0:T(1,128)S(1)}, /*index=5*/bf16[256,512]{1,0:T(8,128)(2,1)S(1)}) custom-call(s32[1,2]{1,0:T(1,128)S(1)} %add_bitcast_fusion.place_ref, f32[1,3]{1,0:T(1,128)S(1)} %get-tuple-element.21.lengths_ref, ...), custom_call_target="tpu_custom_call" | custom-call | tf_op jit(solution)/shard_map/pallas_call | solution.py:356
  10.1 11.2 %all-to-all-start = ((bf16[32,32,128]{2,1,0:T(8,128)(2,1)}), bf16[32,32,128]{2,1,0:T(8,128)(2,1)S(1)}, u32[]{:S(2)}, u32[]{:S(2)}) async-start(bf16[32,32,128]{2,1,0:T(8,128)(2,1)} %bitcast.8), calls=%async_computation | async-start | bytes 524288 | tf_op jit(solution)/shard_map/all_to_all | solution.py:433
  21.3 0.2 reshape.53
  21.5 0.1 copy.12
  21.6 0.1 reshape.54.own_potential_ref
  21.8 1.9 %collective-permute-start.3 = (bf16[2,2,64,128]{3,2,1,0:T(8,128)(2,1)S(1)}, bf16[2,2,64,128]{3,2,1,0:T(8,128)(2,1)S(1)}, u32[]{:S(2)}, u32[]{:S(2)}) collective-permute-start(bf16[2,2,64,128]{3,2,1,0:T(8,128)(2,1)S(1)} %reshape.54.own_potential_ref), channel_id=1, source_target_pairs={{0,1},{1,0},{2,3},{3,2},{4,5},{5,4},{6,7},{7,6},{8,9},{9,8},{10,11... | collective-permute-start | bytes 196616 | tf_op jit(solution)/shard_map/ppermute | solution.py:368
  23.6 0.9 collective-permute-done.3.potential_ref
  24.5 7.2 %all-to-all-done.parts_ref = bf16[32,32,128]{2,1,0:T(8,128)(2,1)S(1)} async-done(((bf16[32,32,128]{2,1,0:T(8,128)(2,1)}), bf16[32,32,128]{2,1,0:T(8,128)(2,1)S(1)}, u32[]{:S(2)}, u32[]{:S(2)}) %all-to-all-start) | async-done | bytes 262176 | tf_op jit(solution)/shard_map/all_to_all | solution.py:433
  31.7 0.2 shard_map.97
  32.0 15.2 %all_to_all.20 = bf16[32,32,128]{2,1,0:T(8,128)(2,1)S(1)} all-to-all(bf16[32,32,128]{2,1,0:T(8,128)(2,1)S(1)} %shard_map.97), channel_id=1, replica_groups=mesh['yl'=2,'zx'=32,'yh'=2,'core'=2] {'zx'}, dimensions={0} | all-to-all | bytes 524288 | tf_op jit(solution)/shard_map/all_to_all | solution.py:439
  47.2 1.8 %shard_map.98.mine_ref = f32[2,8,512]{2,1,0:T(8,128)S(1)} custom-call(bf16[1024,128]{1,0:T(8,128)(2,1)S(1)} %bitcast.27, bf16[128,512]{1,0:T(8,128)(2,1)S(1)} %bitcast.24, bf16[128,512]{1,0:T(8,128)(2,1)S(1)} %collective-permute-done.2.template_ref, f32[256,512]{1,0:T(8,128)S(1)} %get-tuple-element.25.own_cos_ref, ...), custom_call_target="tpu_custom_call" | custom-call | tf_op jit(solution)/shard_map/pallas_call | solution.py:356
  49.0 2.6 %collective-permute-start.6 = (f32[2,8,512]{2,1,0:T(8,128)S(1)}, f32[2,8,512]{2,1,0:T(8,128)S(1)}, u32[]{:S(2)}, u32[]{:S(2)}) collective-permute-start(f32[2,8,512]{2,1,0:T(8,128)S(1)} %shard_map.98.mine_ref), channel_id=1, source_target_pairs={{0,130},{2,128},{128,2},{130,0},{1,131},{3,129},{129,3},{131,1},{4... | collective-permute-start | bytes 98312 | tf_op jit(solution)/shard_map/ppermute | solution.py:368
  51.6 0.3 collective-permute-start.5
  52.0 0.4 collective-permute-start.4
  52.3 0.7 collective-permute-done.6.both_ref
  53.0 2.8 %collective-permute-done.5.high_ref = f32[2,8,512]{2,1,0:T(8,128)S(1)} collective-permute-done((f32[2,8,512]{2,1,0:T(8,128)S(1)}, f32[2,8,512]{2,1,0:T(8,128)S(1)}, u32[]{:S(2)}, u32[]{:S(2)}) %collective-permute-start.5) | collective-permute-done | bytes 32800 | tf_op jit(solution)/shard_map/ppermute | solution.py:368
  55.9 1.6 %shard_map.99 = (f32[8,512]{1,0:T(8,128)S(1)}, bf16[1024,128]{1,0:T(8,128)(2,1)S(1)}) custom-call(f32[1,512]{1,0:T(1,128)S(1)} %get-tuple-element.20.own_kinetic_ref.kinetic_ref, f32[1,512]{1,0:T(1,128)S(1)} %get-tuple-element.28.kinetic_ref, f32[8,512]{1,0:T(8,128)S(1)} %get-tuple-element.23.own_ref, f32[8,512]{1,0:T(8,128)S(1)} %get-tuple-element.29.other_ref, ...), custom_call_target="tpu_custom_call" | custom-call | tf_op jit(solution)/shard_map/pallas_call | solution.py:356
  57.5 14.0 %all_to_all.21.parts_ref = bf16[32,32,128]{2,1,0:T(8,128)(2,1)S(1)} all-to-all(bf16[32,32,128]{2,1,0:T(8,128)(2,1)S(1)} %bitcast.28), channel_id=1, replica_groups=mesh['yl'=2,'zx'=32,'yh'=2,'core'=2] {'zx'}, dimensions={0} | all-to-all | bytes 524288 | tf_op jit(solution)/shard_map/all_to_all | solution.py:433
  71.4 0.2 shard_map.100
  71.7 13.9 %all_to_all.22 = bf16[32,32,128]{2,1,0:T(8,128)(2,1)S(1)} all-to-all(bf16[32,32,128]{2,1,0:T(8,128)(2,1)S(1)} %shard_map.100), channel_id=1, replica_groups=mesh['yl'=2,'zx'=32,'yh'=2,'core'=2] {'zx'}, dimensions={0} | all-to-all | bytes 524288 | tf_op jit(solution)/shard_map/all_to_all | solution.py:439
  85.5 1.8 %shard_map.101.mine_ref = f32[2,8,512]{2,1,0:T(8,128)S(1)} custom-call(bf16[1024,128]{1,0:T(8,128)(2,1)S(1)} %bitcast.26, bf16[128,512]{1,0:T(8,128)(2,1)S(1)} %bitcast.25, bf16[128,512]{1,0:T(8,128)(2,1)S(1)} %collective-permute-done.2.template_ref, f32[256,512]{1,0:T(8,128)S(1)} %get-tuple-element.25.own_cos_ref, ...), custom_call_target="tpu_custom_call" | custom-call | tf_op jit(solution)/shard_map/pallas_call | solution.py:356
  87.3 1.5 %collective-permute-start.8 = (f32[8,512]{1,0:T(8,128)S(1)}, f32[8,512]{1,0:T(8,128)S(1)}, u32[]{:S(2)}, u32[]{:S(2)}) collective-permute-start(f32[8,512]{1,0:T(8,128)S(1)} %get-tuple-element.38), channel_id=1, source_target_pairs={{0,2},{2,0},{1,3},{3,1},{4,6},{6,4},{5,7},{7,5},{8,10},{10,8},{9,1... | collective-permute-start | bytes 49160 | tf_op jit(solution)/shard_map/ppermute | solution.py:368
  88.9 0.8 collective-permute-start.9
  89.6 0.4 collective-permute-start.7
  90.0 1.7 %collective-permute-done.8.high_ref = f32[8,512]{1,0:T(8,128)S(1)} collective-permute-done((f32[8,512]{1,0:T(8,128)S(1)}, f32[8,512]{1,0:T(8,128)S(1)}, u32[]{:S(2)}, u32[]{:S(2)}) %collective-permute-start.8) | collective-permute-done | bytes 16416 | tf_op jit(solution)/shard_map/ppermute | solution.py:368
  91.8 1.0 collective-permute-done.9.both_ref
  92.8 9.3 %collective-permute-start.10 = (f32[2,8,512]{2,1,0:T(8,128)S(1)}, f32[2,8,512]{2,1,0:T(8,128)S(1)}, u32[]{:S(2)}, u32[]{:S(2)}) collective-permute-start(f32[2,8,512]{2,1,0:T(8,128)S(1)} %shard_map.102.mine_ref), channel_id=1, source_target_pairs={{0,1},{1,0},{2,3},{3,2},{4,5},{5,4},{6,7},{7,6},{8,9},{9,8},{10,11... | collective-permute-start | bytes 98312 | tf_op jit(solution)/shard_map/ppermute | solution.py:368
  102.1 0.9 collective-permute-done.10.other_ref
  102.9 0.7 shard_map.103
  (13 shorter events, 0.2 us)
Async XLA Ops:
  0.6 6.4 %collective-permute-start.2 = (bf16[128,512]{1,0:T(8,128)(2,1)}, bf16[128,512]{1,0:T(8,128)(2,1)S(1)}, u32[]{:S(2)}, u32[]{:S(2)}) collective-permute-start(bf16[128,512]{1,0:T(8,128)(2,1)} %bitcast.22), channel_id=1, source_target_pairs={{0,128},{128,0},{1,129},{129,1},{2,130},{130,2},{3,131},{131,3},{4... | collective-permute-start | bytes 393224 | tf_op jit(solution)/shard_map/ppermute | solution.py:368
  2.8 4.2 %collective-permute-start = (s32[3,512]{1,0:T(4,128)}, s32[3,512]{1,0:T(4,128)S(1)}, u32[]{:S(2)}, u32[]{:S(2)}) collective-permute-start(s32[3,512]{1,0:T(4,128)} %refs_3_.1), channel_id=1, source_target_pairs={{0,128},{128,0},{1,129},{129,1},{2,130},{130,2},{3,131},{131,3},{4... | collective-permute-start | bytes 18440 | tf_op jit(solution)/shard_map/ppermute | solution.py:368
  2.9 4.1 %collective-permute-start.1 = (f32[16,512]{1,0:T(8,128)}, f32[16,512]{1,0:T(8,128)S(1)}, u32[]{:S(2)}, u32[]{:S(2)}) collective-permute-start(f32[16,512]{1,0:T(8,128)} %bitcast.30), channel_id=1, source_target_pairs={{0,128},{128,0},{1,129},{129,1},{2,130},{130,2},{3,131},{131,3},{4... | collective-permute-start | bytes 98312 | tf_op jit(solution)/shard_map/ppermute | solution.py:368
  10.1 11.2 %copy-start.1 = (bf16[4,8192]{1,0:T(4,128)(2,1)S(1)}, bf16[4,8192]{1,0:T(4,128)(2,1)}, u32[]{:S(2)}) copy-start(bf16[4,8192]{1,0:T(4,128)(2,1)} %param.10) | copy-start | bytes 196612
  10.1 21.6 %all-to-all-start = ((bf16[32,32,128]{2,1,0:T(8,128)(2,1)}), bf16[32,32,128]{2,1,0:T(8,128)(2,1)S(1)}, u32[]{:S(2)}, u32[]{:S(2)}) async-start(bf16[32,32,128]{2,1,0:T(8,128)(2,1)} %bitcast.8), calls=%async_computation | async-start | bytes 524288 | tf_op jit(solution)/shard_map/all_to_all | solution.py:433
  21.8 2.8 %collective-permute-start.3 = (bf16[2,2,64,128]{3,2,1,0:T(8,128)(2,1)S(1)}, bf16[2,2,64,128]{3,2,1,0:T(8,128)(2,1)S(1)}, u32[]{:S(2)}, u32[]{:S(2)}) collective-permute-start(bf16[2,2,64,128]{3,2,1,0:T(8,128)(2,1)S(1)} %reshape.54.own_potential_ref), channel_id=1, source_target_pairs={{0,1},{1,0},{2,3},{3,2},{4,5},{5,4},{6,7},{7,6},{8,9},{9,8},{10,11... | collective-permute-start | bytes 196616 | tf_op jit(solution)/shard_map/ppermute | solution.py:368
  32.0 15.2 %copy-start = (bf16[2,64,512]{2,1,0:T(8,128)(2,1)S(1)}, bf16[2,64,512]{2,1,0:T(8,128)(2,1)}, u32[]{:S(2)}) copy-start(bf16[2,64,512]{2,1,0:T(8,128)(2,1)} %param.9) | copy-start | bytes 393220
  49.0 4.1 %collective-permute-start.6 = (f32[2,8,512]{2,1,0:T(8,128)S(1)}, f32[2,8,512]{2,1,0:T(8,128)S(1)}, u32[]{:S(2)}, u32[]{:S(2)}) collective-permute-start(f32[2,8,512]{2,1,0:T(8,128)S(1)} %shard_map.98.mine_ref), channel_id=1, source_target_pairs={{0,130},{2,128},{128,2},{130,0},{1,131},{3,129},{129,3},{131,1},{4... | collective-permute-start | bytes 98312 | tf_op jit(solution)/shard_map/ppermute | solution.py:368
  51.6 4.3 %collective-permute-start.5 = (f32[2,8,512]{2,1,0:T(8,128)S(1)}, f32[2,8,512]{2,1,0:T(8,128)S(1)}, u32[]{:S(2)}, u32[]{:S(2)}) collective-permute-start(f32[2,8,512]{2,1,0:T(8,128)S(1)} %shard_map.98.mine_ref), channel_id=1, source_target_pairs={{0,2},{2,0},{1,3},{3,1},{4,6},{6,4},{5,7},{7,5},{8,10},{10,8},{9,1... | collective-permute-start | bytes 98312 | tf_op jit(solution)/shard_map/ppermute | solution.py:368
  52.0 3.9 %collective-permute-start.4 = (f32[2,8,512]{2,1,0:T(8,128)S(1)}, f32[2,8,512]{2,1,0:T(8,128)S(1)}, u32[]{:S(2)}, u32[]{:S(2)}) collective-permute-start(f32[2,8,512]{2,1,0:T(8,128)S(1)} %shard_map.98.mine_ref), channel_id=1, source_target_pairs={{0,128},{128,0},{1,129},{129,1},{2,130},{130,2},{3,131},{131,3},{4... | collective-permute-start | bytes 98312 | tf_op jit(solution)/shard_map/ppermute | solution.py:368
  87.3 4.5 %collective-permute-start.8 = (f32[8,512]{1,0:T(8,128)S(1)}, f32[8,512]{1,0:T(8,128)S(1)}, u32[]{:S(2)}, u32[]{:S(2)}) collective-permute-start(f32[8,512]{1,0:T(8,128)S(1)} %get-tuple-element.38), channel_id=1, source_target_pairs={{0,2},{2,0},{1,3},{3,1},{4,6},{6,4},{5,7},{7,5},{8,10},{10,8},{9,1... | collective-permute-start | bytes 49160 | tf_op jit(solution)/shard_map/ppermute | solution.py:368
  88.9 3.9 %collective-permute-start.9 = (f32[8,512]{1,0:T(8,128)S(1)}, f32[8,512]{1,0:T(8,128)S(1)}, u32[]{:S(2)}, u32[]{:S(2)}) collective-permute-start(f32[8,512]{1,0:T(8,128)S(1)} %get-tuple-element.39), channel_id=1, source_target_pairs={{0,130},{2,128},{128,2},{130,0},{1,131},{3,129},{129,3},{131,1},{4... | collective-permute-start | bytes 49160 | tf_op jit(solution)/shard_map/ppermute | solution.py:368
  89.6 3.1 %collective-permute-start.7 = (f32[8,512]{1,0:T(8,128)S(1)}, f32[8,512]{1,0:T(8,128)S(1)}, u32[]{:S(2)}, u32[]{:S(2)}) collective-permute-start(f32[8,512]{1,0:T(8,128)S(1)} %get-tuple-element.39), channel_id=1, source_target_pairs={{0,128},{128,0},{1,129},{129,1},{2,130},{130,2},{3,131},{131,3},{4... | collective-permute-start | bytes 49160 | tf_op jit(solution)/shard_map/ppermute | solution.py:368
  92.8 10.2 %collective-permute-start.10 = (f32[2,8,512]{2,1,0:T(8,128)S(1)}, f32[2,8,512]{2,1,0:T(8,128)S(1)}, u32[]{:S(2)}, u32[]{:S(2)}) collective-permute-start(f32[2,8,512]{2,1,0:T(8,128)S(1)} %shard_map.102.mine_ref), channel_id=1, source_target_pairs={{0,1},{1,0},{2,3},{3,2},{4,5},{5,4},{6,7},{7,6},{8,9},{9,8},{10,11... | collective-permute-start | bytes 98312 | tf_op jit(solution)/shard_map/ppermute | solution.py:368

commit v8 on v7

--- a/solution.py
+++ b/solution.py
@@ -59,7 +59,9 @@
     row = lax.broadcasted_iota(jnp.int32, (rows, 1), 0)
     pair = 2 * slot_dev
     side = (row % pair // slot_dev) ^ core
-    slot = first_slot + row // pair * stride + side * slot_dev + row % slot_dev
+    member = row // pair
+    member = member % 8 * (rows // pair // 8) + member // 8
+    slot = first_slot + member * stride + side * slot_dev + row % slot_dev
     lane = lax.broadcasted_iota(jnp.int32, (rows, atoms), 1)
     pick_slot = jnp.where(lane == slot, 1.0, 0.0).astype(bf16)
     coarse, fine = order // 128, order % 128
@@ -369,7 +371,7 @@
 
 
 def per_device(bands_in, template, potential, miller, positions, species, atom_order, reciprocal):
-    plane = lax.axis_size("zx")
+    plane = lax.axis_size("z") * lax.axis_size("x")
     groups = lax.axis_size("yh") * lax.axis_size("core")
     slot_dev = potential.shape[0]
     atoms = 2 * slot_dev * plane
@@ -430,13 +432,13 @@
     phases = (own_cos, own_sin, other_cos, other_sin, select)
 
     def return_fields(coefs):
-        parts = lax.all_to_all(coefs.reshape(plane, message, width), "zx", 0, 0, tiled=True)
+        parts = lax.all_to_all(coefs.reshape(plane, message, width), ("x", "z"), 0, 0, tiled=True)
         (applied,) = call(
             potential_kernel,
             (parts, matrices, other_matrices),
             (shape((plane, message, width), bf16),),
         )
-        applied = lax.all_to_all(applied, "zx", 0, 0, tiled=True)
+        applied = lax.all_to_all(applied, ("x", "z"), 0, 0, tiled=True)
         (mine,) = call(
             return_kernel,
             (applied.reshape(atoms // 2 * rows, width), template, other_template) + phases,
@@ -473,8 +475,10 @@
 
 def solution(mesh):
     pw, groups = mesh.devices.shape
-    fine = Mesh(mesh.devices.reshape(2, pw // 2, 2, groups // 2), ("yl", "zx", "yh", "core"))
-    waves, slots = ("yl", "zx"), ("yl", "zx", "yh", "core")
+    fine = Mesh(
+        mesh.devices.reshape(2, 8, pw // 16, 2, groups // 2), ("yl", "z", "x", "yh", "core")
+    )
+    waves, slots = ("yl", "z", "x"), ("yl", "z", "x", "yh", "core")
     in_specs = (
         P(None, None, waves),
         P(None, None, waves),

time: 104 us -> 104 us (level)
  no operation moved by 1% of the time
where the time goes in v8:
time: 104 us; the launch traced here: 103 us
  blocking collectives  43.9 us (42%)
  starting transfers between devices  31.8 us (31%)
  waiting for transfers between devices  14.3 us (14%)
  Pallas kernels  12 us (12%)
    all_to_all x2, blocking collectives, return_fields(): applied = lax.all_to_all(applied, ('x', 'z'), 0, 0, tiled=True)  29.6 us
    ppermute x11, starting transfers between devices, flip(): return lax.ppermute(array, axes, pairs)  20.6 us
    all_to_all x1, blocking collectives, return_fields(): lax.all_to_all(coefs.reshape(plane, message, width), ('x', 'z'), 0, 0, ti...  14.3 us
    pallas_call x9, Pallas kernels, call(): pl.pallas_call(kernel, in_specs=vmem(len(args) - unread) + [pl.BlockSpec(...  12 us
    all_to_all x1, starting transfers between devices, return_fields(): lax.all_to_all(coefs.reshape(plane, message, width), ('x', 'z'), 0, 0, ti...  11.2 us
    ppermute x11, waiting for transfers between devices, flip(): return lax.ppermute(array, axes, pairs)  7.87 us
    all_to_all x1, waiting for transfers between devices, return_fields(): lax.all_to_all(coefs.reshape(plane, message, width), ('x', 'z'), 0, 0, ti...  6.43 us
  transfers between devices with their start and end apart: 12, of which 7 were waited for; matrix products, arithmetic and copies ran while one was open for 0% of the time, Pallas kernels for 3%

profile of v8, /device:TPU:1, one launch (start us, length us, event | category | flops | bytes accessed | tf_op | source)
XLA Modules:
  0.0 103.3 jit_solution(13924737044383868194)
XLA Ops:
  0.6 2.2 %collective-permute-start.2 = (bf16[128,512]{1,0:T(8,128)(2,1)}, bf16[128,512]{1,0:T(8,128)(2,1)S(1)}, u32[]{:S(2)}, u32[]{:S(2)}) collective-permute-start(bf16[128,512]{1,0:T(8,128)(2,1)} %bitcast.22), channel_id=1, source_target_pairs={{0,128},{128,0},{1,129},{129,1},{2,130},{130,2},{3,131},{131,3},{4... | collective-permute-start | bytes 393224 | tf_op jit(solution)/shard_map/ppermute | solution.py:370
  2.9 1.4 %collective-permute-start.1 = (f32[16,512]{1,0:T(8,128)}, f32[16,512]{1,0:T(8,128)S(1)}, u32[]{:S(2)}, u32[]{:S(2)}) collective-permute-start(f32[16,512]{1,0:T(8,128)} %bitcast.30), channel_id=1, source_target_pairs={{0,128},{128,0},{1,129},{129,1},{2,130},{130,2},{3,131},{131,3},{4... | collective-permute-start | bytes 98312 | tf_op jit(solution)/shard_map/ppermute | solution.py:370
  4.4 2.6 %shard_map.95 = (f32[256,512]{1,0:T(8,128)S(1)}, f32[256,512]{1,0:T(8,128)S(1)}, f32[128,128]{1,0:T(8,128)S(1)}, f32[256,16]{1,0:T(8,128)S(1)}, f32[8,512]{1,0:T...) custom-call(s32[1,2]{1,0:T(1,128)S(1)} %add_bitcast_fusion.place_ref, ...), custom_call_target="tpu_custom_call" | custom-call | tf_op jit(solution)/shard_map/pallas_call | solution.py:358
  7.0 3.1 %shard_map.96 = (bf16[1024,128]{1,0:T(8,128)(2,1)}, f32[256,512]{1,0:T(8,128)S(1)}, f32[256,512]{1,0:T(8,128)S(1)}, f32[8,512]{1,0:T(8,128)S(1)}, f32[1,512]{1,0:T(1,128)S(1)}, /*index=5*/bf16[256,512]{1,0:T(8,128)(2,1)S(1)}) custom-call(s32[1,2]{1,0:T(1,128)S(1)} %add_bitcast_fusion.place_ref, f32[1,3]{1,0:T(1,128)S(1)} %get-tuple-element.21.lengths_ref, ...), custom_call_target="tpu_custom_call" | custom-call | tf_op jit(solution)/shard_map/pallas_call | solution.py:358
  10.1 11.2 %all-to-all-start = ((bf16[32,32,128]{2,1,0:T(8,128)(2,1)}), bf16[32,32,128]{2,1,0:T(8,128)(2,1)S(1)}, u32[]{:S(2)}, u32[]{:S(2)}) async-start(bf16[32,32,128]{2,1,0:T(8,128)(2,1)} %bitcast.8), calls=%async_computation | async-start | bytes 524288 | tf_op jit(solution)/shard_map/all_to_all | solution.py:435
  21.3 0.2 reshape.53
  21.5 0.1 copy.12
  21.6 0.1 reshape.54.own_potential_ref
  21.8 1.9 %collective-permute-start.3 = (bf16[2,2,64,128]{3,2,1,0:T(8,128)(2,1)S(1)}, bf16[2,2,64,128]{3,2,1,0:T(8,128)(2,1)S(1)}, u32[]{:S(2)}, u32[]{:S(2)}) collective-permute-start(bf16[2,2,64,128]{3,2,1,0:T(8,128)(2,1)S(1)} %reshape.54.own_potential_ref), channel_id=1, source_target_pairs={{0,1},{1,0},{2,3},{3,2},{4,5},{5,4},{6,7},{7,6},{8,9},{9,8},{10,11... | collective-permute-start | bytes 196616 | tf_op jit(solution)/shard_map/ppermute | solution.py:370
  23.6 0.9 collective-permute-done.3.potential_ref
  24.5 6.4 %all-to-all-done.parts_ref = bf16[32,32,128]{2,1,0:T(8,128)(2,1)S(1)} async-done(((bf16[32,32,128]{2,1,0:T(8,128)(2,1)}), bf16[32,32,128]{2,1,0:T(8,128)(2,1)S(1)}, u32[]{:S(2)}, u32[]{:S(2)}) %all-to-all-start) | async-done | bytes 262176 | tf_op jit(solution)/shard_map/all_to_all | solution.py:435
  31.0 0.2 shard_map.97
  31.2 15.7 %all_to_all.20 = bf16[32,32,128]{2,1,0:T(8,128)(2,1)S(1)} all-to-all(bf16[32,32,128]{2,1,0:T(8,128)(2,1)S(1)} %shard_map.97), channel_id=1, replica_groups=mesh['yl'=2,'z'=8,'x'=4,'yh'=2,'core'=2] {'x','z'}, dimensions={0} | all-to-all | bytes 524288 | tf_op jit(solution)/shard_map/all_to_all | solution.py:441
  46.9 1.8 %shard_map.98.mine_ref = f32[2,8,512]{2,1,0:T(8,128)S(1)} custom-call(bf16[1024,128]{1,0:T(8,128)(2,1)S(1)} %bitcast.27, bf16[128,512]{1,0:T(8,128)(2,1)S(1)} %bitcast.24, bf16[128,512]{1,0:T(8,128)(2,1)S(1)} %collective-permute-done.2.template_ref, f32[256,512]{1,0:T(8,128)S(1)} %get-tuple-element.25.own_cos_ref, ...), custom_call_target="tpu_custom_call" | custom-call | tf_op jit(solution)/shard_map/pallas_call | solution.py:358
  48.7 2.6 %collective-permute-start.6 = (f32[2,8,512]{2,1,0:T(8,128)S(1)}, f32[2,8,512]{2,1,0:T(8,128)S(1)}, u32[]{:S(2)}, u32[]{:S(2)}) collective-permute-start(f32[2,8,512]{2,1,0:T(8,128)S(1)} %shard_map.98.mine_ref), channel_id=1, source_target_pairs={{0,130},{2,128},{128,2},{130,0},{1,131},{3,129},{129,3},{131,1},{4... | collective-permute-start | bytes 98312 | tf_op jit(solution)/shard_map/ppermute | solution.py:370
  51.3 0.3 collective-permute-start.5
  51.6 0.4 collective-permute-start.4
  52.0 0.7 collective-permute-done.6.both_ref
  52.8 2.8 %collective-permute-done.5.high_ref = f32[2,8,512]{2,1,0:T(8,128)S(1)} collective-permute-done((f32[2,8,512]{2,1,0:T(8,128)S(1)}, f32[2,8,512]{2,1,0:T(8,128)S(1)}, u32[]{:S(2)}, u32[]{:S(2)}) %collective-permute-start.5) | collective-permute-done | bytes 32800 | tf_op jit(solution)/shard_map/ppermute | solution.py:370
  55.5 1.6 %shard_map.99 = (f32[8,512]{1,0:T(8,128)S(1)}, bf16[1024,128]{1,0:T(8,128)(2,1)S(1)}) custom-call(f32[1,512]{1,0:T(1,128)S(1)} %get-tuple-element.20.own_kinetic_ref.kinetic_ref, f32[1,512]{1,0:T(1,128)S(1)} %get-tuple-element.28.kinetic_ref, f32[8,512]{1,0:T(8,128)S(1)} %get-tuple-element.23.own_ref, f32[8,512]{1,0:T(8,128)S(1)} %get-tuple-element.29.other_ref, ...), custom_call_target="tpu_custom_call" | custom-call | tf_op jit(solution)/shard_map/pallas_call | solution.py:358
  57.1 14.3 %all_to_all.21.parts_ref = bf16[32,32,128]{2,1,0:T(8,128)(2,1)S(1)} all-to-all(bf16[32,32,128]{2,1,0:T(8,128)(2,1)S(1)} %bitcast.28), channel_id=1, replica_groups=mesh['yl'=2,'z'=8,'x'=4,'yh'=2,'core'=2] {'x','z'}, dimensions={0} | all-to-all | bytes 524288 | tf_op jit(solution)/shard_map/all_to_all | solution.py:435
  71.4 0.2 shard_map.100
  71.6 13.9 %all_to_all.22 = bf16[32,32,128]{2,1,0:T(8,128)(2,1)S(1)} all-to-all(bf16[32,32,128]{2,1,0:T(8,128)(2,1)S(1)} %shard_map.100), channel_id=1, replica_groups=mesh['yl'=2,'z'=8,'x'=4,'yh'=2,'core'=2] {'x','z'}, dimensions={0} | all-to-all | bytes 524288 | tf_op jit(solution)/shard_map/all_to_all | solution.py:441
  85.6 1.8 %shard_map.101.mine_ref = f32[2,8,512]{2,1,0:T(8,128)S(1)} custom-call(bf16[1024,128]{1,0:T(8,128)(2,1)S(1)} %bitcast.26, bf16[128,512]{1,0:T(8,128)(2,1)S(1)} %bitcast.25, bf16[128,512]{1,0:T(8,128)(2,1)S(1)} %collective-permute-done.2.template_ref, f32[256,512]{1,0:T(8,128)S(1)} %get-tuple-element.25.own_cos_ref, ...), custom_call_target="tpu_custom_call" | custom-call | tf_op jit(solution)/shard_map/pallas_call | solution.py:358
  87.3 1.5 %collective-permute-start.8 = (f32[8,512]{1,0:T(8,128)S(1)}, f32[8,512]{1,0:T(8,128)S(1)}, u32[]{:S(2)}, u32[]{:S(2)}) collective-permute-start(f32[8,512]{1,0:T(8,128)S(1)} %get-tuple-element.38), channel_id=1, source_target_pairs={{0,2},{2,0},{1,3},{3,1},{4,6},{6,4},{5,7},{7,5},{8,10},{10,8},{9,1... | collective-permute-start | bytes 49160 | tf_op jit(solution)/shard_map/ppermute | solution.py:370
  88.9 0.8 collective-permute-start.9
  89.7 0.4 collective-permute-start.7
  90.1 1.7 %collective-permute-done.8.high_ref = f32[8,512]{1,0:T(8,128)S(1)} collective-permute-done((f32[8,512]{1,0:T(8,128)S(1)}, f32[8,512]{1,0:T(8,128)S(1)}, u32[]{:S(2)}, u32[]{:S(2)}) %collective-permute-start.8) | collective-permute-done | bytes 16416 | tf_op jit(solution)/shard_map/ppermute | solution.py:370
  91.8 0.9 collective-permute-done.9.both_ref
  92.7 9.0 %collective-permute-start.10 = (f32[2,8,512]{2,1,0:T(8,128)S(1)}, f32[2,8,512]{2,1,0:T(8,128)S(1)}, u32[]{:S(2)}, u32[]{:S(2)}) collective-permute-start(f32[2,8,512]{2,1,0:T(8,128)S(1)} %shard_map.102.mine_ref), channel_id=1, source_target_pairs={{0,1},{1,0},{2,3},{3,2},{4,5},{5,4},{6,7},{7,6},{8,9},{9,8},{10,11... | collective-permute-start | bytes 98312 | tf_op jit(solution)/shard_map/ppermute | solution.py:370
  101.7 0.9 collective-permute-done.10.other_ref
  102.6 0.7 shard_map.103
  (13 shorter events, 0.2 us)
Async XLA Ops:
  0.6 6.4 %collective-permute-start.2 = (bf16[128,512]{1,0:T(8,128)(2,1)}, bf16[128,512]{1,0:T(8,128)(2,1)S(1)}, u32[]{:S(2)}, u32[]{:S(2)}) collective-permute-start(bf16[128,512]{1,0:T(8,128)(2,1)} %bitcast.22), channel_id=1, source_target_pairs={{0,128},{128,0},{1,129},{129,1},{2,130},{130,2},{3,131},{131,3},{4... | collective-permute-start | bytes 393224 | tf_op jit(solution)/shard_map/ppermute | solution.py:370
  2.8 4.2 %collective-permute-start = (s32[3,512]{1,0:T(4,128)}, s32[3,512]{1,0:T(4,128)S(1)}, u32[]{:S(2)}, u32[]{:S(2)}) collective-permute-start(s32[3,512]{1,0:T(4,128)} %refs_3_.1), channel_id=1, source_target_pairs={{0,128},{128,0},{1,129},{129,1},{2,130},{130,2},{3,131},{131,3},{4... | collective-permute-start | bytes 18440 | tf_op jit(solution)/shard_map/ppermute | solution.py:370
  2.9 4.1 %collective-permute-start.1 = (f32[16,512]{1,0:T(8,128)}, f32[16,512]{1,0:T(8,128)S(1)}, u32[]{:S(2)}, u32[]{:S(2)}) collective-permute-start(f32[16,512]{1,0:T(8,128)} %bitcast.30), channel_id=1, source_target_pairs={{0,128},{128,0},{1,129},{129,1},{2,130},{130,2},{3,131},{131,3},{4... | collective-permute-start | bytes 98312 | tf_op jit(solution)/shard_map/ppermute | solution.py:370
  10.1 11.2 %copy-start.1 = (bf16[4,8192]{1,0:T(4,128)(2,1)S(1)}, bf16[4,8192]{1,0:T(4,128)(2,1)}, u32[]{:S(2)}) copy-start(bf16[4,8192]{1,0:T(4,128)(2,1)} %param.10) | copy-start | bytes 196612
  10.1 20.8 %all-to-all-start = ((bf16[32,32,128]{2,1,0:T(8,128)(2,1)}), bf16[32,32,128]{2,1,0:T(8,128)(2,1)S(1)}, u32[]{:S(2)}, u32[]{:S(2)}) async-start(bf16[32,32,128]{2,1,0:T(8,128)(2,1)} %bitcast.8), calls=%async_computation | async-start | bytes 524288 | tf_op jit(solution)/shard_map/all_to_all | solution.py:435
  21.8 2.8 %collective-permute-start.3 = (bf16[2,2,64,128]{3,2,1,0:T(8,128)(2,1)S(1)}, bf16[2,2,64,128]{3,2,1,0:T(8,128)(2,1)S(1)}, u32[]{:S(2)}, u32[]{:S(2)}) collective-permute-start(bf16[2,2,64,128]{3,2,1,0:T(8,128)(2,1)S(1)} %reshape.54.own_potential_ref), channel_id=1, source_target_pairs={{0,1},{1,0},{2,3},{3,2},{4,5},{5,4},{6,7},{7,6},{8,9},{9,8},{10,11... | collective-permute-start | bytes 196616 | tf_op jit(solution)/shard_map/ppermute | solution.py:370
  31.2 15.7 %copy-start = (bf16[2,64,512]{2,1,0:T(8,128)(2,1)S(1)}, bf16[2,64,512]{2,1,0:T(8,128)(2,1)}, u32[]{:S(2)}) copy-start(bf16[2,64,512]{2,1,0:T(8,128)(2,1)} %param.9) | copy-start | bytes 393220
  48.7 4.1 %collective-permute-start.6 = (f32[2,8,512]{2,1,0:T(8,128)S(1)}, f32[2,8,512]{2,1,0:T(8,128)S(1)}, u32[]{:S(2)}, u32[]{:S(2)}) collective-permute-start(f32[2,8,512]{2,1,0:T(8,128)S(1)} %shard_map.98.mine_ref), channel_id=1, source_target_pairs={{0,130},{2,128},{128,2},{130,0},{1,131},{3,129},{129,3},{131,1},{4... | collective-permute-start | bytes 98312 | tf_op jit(solution)/shard_map/ppermute | solution.py:370
  51.3 4.3 %collective-permute-start.5 = (f32[2,8,512]{2,1,0:T(8,128)S(1)}, f32[2,8,512]{2,1,0:T(8,128)S(1)}, u32[]{:S(2)}, u32[]{:S(2)}) collective-permute-start(f32[2,8,512]{2,1,0:T(8,128)S(1)} %shard_map.98.mine_ref), channel_id=1, source_target_pairs={{0,2},{2,0},{1,3},{3,1},{4,6},{6,4},{5,7},{7,5},{8,10},{10,8},{9,1... | collective-permute-start | bytes 98312 | tf_op jit(solution)/shard_map/ppermute | solution.py:370
  51.6 3.9 %collective-permute-start.4 = (f32[2,8,512]{2,1,0:T(8,128)S(1)}, f32[2,8,512]{2,1,0:T(8,128)S(1)}, u32[]{:S(2)}, u32[]{:S(2)}) collective-permute-start(f32[2,8,512]{2,1,0:T(8,128)S(1)} %shard_map.98.mine_ref), channel_id=1, source_target_pairs={{0,128},{128,0},{1,129},{129,1},{2,130},{130,2},{3,131},{131,3},{4... | collective-permute-start | bytes 98312 | tf_op jit(solution)/shard_map/ppermute | solution.py:370
  87.3 4.5 %collective-permute-start.8 = (f32[8,512]{1,0:T(8,128)S(1)}, f32[8,512]{1,0:T(8,128)S(1)}, u32[]{:S(2)}, u32[]{:S(2)}) collective-permute-start(f32[8,512]{1,0:T(8,128)S(1)} %get-tuple-element.38), channel_id=1, source_target_pairs={{0,2},{2,0},{1,3},{3,1},{4,6},{6,4},{5,7},{7,5},{8,10},{10,8},{9,1... | collective-permute-start | bytes 49160 | tf_op jit(solution)/shard_map/ppermute | solution.py:370
  88.9 3.8 %collective-permute-start.9 = (f32[8,512]{1,0:T(8,128)S(1)}, f32[8,512]{1,0:T(8,128)S(1)}, u32[]{:S(2)}, u32[]{:S(2)}) collective-permute-start(f32[8,512]{1,0:T(8,128)S(1)} %get-tuple-element.39), channel_id=1, source_target_pairs={{0,130},{2,128},{128,2},{130,0},{1,131},{3,129},{129,3},{131,1},{4... | collective-permute-start | bytes 49160 | tf_op jit(solution)/shard_map/ppermute | solution.py:370
  89.7 3.0 %collective-permute-start.7 = (f32[8,512]{1,0:T(8,128)S(1)}, f32[8,512]{1,0:T(8,128)S(1)}, u32[]{:S(2)}, u32[]{:S(2)}) collective-permute-start(f32[8,512]{1,0:T(8,128)S(1)} %get-tuple-element.39), channel_id=1, source_target_pairs={{0,128},{128,0},{1,129},{129,1},{2,130},{130,2},{3,131},{131,3},{4... | collective-permute-start | bytes 49160 | tf_op jit(solution)/shard_map/ppermute | solution.py:370
  92.7 9.9 %collective-permute-start.10 = (f32[2,8,512]{2,1,0:T(8,128)S(1)}, f32[2,8,512]{2,1,0:T(8,128)S(1)}, u32[]{:S(2)}, u32[]{:S(2)}) collective-permute-start(f32[2,8,512]{2,1,0:T(8,128)S(1)} %shard_map.102.mine_ref), channel_id=1, source_target_pairs={{0,1},{1,0},{2,3},{3,2},{4,5},{5,4},{6,7},{7,6},{8,9},{9,8},{10,11... | collective-permute-start | bytes 98312 | tf_op jit(solution)/shard_map/ppermute | solution.py:370
